TPU v7x, 32 devices: a whole 2x2x4 slice. The times are simulated.
32 devices in a mesh: parts: 2 (over y), row: 4 (over z), col: 2 (over x), cores: 2 (over core).
Axes of the slice: x: 2, y: 2, z: 4, core: 2. Of those that a mesh axis runs over, the one named last changes fastest.
Arguments:
- latent: float32 [128, 256, 128], P(('parts', 'row', 'cores'), 'col'), parts along dimension 0, may hold values from -6 to 6
- moment_one: float32 [128, 256, 128], P(('parts', 'row', 'cores'), 'col'), parts along dimension 0, may hold values from -0.3 to 0.3
- moment_two: float32 [128, 256, 128], P(('parts', 'row', 'cores'), 'col'), parts along dimension 0, may hold values from 0.001 to 0.01
- hole_mask: int32 [128, 256], P(('parts', 'row', 'cores'), 'col'), parts along dimension 0, may hold values 0 or 1
- target_rgb: float32 [3, 128, 256], P(None, ('parts', 'row', 'cores'), 'col'), parts along dimension 1, may hold values from -4 to 4
- kernel_one: bfloat16 [3, 3, 128, 128], replicated, may hold values from -0.1875 to 0.1875
- bias_one: float32 [128], replicated, may hold values from -3 to 3
- kernel_two: bfloat16 [3, 3, 128, 128], replicated, may hold values from -0.1875 to 0.1875
- bias_two: float32 [128], replicated, may hold values from -3 to 3
- rgb_weight: bfloat16 [3, 128], replicated, may hold values from -0.5 to 0.5
Outputs:
- latent_out: float32 [128, 256, 128], P(('parts', 'row', 'cores'), 'col'), parts along dimension 0
- moment_one_out: float32 [128, 256, 128], P(('parts', 'row', 'cores'), 'col'), parts along dimension 0
- moment_two_out: float32 [128, 256, 128], P(('parts', 'row', 'cores'), 'col'), parts along dimension 0
There are 2 independent parts, one for each index of `parts`. A program takes and returns all parts, laid end to end along the dimension named above; an argument that names none is the same for every part. Nothing has to cross between parts.
All inputs are finite; a program needn't handle non-finite values. No bound on the sum of `hole_mask` on one device may be relied on, other than what follows from the above.
Results may differ from a plain program's by a relative error of at most 0.0045.
Values may be sent and summed in bfloat16 or wider, within the bound.
No kernel may reach another device: no remote copies, remote signals or barrier semaphores. Data moves between devices by JAX's collectives and lax.ppermute only.
A program may use at most 64 MiB of HBM per device.

v0:
```python
import jax
import jax.numpy as jnp
from jax import lax
from jax.sharding import PartitionSpec as P

STEPS = 2


BETA_ONE = 0.6
BETA_TWO = 0.9
LEARN_RATE = 0.4
EPSILON = 1e-08


def extended(block, sides, width):
    for axis, dim in sides:
        count = lax.axis_size(axis)
        forward = [(i, i + 1) for i in range(count - 1)]
        backward = [(target, source) for source, target in forward]
        low = lax.ppermute(
            lax.slice_in_dim(block, block.shape[dim] - width, None, axis=dim), axis, forward
        )
        high = lax.ppermute(lax.slice_in_dim(block, 0, width, axis=dim), axis, backward)
        block = jnp.concatenate([low, block, high], axis=dim)
    return block


def tap_sum(padded, kernel, height, breadth, transposed):
    channels = padded.shape[2]
    summed = None
    for tap_row in range(3):
        for tap_col in range(3):
            if transposed:
                section = padded[
                    2 - tap_row : 2 - tap_row + height, 2 - tap_col : 2 - tap_col + breadth
                ]
                contract = (((1,), (1,)), ((), ()))
            else:
                section = padded[tap_row : tap_row + height, tap_col : tap_col + breadth]
                contract = (((1,), (0,)), ((), ()))
            product = lax.dot_general(
                section.reshape(height * breadth, channels),
                kernel[tap_row, tap_col],
                contract,
                preferred_element_type=jnp.float32,
            )
            summed = product if summed is None else summed + product
    return summed.reshape(height, breadth, -1)


def silu_slope(value):
    sigma = jax.nn.sigmoid(value)
    return sigma * (1.0 + value * (1.0 - sigma))


def border(height, breadth, margin):
    row_place = lax.axis_index(("row", "cores")) * height - margin + jnp.arange(height + 2 * margin)
    col_place = lax.axis_index("col") * breadth - margin + jnp.arange(breadth + 2 * margin)
    row_inside = (row_place >= 0) & (row_place < height * lax.axis_size(("row", "cores")))
    col_inside = (col_place >= 0) & (col_place < breadth * lax.axis_size("col"))
    return (row_inside[:, None] & col_inside[None, :]).astype(jnp.float32)[:, :, None]


def body(
    latent,
    moment_one,
    moment_two,
    hole_mask,
    target_rgb,
    kernel_one,
    bias_one,
    kernel_two,
    bias_two,
    rgb_weight,
):
    height, breadth = (latent.shape[0], latent.shape[1])
    current, first, second = (latent, moment_one, moment_two)
    known = hole_mask.astype(jnp.float32)
    projection = rgb_weight.astype(jnp.float32)
    inside = border(height, breadth, 1)
    for iteration in range(STEPS):
        rounded = current.astype(jnp.bfloat16)
        wide_latent = extended(rounded, ((("row", "cores"), 0), ("col", 1)), 2)
        pre_one = tap_sum(wide_latent, kernel_one, height + 2, breadth + 2, False) + bias_one
        hidden_one = (jax.nn.silu(pre_one) * inside).astype(jnp.bfloat16)
        pre_two = tap_sum(hidden_one, kernel_two, height, breadth, False) + bias_two
        hidden_two = jax.nn.silu(pre_two).astype(jnp.bfloat16)
        color = jnp.einsum(
            "yxc,kc->kyx", hidden_two, rgb_weight, preferred_element_type=jnp.float32
        )
        residual = known[None] * (color - target_rgb)
        grad_hidden = jnp.einsum(
            "kyx,kc->yxc", residual, projection, precision=lax.Precision.HIGHEST
        )
        grad_two = (grad_hidden * silu_slope(pre_two)).astype(jnp.bfloat16)
        wide_grad = extended(grad_two, ((("row", "cores"), 0), ("col", 1)), 2)
        grad_inner = tap_sum(wide_grad, kernel_two, height + 2, breadth + 2, True)
        grad_one = (grad_inner * silu_slope(pre_one) * inside).astype(jnp.bfloat16)
        gradient = tap_sum(grad_one, kernel_one, height, breadth, True)
        first = BETA_ONE * first + (1.0 - BETA_ONE) * gradient
        second = BETA_TWO * second + (1.0 - BETA_TWO) * gradient * gradient
        current = current - LEARN_RATE * first / (jnp.sqrt(second) + EPSILON)
    return (current, first, second)


def solution(mesh):
    return jax.shard_map(
        body,
        mesh=mesh,
        in_specs=(
            P(("parts", "row", "cores"), "col", None),
            P(("parts", "row", "cores"), "col", None),
            P(("parts", "row", "cores"), "col", None),
            P(("parts", "row", "cores"), "col"),
            P(None, ("parts", "row", "cores"), "col"),
            P(),
            P(),
            P(),
            P(),
            P(),
        ),
        out_specs=(
            P(("parts", "row", "cores"), "col", None),
            P(("parts", "row", "cores"), "col", None),
            P(("parts", "row", "cores"), "col", None),
        ),
        check_vma=False,
    )
```

profile of v0, /device:TPU:26, one launch (start us, length us, event | category | flops | bytes accessed | tf_op | source)
XLA Modules:
  0.0 146.1 jit_solution(4057383952895481771)
XLA Ops:
  0.6 1.1 convert_element_type.42
  1.8 1.9 %collective-permute-start.1 = (bf16[2,128,128]{2,1,0:T(8,128)(2,1)S(1)}, bf16[2,128,128]{2,1,0:T(8,128)(2,1)S(1)}, u32[]{:S(2)}, u32[]{:S(2)}) collective-permute-start(bf16[2,128,128]{2,1,0:T(8,128)(2,1)S(1)} %get-tuple-element.103), channel_id=1, source_target_pairs={{1,0},{4,1},{5,4},{8,5},{9,8},{12,9},{13,12},{3,2},{6,3},{7,6},{10... | collective-permute-start | bytes 196616 | tf_op jit(solution)/shard_map/ppermute | solution.py:23
  3.7 2.4 %collective-permute-start = (bf16[2,128,128]{2,1,0:T(8,128)(2,1)S(1)}, bf16[2,128,128]{2,1,0:T(8,128)(2,1)S(1)}, u32[]{:S(2)}, u32[]{:S(2)}) collective-permute-start(bf16[2,128,128]{2,1,0:T(8,128)(2,1)S(1)} %get-tuple-element.102), channel_id=1, source_target_pairs={{0,1},{1,4},{4,5},{5,8},{8,9},{9,12},{12,13},{2,3},{3,6},{6,7},{7,... | collective-permute-start | bytes 196616 | tf_op jit(solution)/shard_map/ppermute | solution.py:20
  6.1 3.1 %collective-permute-done = bf16[2,128,128]{2,1,0:T(8,128)(2,1)S(1)} collective-permute-done((bf16[2,128,128]{2,1,0:T(8,128)(2,1)S(1)}, bf16[2,128,128]{2,1,0:T(8,128)(2,1)S(1)}, u32[]{:S(2)}, u32[]{:S(2)}) %collective-permute-start) | collective-permute-done | bytes 65568 | tf_op jit(solution)/shard_map/ppermute | solution.py:20
  9.3 2.4 %collective-permute-start.3 = (bf16[12,2,128]{2,1,0:T(2,128)(2,1)S(1)}, bf16[12,2,128]{2,1,0:T(2,128)(2,1)S(1)}, u32[]{:S(2)}, u32[]{:S(2)}) collective-permute-start(bf16[12,2,128]{2,1,0:T(2,128)(2,1)S(1)} %get-tuple-element.59), channel_id=1, source_target_pairs={{2,0},{3,1},{6,4},{7,5},{10,8},{11,9},{14,12},{15,13},{18,16},{19,... | collective-permute-start | bytes 18440 | tf_op jit(solution)/shard_map/ppermute | solution.py:23
  11.7 1.3 collective-permute-start.2
  13.1 4.1 %collective-permute-done.2 = bf16[12,2,128]{2,1,0:T(2,128)(2,1)S(1)} collective-permute-done((bf16[12,2,128]{2,1,0:T(2,128)(2,1)S(1)}, bf16[12,2,128]{2,1,0:T(2,128)(2,1)S(1)}, u32[]{:S(2)}, u32[]{:S(2)}) %collective-permute-start.2) | collective-permute-done | bytes 6176 | tf_op jit(solution)/shard_map/ppermute | solution.py:20
  18.1 0.8 reshape.291
  18.9 0.8 reshape.293
  20.3 0.9 copy-done.2
  21.5 0.7 copy-done.38
  22.5 0.7 copy-done.34
  31.2 1.9 %collective-permute-start.5 = (bf16[2,128,128]{2,1,0:T(8,128)(2,1)S(1)}, bf16[2,128,128]{2,1,0:T(8,128)(2,1)S(1)}, u32[]{:S(2)}, u32[]{:S(2)}) collective-permute-start(bf16[2,128,128]{2,1,0:T(8,128)(2,1)S(1)} %get-tuple-element.101), channel_id=1, source_target_pairs={{1,0},{4,1},{5,4},{8,5},{9,8},{12,9},{13,12},{3,2},{6,3},{7,6},{10... | collective-permute-start | bytes 196616 | tf_op jit(solution)/shard_map/ppermute | solution.py:23
  33.1 2.4 %collective-permute-start.4 = (bf16[2,128,128]{2,1,0:T(8,128)(2,1)S(1)}, bf16[2,128,128]{2,1,0:T(8,128)(2,1)S(1)}, u32[]{:S(2)}, u32[]{:S(2)}) collective-permute-start(bf16[2,128,128]{2,1,0:T(8,128)(2,1)S(1)} %get-tuple-element.100), channel_id=1, source_target_pairs={{0,1},{1,4},{4,5},{5,8},{8,9},{9,12},{12,13},{2,3},{3,6},{6,7},{7,... | collective-permute-start | bytes 196616 | tf_op jit(solution)/shard_map/ppermute | solution.py:20
  35.6 3.2 %collective-permute-done.4 = bf16[2,128,128]{2,1,0:T(8,128)(2,1)S(1)} collective-permute-done((bf16[2,128,128]{2,1,0:T(8,128)(2,1)S(1)}, bf16[2,128,128]{2,1,0:T(8,128)(2,1)S(1)}, u32[]{:S(2)}, u32[]{:S(2)}) %collective-permute-start.4) | collective-permute-done | bytes 65568 | tf_op jit(solution)/shard_map/ppermute | solution.py:20
  38.7 1.7 %collective-permute-start.6 = (bf16[12,2,128]{2,1,0:T(2,128)(2,1)S(1)}, bf16[12,2,128]{2,1,0:T(2,128)(2,1)S(1)}, u32[]{:S(2)}, u32[]{:S(2)}) collective-permute-start(bf16[12,2,128]{2,1,0:T(2,128)(2,1)S(1)} %get-tuple-element.55), channel_id=1, source_target_pairs={{2,0},{3,1},{6,4},{7,5},{10,8},{11,9},{14,12},{15,13},{18,16},{19,... | collective-permute-start | bytes 18440 | tf_op jit(solution)/shard_map/ppermute | solution.py:23
  40.4 1.3 collective-permute-start.7
  41.7 4.2 %collective-permute-done.7 = bf16[12,2,128]{2,1,0:T(2,128)(2,1)S(1)} collective-permute-done((bf16[12,2,128]{2,1,0:T(2,128)(2,1)S(1)}, bf16[12,2,128]{2,1,0:T(2,128)(2,1)S(1)}, u32[]{:S(2)}, u32[]{:S(2)}) %collective-permute-start.7) | collective-permute-done | bytes 6176 | tf_op jit(solution)/shard_map/ppermute | solution.py:20
  46.9 1.0 fusion.178
  47.9 1.8 %reshape.311 = bf16[1300,128]{1,0:T(8,128)(2,1)} reshape(bf16[10,130,128]{2,1,0:T(8,128)(2,1)} %get-tuple-element.34) | data formatting | bytes 665600 | tf_op jit(solution)/shard_map/reshape | solution.py:42
  49.7 1.1 fusion.176
  50.7 1.9 %reshape.313 = bf16[1300,128]{1,0:T(8,128)(2,1)} reshape(bf16[10,130,128]{2,1,0:T(8,128)(2,1)} %get-tuple-element.28) | data formatting | bytes 665600 | tf_op jit(solution)/shard_map/reshape | solution.py:42
  52.6 0.8 reshape.314
  53.4 0.8 reshape.315
  54.4 0.8 reshape.316
  55.4 0.9 copy-done.12
  56.3 0.8 reshape.319
  67.1 1.1 fusion.169
  68.3 2.1 %collective-permute-start.9 = (bf16[2,128,128]{2,1,0:T(8,128)(2,1)S(1)}, bf16[2,128,128]{2,1,0:T(8,128)(2,1)S(1)}, u32[]{:S(2)}, u32[]{:S(2)}) collective-permute-start(bf16[2,128,128]{2,1,0:T(8,128)(2,1)S(1)} %get-tuple-element.99), channel_id=1, source_target_pairs={{1,0},{4,1},{5,4},{8,5},{9,8},{12,9},{13,12},{3,2},{6,3},{7,6},{10... | collective-permute-start | bytes 196616 | tf_op jit(solution)/shard_map/ppermute | solution.py:23
  70.4 2.4 %collective-permute-start.8 = (bf16[2,128,128]{2,1,0:T(8,128)(2,1)S(1)}, bf16[2,128,128]{2,1,0:T(8,128)(2,1)S(1)}, u32[]{:S(2)}, u32[]{:S(2)}) collective-permute-start(bf16[2,128,128]{2,1,0:T(8,128)(2,1)S(1)} %get-tuple-element.98), channel_id=1, source_target_pairs={{0,1},{1,4},{4,5},{5,8},{8,9},{9,12},{12,13},{2,3},{3,6},{6,7},{7,... | collective-permute-start | bytes 196616 | tf_op jit(solution)/shard_map/ppermute | solution.py:20
  72.8 3.1 %collective-permute-done.8 = bf16[2,128,128]{2,1,0:T(8,128)(2,1)S(1)} collective-permute-done((bf16[2,128,128]{2,1,0:T(8,128)(2,1)S(1)}, bf16[2,128,128]{2,1,0:T(8,128)(2,1)S(1)}, u32[]{:S(2)}, u32[]{:S(2)}) %collective-permute-start.8) | collective-permute-done | bytes 65568 | tf_op jit(solution)/shard_map/ppermute | solution.py:20
  76.0 1.7 %collective-permute-start.11 = (bf16[12,2,128]{2,1,0:T(2,128)(2,1)S(1)}, bf16[12,2,128]{2,1,0:T(2,128)(2,1)S(1)}, u32[]{:S(2)}, u32[]{:S(2)}) collective-permute-start(bf16[12,2,128]{2,1,0:T(2,128)(2,1)S(1)} %get-tuple-element.51), channel_id=1, source_target_pairs={{2,0},{3,1},{6,4},{7,5},{10,8},{11,9},{14,12},{15,13},{18,16},{19,... | collective-permute-start | bytes 18440 | tf_op jit(solution)/shard_map/ppermute | solution.py:23
  77.6 1.3 collective-permute-start.10
  79.0 4.2 %collective-permute-done.10 = bf16[12,2,128]{2,1,0:T(2,128)(2,1)S(1)} collective-permute-done((bf16[12,2,128]{2,1,0:T(2,128)(2,1)S(1)}, bf16[12,2,128]{2,1,0:T(2,128)(2,1)S(1)}, u32[]{:S(2)}, u32[]{:S(2)}) %collective-permute-start.10) | collective-permute-done | bytes 6176 | tf_op jit(solution)/shard_map/ppermute | solution.py:20
  85.1 1.0 fusion.175
  86.0 1.8 %reshape.331 = bf16[1300,128]{1,0:T(8,128)(2,1)} reshape(bf16[10,130,128]{2,1,0:T(8,128)(2,1)} %get-tuple-element.25) | data formatting | bytes 665600 | tf_op jit(solution)/shard_map/reshape | solution.py:42
  87.8 1.0 fusion.173
  88.9 1.9 %reshape.333 = bf16[1300,128]{1,0:T(8,128)(2,1)} reshape(bf16[10,130,128]{2,1,0:T(8,128)(2,1)} %get-tuple-element.19) | data formatting | bytes 665600 | tf_op jit(solution)/shard_map/reshape | solution.py:42
  90.7 0.8 reshape.334
  91.5 0.8 reshape.335
  92.5 0.8 reshape.336
  93.5 0.9 copy-done.13
  94.4 0.8 reshape.339
  95.7 0.7 copy-done.40
  96.7 0.7 copy-done.36
  105.5 1.9 %collective-permute-start.13 = (bf16[2,128,128]{2,1,0:T(8,128)(2,1)S(1)}, bf16[2,128,128]{2,1,0:T(8,128)(2,1)S(1)}, u32[]{:S(2)}, u32[]{:S(2)}) collective-permute-start(bf16[2,128,128]{2,1,0:T(8,128)(2,1)S(1)} %get-tuple-element.97), channel_id=1, source_target_pairs={{1,0},{4,1},{5,4},{8,5},{9,8},{12,9},{13,12},{3,2},{6,3},{7,6},{10... | collective-permute-start | bytes 196616 | tf_op jit(solution)/shard_map/ppermute | solution.py:23
  107.4 2.4 %collective-permute-start.12 = (bf16[2,128,128]{2,1,0:T(8,128)(2,1)S(1)}, bf16[2,128,128]{2,1,0:T(8,128)(2,1)S(1)}, u32[]{:S(2)}, u32[]{:S(2)}) collective-permute-start(bf16[2,128,128]{2,1,0:T(8,128)(2,1)S(1)} %get-tuple-element.96), channel_id=1, source_target_pairs={{0,1},{1,4},{4,5},{5,8},{8,9},{9,12},{12,13},{2,3},{3,6},{6,7},{7,... | collective-permute-start | bytes 196616 | tf_op jit(solution)/shard_map/ppermute | solution.py:20
  109.8 3.2 %collective-permute-done.12 = bf16[2,128,128]{2,1,0:T(8,128)(2,1)S(1)} collective-permute-done((bf16[2,128,128]{2,1,0:T(8,128)(2,1)S(1)}, bf16[2,128,128]{2,1,0:T(8,128)(2,1)S(1)}, u32[]{:S(2)}, u32[]{:S(2)}) %collective-permute-start.12) | collective-permute-done | bytes 65568 | tf_op jit(solution)/shard_map/ppermute | solution.py:20
  113.0 1.6 %collective-permute-start.14 = (bf16[12,2,128]{2,1,0:T(2,128)(2,1)S(1)}, bf16[12,2,128]{2,1,0:T(2,128)(2,1)S(1)}, u32[]{:S(2)}, u32[]{:S(2)}) collective-permute-start(bf16[12,2,128]{2,1,0:T(2,128)(2,1)S(1)} %get-tuple-element.47), channel_id=1, source_target_pairs={{2,0},{3,1},{6,4},{7,5},{10,8},{11,9},{14,12},{15,13},{18,16},{19,... | collective-permute-start | bytes 18440 | tf_op jit(solution)/shard_map/ppermute | solution.py:23
  114.7 1.3 collective-permute-start.15
  116.0 4.2 %collective-permute-done.15 = bf16[12,2,128]{2,1,0:T(2,128)(2,1)S(1)} collective-permute-done((bf16[12,2,128]{2,1,0:T(2,128)(2,1)S(1)}, bf16[12,2,128]{2,1,0:T(2,128)(2,1)S(1)}, u32[]{:S(2)}, u32[]{:S(2)}) %collective-permute-start.15) | collective-permute-done | bytes 6176 | tf_op jit(solution)/shard_map/ppermute | solution.py:20
  120.3 0.9 fusion.171
  121.2 0.8 reshape.352
  122.0 1.3 fusion.34
  123.6 1.0 fusion.172
  124.6 1.8 %reshape.351 = bf16[1300,128]{1,0:T(8,128)(2,1)} reshape(bf16[10,130,128]{2,1,0:T(8,128)(2,1)} %get-tuple-element.16) | data formatting | bytes 665600 | tf_op jit(solution)/shard_map/reshape | solution.py:42
  126.4 1.1 fusion.170
  127.5 1.9 %reshape.353 = bf16[1300,128]{1,0:T(8,128)(2,1)} reshape(bf16[10,130,128]{2,1,0:T(8,128)(2,1)} %get-tuple-element.10) | data formatting | bytes 665600 | tf_op jit(solution)/shard_map/reshape | solution.py:42
  129.3 0.8 reshape.354
  130.3 0.8 reshape.355
  131.2 0.8 reshape.356
  132.2 0.8 reshape.358
  133.2 0.8 reshape.359
  144.6 1.4 divide_subtract_fusion
  (242 shorter events, 43.7 us)
Async XLA Ops:
  0.6 28.6 %copy-start = (bf16[3,128]{1,0:T(4,128)(2,1)S(1)}, bf16[3,128]{1,0:T(4,128)(2,1)}, u32[]{:S(2)}) copy-start(bf16[3,128]{1,0:T(4,128)(2,1)} %param.19) | copy-start | bytes 2308
  1.8 4.4 %collective-permute-start.1 = (bf16[2,128,128]{2,1,0:T(8,128)(2,1)S(1)}, bf16[2,128,128]{2,1,0:T(8,128)(2,1)S(1)}, u32[]{:S(2)}, u32[]{:S(2)}) collective-permute-start(bf16[2,128,128]{2,1,0:T(8,128)(2,1)S(1)} %get-tuple-element.103), channel_id=1, source_target_pairs={{1,0},{4,1},{5,4},{8,5},{9,8},{12,9},{13,12},{3,2},{6,3},{7,6},{10... | collective-permute-start | bytes 196616 | tf_op jit(solution)/shard_map/ppermute | solution.py:23
  3.7 5.6 %collective-permute-start = (bf16[2,128,128]{2,1,0:T(8,128)(2,1)S(1)}, bf16[2,128,128]{2,1,0:T(8,128)(2,1)S(1)}, u32[]{:S(2)}, u32[]{:S(2)}) collective-permute-start(bf16[2,128,128]{2,1,0:T(8,128)(2,1)S(1)} %get-tuple-element.102), channel_id=1, source_target_pairs={{0,1},{1,4},{4,5},{5,8},{8,9},{9,12},{12,13},{2,3},{3,6},{6,7},{7,... | collective-permute-start | bytes 196616 | tf_op jit(solution)/shard_map/ppermute | solution.py:20
  9.3 3.8 %collective-permute-start.3 = (bf16[12,2,128]{2,1,0:T(2,128)(2,1)S(1)}, bf16[12,2,128]{2,1,0:T(2,128)(2,1)S(1)}, u32[]{:S(2)}, u32[]{:S(2)}) collective-permute-start(bf16[12,2,128]{2,1,0:T(2,128)(2,1)S(1)} %get-tuple-element.59), channel_id=1, source_target_pairs={{2,0},{3,1},{6,4},{7,5},{10,8},{11,9},{14,12},{15,13},{18,16},{19,... | collective-permute-start | bytes 18440 | tf_op jit(solution)/shard_map/ppermute | solution.py:23
  11.7 1.4 copy-start.54
  11.7 5.5 %collective-permute-start.2 = (bf16[12,2,128]{2,1,0:T(2,128)(2,1)S(1)}, bf16[12,2,128]{2,1,0:T(2,128)(2,1)S(1)}, u32[]{:S(2)}, u32[]{:S(2)}) collective-permute-start(bf16[12,2,128]{2,1,0:T(2,128)(2,1)S(1)} %get-tuple-element.58), channel_id=1, source_target_pairs={{0,2},{1,3},{4,6},{5,7},{8,10},{9,11},{12,14},{13,15},{16,18},{17,... | collective-permute-start | bytes 18440 | tf_op jit(solution)/shard_map/ppermute | solution.py:20
  20.2 1.0 copy-start.2
  21.2 1.0 copy-start.38
  22.1 1.0 copy-start.34
  31.2 4.3 %collective-permute-start.5 = (bf16[2,128,128]{2,1,0:T(8,128)(2,1)S(1)}, bf16[2,128,128]{2,1,0:T(8,128)(2,1)S(1)}, u32[]{:S(2)}, u32[]{:S(2)}) collective-permute-start(bf16[2,128,128]{2,1,0:T(8,128)(2,1)S(1)} %get-tuple-element.101), channel_id=1, source_target_pairs={{1,0},{4,1},{5,4},{8,5},{9,8},{12,9},{13,12},{3,2},{6,3},{7,6},{10... | collective-permute-start | bytes 196616 | tf_op jit(solution)/shard_map/ppermute | solution.py:23
  33.1 5.6 %collective-permute-start.4 = (bf16[2,128,128]{2,1,0:T(8,128)(2,1)S(1)}, bf16[2,128,128]{2,1,0:T(8,128)(2,1)S(1)}, u32[]{:S(2)}, u32[]{:S(2)}) collective-permute-start(bf16[2,128,128]{2,1,0:T(8,128)(2,1)S(1)} %get-tuple-element.100), channel_id=1, source_target_pairs={{0,1},{1,4},{4,5},{5,8},{8,9},{9,12},{12,13},{2,3},{3,6},{6,7},{7,... | collective-permute-start | bytes 196616 | tf_op jit(solution)/shard_map/ppermute | solution.py:20
  38.7 3.0 %collective-permute-start.6 = (bf16[12,2,128]{2,1,0:T(2,128)(2,1)S(1)}, bf16[12,2,128]{2,1,0:T(2,128)(2,1)S(1)}, u32[]{:S(2)}, u32[]{:S(2)}) collective-permute-start(bf16[12,2,128]{2,1,0:T(2,128)(2,1)S(1)} %get-tuple-element.55), channel_id=1, source_target_pairs={{2,0},{3,1},{6,4},{7,5},{10,8},{11,9},{14,12},{15,13},{18,16},{19,... | collective-permute-start | bytes 18440 | tf_op jit(solution)/shard_map/ppermute | solution.py:23
  40.4 5.5 %collective-permute-start.7 = (bf16[12,2,128]{2,1,0:T(2,128)(2,1)S(1)}, bf16[12,2,128]{2,1,0:T(2,128)(2,1)S(1)}, u32[]{:S(2)}, u32[]{:S(2)}) collective-permute-start(bf16[12,2,128]{2,1,0:T(2,128)(2,1)S(1)} %get-tuple-element.54), channel_id=1, source_target_pairs={{0,2},{1,3},{4,6},{5,7},{8,10},{9,11},{12,14},{13,15},{16,18},{17,... | collective-permute-start | bytes 18440 | tf_op jit(solution)/shard_map/ppermute | solution.py:20
  50.7 1.9 %copy-start.15 = (bf16[10,130,128]{2,1,0:T(8,128)(2,1)S(1)}, bf16[10,130,128]{2,1,0:T(8,128)(2,1)}, u32[]{:S(2)}) copy-start(bf16[10,130,128]{2,1,0:T(8,128)(2,1)} %get-tuple-element.33) | copy-start | bytes 998404
  53.4 1.0 copy-start.18
  54.2 1.0 copy-start.10
  55.3 1.0 copy-start.12
  56.3 1.0 copy-start.21
  57.3 1.0 copy-start.39
  58.2 1.0 copy-start.35
  59.2 1.0 copy-start.31
  60.2 1.0 copy-start.24
  61.8 1.0 copy-start.25
  65.6 1.0 copy-start.6
  65.9 1.1 copy-start.3
  65.9 1.2 copy-start.4
  68.3 4.5 %collective-permute-start.9 = (bf16[2,128,128]{2,1,0:T(8,128)(2,1)S(1)}, bf16[2,128,128]{2,1,0:T(8,128)(2,1)S(1)}, u32[]{:S(2)}, u32[]{:S(2)}) collective-permute-start(bf16[2,128,128]{2,1,0:T(8,128)(2,1)S(1)} %get-tuple-element.99), channel_id=1, source_target_pairs={{1,0},{4,1},{5,4},{8,5},{9,8},{12,9},{13,12},{3,2},{6,3},{7,6},{10... | collective-permute-start | bytes 196616 | tf_op jit(solution)/shard_map/ppermute | solution.py:23
  70.4 5.6 %collective-permute-start.8 = (bf16[2,128,128]{2,1,0:T(8,128)(2,1)S(1)}, bf16[2,128,128]{2,1,0:T(8,128)(2,1)S(1)}, u32[]{:S(2)}, u32[]{:S(2)}) collective-permute-start(bf16[2,128,128]{2,1,0:T(8,128)(2,1)S(1)} %get-tuple-element.98), channel_id=1, source_target_pairs={{0,1},{1,4},{4,5},{5,8},{8,9},{9,12},{12,13},{2,3},{3,6},{6,7},{7,... | collective-permute-start | bytes 196616 | tf_op jit(solution)/shard_map/ppermute | solution.py:20
  72.8 10.4 %copy-start.42 = (bf16[2,128,128]{2,1,0:T(8,128)(2,1)}, bf16[2,128,128]{2,1,0:T(8,128)(2,1)S(1)}, u32[]{:S(2)}) copy-start(bf16[2,128,128]{2,1,0:T(8,128)(2,1)S(1)} %collective-permute-done.9) | copy-start | bytes 196612
  75.9 7.2 %copy-start.46 = (bf16[2,128,128]{2,1,0:T(8,128)(2,1)}, bf16[2,128,128]{2,1,0:T(8,128)(2,1)S(1)}, u32[]{:S(2)}) copy-start(bf16[2,128,128]{2,1,0:T(8,128)(2,1)S(1)} %collective-permute-done.8) | copy-start | bytes 196612
  76.0 3.0 %collective-permute-start.11 = (bf16[12,2,128]{2,1,0:T(2,128)(2,1)S(1)}, bf16[12,2,128]{2,1,0:T(2,128)(2,1)S(1)}, u32[]{:S(2)}, u32[]{:S(2)}) collective-permute-start(bf16[12,2,128]{2,1,0:T(2,128)(2,1)S(1)} %get-tuple-element.51), channel_id=1, source_target_pairs={{2,0},{3,1},{6,4},{7,5},{10,8},{11,9},{14,12},{15,13},{18,16},{19,... | collective-permute-start | bytes 18440 | tf_op jit(solution)/shard_map/ppermute | solution.py:23
  77.6 5.5 %collective-permute-start.10 = (bf16[12,2,128]{2,1,0:T(2,128)(2,1)S(1)}, bf16[12,2,128]{2,1,0:T(2,128)(2,1)S(1)}, u32[]{:S(2)}, u32[]{:S(2)}) collective-permute-start(bf16[12,2,128]{2,1,0:T(2,128)(2,1)S(1)} %get-tuple-element.50), channel_id=1, source_target_pairs={{0,2},{1,3},{4,6},{5,7},{8,10},{9,11},{12,14},{13,15},{16,18},{17,... | collective-permute-start | bytes 18440 | tf_op jit(solution)/shard_map/ppermute | solution.py:20
  88.9 1.9 %copy-start.16 = (bf16[10,130,128]{2,1,0:T(8,128)(2,1)S(1)}, bf16[10,130,128]{2,1,0:T(8,128)(2,1)}, u32[]{:S(2)}) copy-start(bf16[10,130,128]{2,1,0:T(8,128)(2,1)} %get-tuple-element.24) | copy-start | bytes 998404
  91.5 1.0 copy-start.19
  93.4 1.0 copy-start.13
  94.4 1.0 copy-start.22
  95.4 1.0 copy-start.40
  96.3 1.0 copy-start.36
  97.3 1.0 copy-start.32
  98.3 1.0 copy-start.26
  99.9 1.0 copy-start.27
  105.5 4.3 %collective-permute-start.13 = (bf16[2,128,128]{2,1,0:T(8,128)(2,1)S(1)}, bf16[2,128,128]{2,1,0:T(8,128)(2,1)S(1)}, u32[]{:S(2)}, u32[]{:S(2)}) collective-permute-start(bf16[2,128,128]{2,1,0:T(8,128)(2,1)S(1)} %get-tuple-element.97), channel_id=1, source_target_pairs={{1,0},{4,1},{5,4},{8,5},{9,8},{12,9},{13,12},{3,2},{6,3},{7,6},{10... | collective-permute-start | bytes 196616 | tf_op jit(solution)/shard_map/ppermute | solution.py:23
  107.4 5.6 %collective-permute-start.12 = (bf16[2,128,128]{2,1,0:T(8,128)(2,1)S(1)}, bf16[2,128,128]{2,1,0:T(8,128)(2,1)S(1)}, u32[]{:S(2)}, u32[]{:S(2)}) collective-permute-start(bf16[2,128,128]{2,1,0:T(8,128)(2,1)S(1)} %get-tuple-element.96), channel_id=1, source_target_pairs={{0,1},{1,4},{4,5},{5,8},{8,9},{9,12},{12,13},{2,3},{3,6},{6,7},{7,... | collective-permute-start | bytes 196616 | tf_op jit(solution)/shard_map/ppermute | solution.py:20
  109.8 10.4 %copy-start.44 = (bf16[2,128,128]{2,1,0:T(8,128)(2,1)}, bf16[2,128,128]{2,1,0:T(8,128)(2,1)S(1)}, u32[]{:S(2)}) copy-start(bf16[2,128,128]{2,1,0:T(8,128)(2,1)S(1)} %collective-permute-done.13) | copy-start | bytes 196612
  113.0 7.2 %copy-start.48 = (bf16[2,128,128]{2,1,0:T(8,128)(2,1)}, bf16[2,128,128]{2,1,0:T(8,128)(2,1)S(1)}, u32[]{:S(2)}) copy-start(bf16[2,128,128]{2,1,0:T(8,128)(2,1)S(1)} %collective-permute-done.12) | copy-start | bytes 196612
  113.0 3.0 %collective-permute-start.14 = (bf16[12,2,128]{2,1,0:T(2,128)(2,1)S(1)}, bf16[12,2,128]{2,1,0:T(2,128)(2,1)S(1)}, u32[]{:S(2)}, u32[]{:S(2)}) collective-permute-start(bf16[12,2,128]{2,1,0:T(2,128)(2,1)S(1)} %get-tuple-element.47), channel_id=1, source_target_pairs={{2,0},{3,1},{6,4},{7,5},{10,8},{11,9},{14,12},{15,13},{18,16},{19,... | collective-permute-start | bytes 18440 | tf_op jit(solution)/shard_map/ppermute | solution.py:23
  114.7 5.5 %collective-permute-start.15 = (bf16[12,2,128]{2,1,0:T(2,128)(2,1)S(1)}, bf16[12,2,128]{2,1,0:T(2,128)(2,1)S(1)}, u32[]{:S(2)}, u32[]{:S(2)}) collective-permute-start(bf16[12,2,128]{2,1,0:T(2,128)(2,1)S(1)} %get-tuple-element.46), channel_id=1, source_target_pairs={{0,2},{1,3},{4,6},{5,7},{8,10},{9,11},{12,14},{13,15},{16,18},{17,... | collective-permute-start | bytes 18440 | tf_op jit(solution)/shard_map/ppermute | solution.py:20
  122.0 1.4 copy-start.45
  122.0 1.4 copy-start.49
  127.5 1.9 %copy-start.17 = (bf16[10,130,128]{2,1,0:T(8,128)(2,1)S(1)}, bf16[10,130,128]{2,1,0:T(8,128)(2,1)}, u32[]{:S(2)}) copy-start(bf16[10,130,128]{2,1,0:T(8,128)(2,1)} %get-tuple-element.15) | copy-start | bytes 998404
  129.3 1.0 copy-start.9
  130.2 1.0 copy-start.20
  131.1 1.0 copy-start.11
  132.2 1.0 copy-start.14
  133.2 1.0 copy-start.23
  134.2 1.0 copy-start.41
  135.1 1.0 copy-start.37
  136.1 1.0 copy-start.33
  137.1 1.0 copy-start.28
  138.4 1.0 copy-start.29
  139.4 1.0 copy-start.30
  143.1 1.0 copy-start.8
  143.4 1.1 copy-start.5
  143.4 1.2 copy-start.7
  (9 other events, 6.8 us)
where the time goes:
time: 148 us; the launch traced here: 146 us
  local copies, waits for them, and re-layouts  56.3 us (38%)
  starting transfers between devices  30.1 us (20%)
  waiting for transfers between devices  29.4 us (20%)
  matrix products  22.2 us (15%)
  other arithmetic  6.22 us (4%)
  between operations  1.83 us (1%)
    ppermute x8, waiting for transfers between devices, extended(): lax.ppermute(lax.slice_in_dim(block, block.shape[dim] - width, None, axis...  29.3 us
    reshape x36, local copies, waits for them, and re-layouts, tap_sum(): section.reshape(height * breadth, channels)  25.1 us
    unnamed x114, local copies, waits for them, and re-layouts  21.4 us
    dot_general x72, matrix products, tap_sum(): lax.dot_general(section.reshape(height * breadth, channels), kernel[tap_r...  20.5 us
    ppermute x8, starting transfers between devices, extended(): lax.ppermute(lax.slice_in_dim(block, 0, width, axis=dim), axis, backward)  15.3 us
    ppermute x8, starting transfers between devices, extended(): lax.ppermute(lax.slice_in_dim(block, block.shape[dim] - width, None, axis...  14.8 us
    slice x8, local copies, waits for them, and re-layouts, tap_sum(): padded[2 - tap_row:2 - tap_row + height, 2 - tap_col:2 - tap_col + breadth]  6.1 us
    slice x7, local copies, waits for them, and re-layouts, tap_sum(): section = padded[tap_row:tap_row + height, tap_col:tap_col + breadth]  3.47 us
  transfers between devices with their start and end apart: 16, of which 8 were waited for; matrix products, arithmetic and copies ran while one was open for 0% of the time, Pallas kernels for 0%

commit v1 on v0

v1 whole, which is shorter than its diff:
```python
import functools
import math

import jax
import jax.numpy as jnp
from jax import lax
from jax.experimental import pallas as pl
from jax.experimental.pallas import tpu as pltpu
from jax.sharding import PartitionSpec as P

STEPS = 2

BETA_ONE = 0.6
BETA_TWO = 0.9
LEARN_RATE = 0.4
EPSILON = 1e-08

ROWS = ("row", "cores")
STRIPS = 16
SIDE = 8
EDGE = 4
PLANES = 7
VMEM = pl.BlockSpec(memory_space=pltpu.VMEM)
ANY = pl.BlockSpec(memory_space=pl.ANY)
F32 = jnp.float32
BF16 = jnp.bfloat16


def row_place():
    cores = lax.axis_size("cores")
    return lax.axis_index("row") * cores + lax.axis_index("cores")


def pairs(count, parity):
    chosen = []
    for low in range(parity, count - 1, 2):
        chosen += [(low, low + 1), (low + 1, low)]
    return chosen


def swap(block, axes, parity):
    return lax.ppermute(block, axes, pairs(lax.axis_size(axes), parity))


def call(kernel, out_shape, in_specs, out_specs, scratch, cost, name):
    return pl.pallas_call(
        kernel,
        out_shape=out_shape,
        in_specs=in_specs,
        out_specs=out_specs,
        scratch_shapes=scratch,
        compiler_params=pltpu.CompilerParams(vmem_limit_bytes=24 << 20),
        cost_estimate=pl.CostEstimate(flops=cost[0], bytes_accessed=cost[1], transcendentals=0),
        name=name,
    )


def shape(dims, dtype):
    return jax.ShapeDtypeStruct(dims, dtype)


def pack_rows(latent, target, mask, near, far, turned, held, planes, sem):
    height = latent.shape[0]
    copy = pltpu.make_async_copy(latent, held, sem)
    copy.start()
    known = mask[...].astype(F32)
    planes[...] = jnp.zeros_like(planes)
    for color in range(3):
        wanted = known * target[color]
        high = wanted.astype(BF16).astype(F32)
        planes[pl.ds(color, height, stride=PLANES), :] = high
        planes[pl.ds(color + 3, height, stride=PLANES), :] = wanted - high
    planes[pl.ds(6, height, stride=PLANES), :] = known
    flat = planes[...].T.astype(BF16)
    turned[...] = flat
    near[EDGE] = flat
    far[EDGE] = flat
    copy.wait()
    even = lax.rem(row_place(), 2) == 0
    last = height - EDGE
    near[:EDGE] = held[pl.ds(jnp.where(even, last, 0), EDGE)].astype(BF16)
    far[:EDGE] = held[pl.ds(jnp.where(even, 0, last), EDGE)].astype(BF16)


def pack_columns(sides, latent, first, second, near, far, turned, *rest):
    outs, (held, flat, sem) = rest[:sides], rest[sides:]
    height, breadth = latent.shape[0], latent.shape[1]
    copies = []
    for number, source in enumerate((latent, first, second)):
        for end, start in enumerate((0, breadth - SIDE)):
            copy = pltpu.make_async_copy(
                source.at[:, pl.ds(start, SIDE)], held.at[number, end], sem.at[number, end]
            )
            copy.start()
            copies.append(copy)
    row_even = lax.rem(row_place(), 2) == 0
    col_even = lax.rem(lax.axis_index("col"), 2) == 0
    starts = (0, breadth - SIDE)
    near_ends = [near[:, s : s + SIDE].astype(F32) for s in starts]
    far_ends = [far[:, s : s + SIDE].astype(F32) for s in starts]
    own_ends = [turned[s : s + SIDE].astype(F32) for s in starts]
    for copy in copies:
        copy.wait()
    full = height + 2 * EDGE
    for side, out in enumerate(outs):
        right = col_even if side == 0 else jnp.logical_not(col_even)
        pick = lambda ends: jnp.where(right, ends[1], ends[0])
        close, away = pick(near_ends), pick(far_ends)
        above = jnp.where(row_even, away, close)
        below = jnp.where(row_even, close, away)
        middle = pick([held[0, end] for end in range(2)])
        flat[: EDGE * SIDE] = above[:EDGE].reshape(EDGE * SIDE, -1)
        flat[EDGE * SIDE : (EDGE + height) * SIDE] = middle.reshape(height * SIDE, -1)
        flat[(EDGE + height) * SIDE : full * SIDE] = below[:EDGE].reshape(EDGE * SIDE, -1)
        at = full * SIDE
        for piece in (above[EDGE], pick(own_ends), below[EDGE]):
            flat[at : at + SIDE] = piece
            at += SIDE
        flat[at : at + SIDE] = jnp.zeros_like(own_ends[0])
        at += SIDE
        low = middle - middle.astype(BF16).astype(F32)
        for piece in (low, pick([held[1, e] for e in range(2)]), pick([held[2, e] for e in range(2)])):
            for row in range(height):
                nearest = jnp.where(right, piece[row, SIDE - EDGE :], piece[row, :EDGE])
                flat[at : at + EDGE] = nearest
                at += EDGE
        out[...] = flat[...].astype(BF16)


def packed_length(height):
    return (height + 2 * EDGE) * SIDE + 4 * SIDE + 3 * height * EDGE


def pack_weights(one, two, rgb, ahead_one, ahead_two, back_one, back_two, colors, held):
    size = one.shape[2]
    for kernel, ahead, back in ((one, ahead_one, back_one), (two, ahead_two, back_two)):
        for row in range(4):
            for col in range(3):
                at = (row * 3 + col) * size
                for out in range(2):
                    tap = row - out
                    if 0 <= tap <= 2:
                        front = kernel[tap, col]
                        rear = kernel[2 - tap, 2 - col].astype(F32).T.astype(BF16)
                    else:
                        front = rear = jnp.zeros((size, size), BF16)
                    ahead[at : at + size, out * size : (out + 1) * size] = front
                    back[at : at + size, out * size : (out + 1) * size] = rear
    held[...] = jnp.zeros_like(held)
    held[0:3] = rgb[...].astype(F32)
    held[3:6] = rgb[...].astype(F32)
    colors[...] = held[...].astype(BF16)


def put(dest, row, value, strip):
    dest[row, 1 : strip + 1] = value.astype(BF16).reshape(strip, STRIPS, -1)
    dest[row, 0] = pltpu.roll(value[(strip - 1) * STRIPS :], 1, 0).astype(BF16)
    dest[row, strip + 1] = pltpu.roll(value[:STRIPS], STRIPS - 1, 0).astype(BF16)


def conv_pair(source, row, weights, strip):
    taps = [
        source[row + down, across : across + strip].reshape(strip * STRIPS, -1)
        for down in range(4)
        for across in range(3)
    ]
    return jnp.dot(jnp.concatenate(taps, axis=1), weights[...], preferred_element_type=F32)


def strips_of(source, row, strip):
    return jnp.concatenate(
        [source[row, pl.ds(j, STRIPS, stride=strip), :] for j in range(strip)], axis=0
    )


def sigma_of(value):
    return 0.5 * jnp.tanh(0.5 * value) + 0.5


def gradient(height, strip, refs, weights, aims, known, inside, emit):
    wide, hidden, slope, grad_two, grad_one = refs
    ahead_one, ahead_two, back_one, back_two, colors, bias_one, bias_two = weights
    size = wide.shape[-1]
    place, count = row_place(), lax.axis_size("row") * lax.axis_size("cores")
    top = (place > 0).astype(F32)
    bottom = (place < count - 1).astype(F32)
    columns = inside[...]
    halves = lambda both: (both[:, :size], both[:, size:])
    pixels = strip * STRIPS

    for pair in range((height + 6) // 2):
        for half, summed in enumerate(halves(conv_pair(wide, 2 * pair, ahead_one, strip))):
            row = 2 * pair + half
            value = summed + bias_one[...]
            sigma = sigma_of(value)
            hid = value * sigma
            keep = columns
            if row < 3:
                keep = columns * top
            elif row >= height + 3:
                keep = columns * bottom
            put(hidden, row, hid * keep, strip)
            if 2 <= row < height + 4:
                slope[row - 2] = (sigma + hid * (1.0 - sigma)) * keep

    lane = lax.broadcasted_iota(jnp.int32, (2 * pixels, size), 1)
    for pair in range((height + 4) // 2):
        both = conv_pair(hidden, 2 * pair, ahead_two, strip)
        value = jnp.concatenate(halves(both), axis=0) + bias_two[...]
        sigma = sigma_of(value)
        hid = value * sigma
        color = lax.dot_general(
            hid.astype(BF16), colors[...], (((1,), (1,)), ((), ())), preferred_element_type=F32
        )
        spot = slice(2 * pair, 2 * pair + 2)
        residual = known[spot].reshape(2 * pixels, -1) * color - aims[spot].reshape(2 * pixels, -1)
        rest = residual - residual.astype(BF16).astype(F32)
        split = jnp.where(lane < 3, residual, rest).astype(BF16)
        spread = jnp.dot(split, colors[...], preferred_element_type=F32)
        result = spread * (sigma + hid * (1.0 - sigma))
        for half in range(2):
            put(grad_two, 2 * pair + half, result[half * pixels : (half + 1) * pixels], strip)

    for pair in range((height + 2) // 2):
        for half, summed in enumerate(halves(conv_pair(grad_two, 2 * pair, back_two, strip))):
            row = 2 * pair + half
            put(grad_one, row, summed * slope[row], strip)

    for pair in range(height // 2):
        for half, summed in enumerate(halves(conv_pair(grad_one, 2 * pair, back_one, strip))):
            emit(2 * pair + half, summed)


def adam(current, first, second, grad):
    first = BETA_ONE * first + (1.0 - BETA_ONE) * grad
    second = BETA_TWO * second + (1.0 - BETA_TWO) * grad * grad
    return current - LEARN_RATE * first / (jnp.sqrt(second) + EPSILON), first, second


def first_step(sides, *refs):
    latent, moment_one, moment_two, near, far, turned = refs[:6]
    columns = refs[6 : 6 + sides]
    refs = refs[6 + sides :]
    weights, refs = refs[:7], refs[7:]
    (own, near_out, far_out, z_out, m_out, v_out, aims, known, inside), refs = refs[:9], refs[9:]
    z_held, m_held, v_held, flat, turn, wide, hidden, slope, grad_two, grad_one, sem = refs
    height, breadth, size = latent.shape
    strip = (breadth + 2 * SIDE) // STRIPS
    pixels = strip * STRIPS
    full = height + 2 * EDGE

    copies = []
    for number, (source, dest) in enumerate(
        (
            (latent, z_held.at[pl.ds(EDGE, height), pl.ds(SIDE, breadth)]),
            (moment_one, m_held.at[:, pl.ds(SIDE, breadth)]),
            (moment_two, v_held.at[:, pl.ds(SIDE, breadth)]),
        )
    ):
        copy = pltpu.make_async_copy(source, dest, sem.at[number])
        copy.start()
        copies.append(copy)

    place, col = row_place(), lax.axis_index("col")
    row_even, col_even = lax.rem(place, 2) == 0, lax.rem(col, 2) == 0

    base = col * breadth - SIDE
    total = lax.axis_size("col") * breadth
    for j in range(strip):
        at = lax.broadcasted_iota(jnp.int32, (STRIPS, size), 0) * strip + (j + base)
        inside[j * STRIPS : (j + 1) * STRIPS] = ((at >= 0) & (at < total)).astype(F32)

    for source, low in ((near, row_even), (far, jnp.logical_not(row_even))):
        start = jnp.where(low, height + EDGE, 0)
        z_held[pl.ds(start, EDGE), SIDE : SIDE + breadth] = source[:EDGE].astype(F32)
        turn[jnp.where(low, 2, 0), SIDE : SIDE + breadth] = source[EDGE].astype(F32)
    turn[1, SIDE : SIDE + breadth] = turned[...].astype(F32)

    for side in range(2):
        right = col_even if side == 0 else jnp.logical_not(col_even)
        start = pl.multiple_of(jnp.where(right, SIDE + breadth, 0), SIDE)
        spot = pl.ds(start, SIDE)
        if side >= sides:
            for held in (z_held, m_held, v_held, turn):
                held[:, spot] = jnp.zeros((held.shape[0], SIDE, size), F32)
            continue
        flat[...] = columns[side][...].astype(F32)
        z_held[:, spot] = flat[: full * SIDE].reshape(full, SIDE, size)
        at = full * SIDE
        turn[:, spot] = flat[at : at + 3 * SIDE].reshape(3, SIDE, size)
        at += 4 * SIDE
        blank = jnp.zeros((SIDE - EDGE, size), F32)
        for number, held in enumerate((z_held, m_held, v_held)):
            for row in range(height):
                piece = flat[at : at + EDGE]
                at += EDGE
                piece = jnp.where(
                    right,
                    jnp.concatenate([piece, blank], axis=0),
                    jnp.concatenate([blank, piece], axis=0),
                )
                if number == 0:
                    held[EDGE + row, spot] += piece
                else:
                    held[row, spot] = piece

    lane_in = lax.broadcasted_iota(jnp.int32, (size, 2 * size), 0)
    lane_out = lax.broadcasted_iota(jnp.int32, (size, 2 * size), 1)
    color = lax.rem(lane_out, 3)
    aimed = (lane_out < 6) & ((lane_in == color) | (lane_in == color + 3))
    masked = (lane_out >= size) & (lane_out < size + 6) & (lane_in == 6)
    chosen = (aimed | masked).astype(F32).astype(BF16)
    turned_strips = [strips_of(turn, slot, strip) for slot in range(3)]
    for row in range(height + 4):
        slot, source = (0, height - 2 + row) if row < 2 else (1, row - 2)
        if row >= height + 2:
            slot, source = 2, row - height - 2
        value = turned_strips[slot]
        if source:
            value = pltpu.roll(value, size - PLANES * source, 1)
        both = jnp.dot(value.astype(BF16), chosen, preferred_element_type=F32)
        aims[row] = both[:, :size]
        known[row] = both[:, size:]

    copies[0].wait()
    for row in range(full):
        put(wide, row, strips_of(z_held, row, strip), strip)
    copies[1].wait()
    copies[2].wait()

    def emit(row, grad):
        current, first, second = adam(
            strips_of(z_held, EDGE + row, strip),
            strips_of(m_held, row, strip),
            strips_of(v_held, row, strip),
            grad,
        )
        current = current * inside[...]
        z_out[row] = current
        m_out[row] = first
        v_out[row] = second
        put(own, row, current, strip)

    gradient(
        height, strip, (wide, hidden, slope, grad_two, grad_one), weights, aims, known, inside, emit
    )
    last = height - EDGE
    near_out[...] = own[pl.ds(jnp.where(row_even, last, 0), EDGE)]
    far_out[...] = own[pl.ds(jnp.where(row_even, 0, last), EDGE)]


def last_step(*refs):
    own, near, far, z_in, m_in, v_in, aims, known, inside = refs[:9]
    weights, refs = refs[9:16], refs[16:]
    (z_out, m_out, v_out), refs = refs[:3], refs[3:]
    z_held, m_held, v_held, wide, hidden, slope, grad_two, grad_one, sem = refs
    height, breadth, size = z_out.shape
    strip = (breadth + 2 * SIDE) // STRIPS
    row_even = lax.rem(row_place(), 2) == 0
    wide[EDGE : EDGE + height] = own[...]
    wide[pl.ds(jnp.where(row_even, height + EDGE, 0), EDGE)] = near[...]
    wide[pl.ds(jnp.where(row_even, 0, height + EDGE), EDGE)] = far[...]
    copies = []

    def emit(row, grad):
        results = adam(z_in[row], m_in[row], v_in[row], grad)
        for number, (held, out, value) in enumerate(
            zip((z_held, m_held, v_held), (z_out, m_out, v_out), results)
        ):
            for j in range(strip):
                held[row, pl.ds(j, STRIPS, stride=strip), :] = value[
                    j * STRIPS : (j + 1) * STRIPS
                ]
            copy = pltpu.make_async_copy(
                held.at[row, pl.ds(SIDE, breadth)], out.at[row], sem.at[number, row]
            )
            copy.start()
            copies.append(copy)

    gradient(
        height, strip, (wide, hidden, slope, grad_two, grad_one), weights, aims, known, inside, emit
    )
    for copy in copies:
        copy.wait()


def body(
    latent,
    moment_one,
    moment_two,
    hole_mask,
    target_rgb,
    kernel_one,
    bias_one,
    kernel_two,
    bias_two,
    rgb_weight,
):
    height, breadth, size = latent.shape
    strip = (breadth + 2 * SIDE) // STRIPS
    assert strip * STRIPS == breadth + 2 * SIDE and height % 2 == 0
    assert height * PLANES <= size and breadth == size
    pixels = strip * STRIPS
    full = height + 2 * EDGE
    sides = 1 if lax.axis_size("col") == 2 else 2
    length = packed_length(height)
    dma = pltpu.SemaphoreType.DMA

    near, far, turned = call(
        pack_rows,
        [shape((EDGE + 1, breadth, size), BF16)] * 2 + [shape((breadth, size), BF16)],
        [ANY, VMEM, VMEM],
        [VMEM] * 3,
        [pltpu.VMEM((height, breadth, size), F32), pltpu.VMEM((size, breadth), F32), dma],
        (10**6, 10**6),
        "pack_rows",
    )(latent, target_rgb, hole_mask)
    near = swap(near, ROWS, 0)
    far = swap(far, ROWS, 1)

    matrix = shape((12 * size, 2 * size), BF16)
    packed = call(
        pack_weights,
        [matrix] * 4 + [shape((size, size), BF16)],
        [VMEM] * 3,
        [VMEM] * 5,
        [pltpu.VMEM((size, size), F32)],
        (10**6, 4 * 10**6),
        "pack_weights",
    )(kernel_one, kernel_two, rgb_weight)
    weights = (*packed, bias_one[None], bias_two[None])

    columns = call(
        functools.partial(pack_columns, sides),
        [shape((length, size), BF16)] * sides,
        [ANY] * 3 + [VMEM] * 3,
        [VMEM] * sides,
        [pltpu.VMEM((3, 2, height, SIDE, size), F32), pltpu.VMEM((length, size), F32), dma((3, 2))],
        (10**5, 10**5),
        "pack_columns",
    )(latent, moment_one, moment_two, near, far, turned)
    columns = [swap(block, "col", side) for side, block in enumerate(columns)]

    work = 4 * 2 * 12 * 11 * pixels * size * size
    tall = lambda rows: pltpu.VMEM((rows, strip + 2, STRIPS, size), BF16)
    scratch = [
        tall(full),
        tall(height + 6),
        pltpu.VMEM((height + 2, pixels, size), F32),
        tall(height + 4),
        tall(height + 2),
    ]
    held = pltpu.VMEM((height, pixels, size), F32)
    half = shape((EDGE, strip + 2, STRIPS, size), BF16)
    lines = shape((height, pixels, size), F32)
    aims = shape((height + 4, pixels, size), F32)
    own, near, far, z, m, v, aims, known, inside = call(
        functools.partial(first_step, sides),
        [shape((height, strip + 2, STRIPS, size), BF16), half, half, lines, lines, lines]
        + [aims, aims, shape((pixels, size), F32)],
        [ANY] * 3 + [VMEM] * (3 + sides + 7),
        [VMEM] * 9,
        [pltpu.VMEM((full, pixels, size), F32), held, held, pltpu.VMEM((length, size), F32)]
        + [pltpu.VMEM((3, pixels, size), F32)]
        + scratch
        + [dma((3,))],
        (work, 10**7),
        "first_step",
    )(latent, moment_one, moment_two, near, far, turned, *columns, *weights)
    near = swap(near, ROWS, 0)
    far = swap(far, ROWS, 1)

    out = shape(latent.shape, F32)
    return call(
        last_step,
        [out] * 3,
        [VMEM] * 16,
        [ANY] * 3,
        [held] * 3 + scratch + [dma((3, height))],
        (work, 10**7),
        "last_step",
    )(own, near, far, z, m, v, aims, known, inside, *weights)


def solution(mesh):
    tile = P(("parts", "row", "cores"), "col", None)
    return jax.shard_map(
        body,
        mesh=mesh,
        in_specs=(
            tile,
            tile,
            tile,
            P(("parts", "row", "cores"), "col"),
            P(None, ("parts", "row", "cores"), "col"),
            P(),
            P(),
            P(),
            P(),
            P(),
        ),
        out_specs=(tile, tile, tile),
        check_vma=False,
    )
```

time: 148 us -> 36.7 us (0.25)
  the two profiles are of different devices: /device:TPU:26 before, /device:TPU:1 now
where the time goes in v1:
time: 36.7 us; the launch traced here: 36.4 us
  Pallas kernels  13 us (35%)
  starting transfers between devices  11.3 us (31%)
  waiting for transfers between devices  7.2 us (20%)
  local copies, waits for them, and re-layouts  4.16 us (11%)
  between operations  0.74 us (2%)
    ppermute x5, starting transfers between devices, swap(): return lax.ppermute(block, axes, pairs(lax.axis_size(axes), parity))  11.3 us
    ppermute x5, waiting for transfers between devices, swap(): return lax.ppermute(block, axes, pairs(lax.axis_size(axes), parity))  7.2 us
    pallas_call x1, Pallas kernels, body(): call(last_step, [out] * 3, [VMEM] * 16, [ANY] * 3, [held] * 3 + scratch +...  6.14 us
    pallas_call x1, Pallas kernels, body(): call(functools.partial(first_step, sides), [shape((height, strip + 2, STR...  5.96 us
    unnamed x24, local copies, waits for them, and re-layouts  4.16 us
  transfers between devices with their start and end apart: 5, of which 3 were waited for; matrix products, arithmetic and copies ran while one was open for 0% of the time, Pallas kernels for 2%

profile of v1, /device:TPU:1, one launch (start us, length us, event | category | flops | bytes accessed | tf_op | source)
XLA Modules:
  0.0 36.4 jit_solution(16157357932492641832)
XLA Ops:
  0.6 0.0 copy-start
  0.6 1.0 %copy-done = f32[8,128,128]{2,1,0:T(8,128)S(1)} copy-done((f32[8,128,128]{2,1,0:T(8,128)S(1)}, f32[8,128,128]{2,1,0:T(8,128)}, u32[]{:S(2)}) %copy-start) | copy-done | bytes 524312
  1.7 0.0 copy-start.7
  1.7 0.7 %copy-done.7 = f32[3,8,128]{2,1,0:T(8,128)S(1)} copy-done((f32[3,8,128]{2,1,0:T(8,128)S(1)}, f32[3,8,128]{2,1,0:T(8,128)}, u32[]{:S(2)}) %copy-start.7) | copy-done | bytes 12312
  2.4 0.0 copy-start.8
  2.4 0.7 %copy-done.8 = s32[8,128]{1,0:T(8,128)S(1)} copy-done((s32[8,128]{1,0:T(8,128)S(1)}, s32[8,128]{1,0:T(8,128)}, u32[]{:S(2)}) %copy-start.8) | copy-done | bytes 4120
  3.1 0.0 copy-start.2
  3.1 0.2 pack_rows.1
  3.3 0.1 collective-permute-start
  3.4 4.6 %collective-permute-start.1 = (bf16[5,128,128]{2,1,0:T(8,128)(2,1)S(1)}, bf16[5,128,128]{2,1,0:T(8,128)(2,1)S(1)}, u32[]{:S(2)}, u32[]{:S(2)}) collective-permute-start(bf16[5,128,128]{2,1,0:T(8,128)(2,1)S(1)} %get-tuple-element.21), channel_id=1, source_target_pairs={{1,4},{4,1},{5,8},{8,5},{9,12},{12,9},{3,6},{6,3},{7,10},{10,7},{1... | collective-permute-start | bytes 491528 | tf_op jit(solution)/shard_map/ppermute | solution.py:42
  7.9 0.0 collective-permute-done.near.refs_3_
  7.9 3.0 %collective-permute-done.1.far.refs_4_ = bf16[5,128,128]{2,1,0:T(8,128)(2,1)S(1)} collective-permute-done((bf16[5,128,128]{2,1,0:T(8,128)(2,1)S(1)}, bf16[5,128,128]{2,1,0:T(8,128)(2,1)S(1)}, u32[]{:S(2)}, u32[]{:S(2)}) %collective-permute-start.1) | collective-permute-done | bytes 163872 | tf_op jit(solution)/shard_map/ppermute | solution.py:42
  10.9 0.0 copy-done.2
  10.9 0.0 copy-start.3
  10.9 1.0 %copy-done.3 = f32[8,128,128]{2,1,0:T(8,128)S(1)} copy-done((f32[8,128,128]{2,1,0:T(8,128)S(1)}, f32[8,128,128]{2,1,0:T(8,128)}, u32[]{:S(2)}) %copy-start.3) | copy-done | bytes 524312
  12.0 0.0 copy-start.5
  12.0 0.0 copy-start.6
  12.0 0.0 copy-start.9
  12.0 0.0 copy-start.4
  12.0 0.1 pack_columns.1
  12.1 0.0 copy-start.1
  12.2 1.8 %collective-permute-start.2 = (bf16[256,128]{1,0:T(8,128)(2,1)S(1)}, bf16[256,128]{1,0:T(8,128)(2,1)S(1)}, u32[]{:S(2)}, u32[]{:S(2)}) collective-permute-start(bf16[256,128]{1,0:T(8,128)(2,1)S(1)} %pack_columns.1), channel_id=1, source_target_pairs={{0,2},{2,0},{1,3},{3,1},{4,6},{6,4},{5,7},{7,5},{8,10},{10,8},{9,1... | collective-permute-start | bytes 196616 | tf_op jit(solution)/shard_map/ppermute | solution.py:42
  14.0 0.0 copy-done.5
  14.0 0.0 copy-done.6
  14.0 0.0 copy-done.9
  14.0 0.6 %pack_weights.1 = (bf16[1536,256]{1,0:T(8,128)(2,1)S(1)}, bf16[1536,256]{1,0:T(8,128)(2,1)S(1)}, bf16[1536,256]{1,0:T(8,128)(2,1)S(1)}, bf16[1536,256]{1,0:T(8,128)(2,1)S(1)}, bf16[128,128]{1,0:T(8,128)(2,1)S(1)}) custom-call(bf16[3,3,128,128]{3,2,1,0:T(8,128)(2,1)S(1)} %copy-done.5, bf16[3,3,128,128]{3,2,1,0:T(8,128)(2,1)S(1)} %copy-done.6, ...), custom_call_target="tpu_custom_call" | custom-call | flops 1000000 | bytes 4000000 | tf_op jit(solution)/shard_map/pack_weights/pallas_call | solution.py:422
  14.5 1.1 %collective-permute-done.2.refs_6_ = bf16[256,128]{1,0:T(8,128)(2,1)S(1)} collective-permute-done((bf16[256,128]{1,0:T(8,128)(2,1)S(1)}, bf16[256,128]{1,0:T(8,128)(2,1)S(1)}, u32[]{:S(2)}, u32[]{:S(2)}) %collective-permute-start.2) | collective-permute-done | bytes 65568 | tf_op jit(solution)/shard_map/ppermute | solution.py:42
  15.6 0.0 copy-start.10
  15.6 0.0 copy-start.11
  15.6 0.0 copy-done.4
  15.6 0.0 copy-done.1
  15.6 0.6 %copy-done.10 = f32[128]{0:T(128)S(1)} copy-done((f32[128]{0:T(128)S(1)}, f32[128]{0:T(128)}, u32[]{:S(2)}) %copy-start.10) | copy-done | bytes 536
  16.3 0.0 copy-done.11
  16.3 6.0 %first_step.1 = (bf16[8,11,16,128]{3,2,1,0:T(8,128)(2,1)S(1)}, bf16[4,11,16,128]{3,2,1,0:T(8,128)(2,1)S(1)}, bf16[4,11,16,128]{3,2,1,0:T(8,128)(2,1)S(1)}, f32[8...) custom-call(f32[8,128,128]{2,1,0:T(8,128)S(1)} %copy-done.1, ...), custom_call_target="tpu_custom_call" | custom-call | flops 2491416576 | bytes 10000000 | tf_op jit(solution)/shard_map/first_step/pallas_call | solution.py:457
  22.2 0.1 collective-permute-start.3
  22.3 4.8 %collective-permute-start.4 = (bf16[4,11,16,128]{3,2,1,0:T(8,128)(2,1)S(1)}, bf16[4,11,16,128]{3,2,1,0:T(8,128)(2,1)S(1)}, u32[]{:S(2)}, u32[]{:S(2)}) collective-permute-start(bf16[4,11,16,128]{3,2,1,0:T(8,128)(2,1)S(1)} %get-tuple-element.30), channel_id=1, source_target_pairs={{1,4},{4,1},{5,8},{8,5},{9,12},{12,9},{3,6},{6,3},{7,10},{10,7},{1... | collective-permute-start | bytes 540680 | tf_op jit(solution)/shard_map/ppermute | solution.py:42
  27.1 0.0 collective-permute-done.3.refs_1_
  27.1 3.2 %collective-permute-done.4.refs_2_ = bf16[4,11,16,128]{3,2,1,0:T(8,128)(2,1)S(1)} collective-permute-done((bf16[4,11,16,128]{3,2,1,0:T(8,128)(2,1)S(1)}, bf16[4,11,16,128]{3,2,1,0:T(8,128)(2,1)S(1)}, u32[]{:S(2)}, u32[]{:S(2)}) %collective-permute-start.4) | collective-permute-done | bytes 180256 | tf_op jit(solution)/shard_map/ppermute | solution.py:42
  30.3 6.1 %last_step.1 = (f32[8,128,128]{2,1,0:T(8,128)}, f32[8,128,128]{2,1,0:T(8,128)}, f32[8,128,128]{2,1,0:T(8,128)}) custom-call(bf16[8,11,16,128]{3,2,1,0:T(8,128)(2,1)S(1)} %get-tuple-element.28.refs_0_, bf16[4,11,16,128]{3,2,1,0:T(8,128)(2,1)S(1)} %collective-permute-done.3.refs_1_, bf16[4,11,16,128]{3,2,1,0:T(8,128)(2,1)S(1)} %collective-permute-done.4.refs_2_, ...), custom_call_target="tpu_custom_call" | custom-call | flops 2491416576 | bytes 10000000 | tf_op jit(solution)/shard_map/last_step/pallas_call | solution.py:474
Async XLA Ops:
  0.6 1.0 %copy-start = (f32[8,128,128]{2,1,0:T(8,128)S(1)}, f32[8,128,128]{2,1,0:T(8,128)}, u32[]{:S(2)}) copy-start(f32[8,128,128]{2,1,0:T(8,128)} %refs_0_.1) | copy-start | bytes 1572868
  1.7 0.7 %copy-start.7 = (f32[3,8,128]{2,1,0:T(8,128)S(1)}, f32[3,8,128]{2,1,0:T(8,128)}, u32[]{:S(2)}) copy-start(f32[3,8,128]{2,1,0:T(8,128)} %target.1) | copy-start | bytes 36868
  2.4 0.7 %copy-start.8 = (s32[8,128]{1,0:T(8,128)S(1)}, s32[8,128]{1,0:T(8,128)}, u32[]{:S(2)}) copy-start(s32[8,128]{1,0:T(8,128)} %mask.1) | copy-start | bytes 12292
  3.1 7.9 %copy-start.2 = (f32[8,128,128]{2,1,0:T(8,128)S(1)}, f32[8,128,128]{2,1,0:T(8,128)}, u32[]{:S(2)}) copy-start(f32[8,128,128]{2,1,0:T(8,128)} %refs_1_.1) | copy-start | bytes 1572868
  3.3 4.7 %collective-permute-start = (bf16[5,128,128]{2,1,0:T(8,128)(2,1)S(1)}, bf16[5,128,128]{2,1,0:T(8,128)(2,1)S(1)}, u32[]{:S(2)}, u32[]{:S(2)}) collective-permute-start(bf16[5,128,128]{2,1,0:T(8,128)(2,1)S(1)} %get-tuple-element.20), channel_id=1, source_target_pairs={{0,1},{1,0},{4,5},{5,4},{8,9},{9,8},{12,13},{13,12},{2,3},{3,2},{6... | collective-permute-start | bytes 491528 | tf_op jit(solution)/shard_map/ppermute | solution.py:42
  3.4 7.6 %collective-permute-start.1 = (bf16[5,128,128]{2,1,0:T(8,128)(2,1)S(1)}, bf16[5,128,128]{2,1,0:T(8,128)(2,1)S(1)}, u32[]{:S(2)}, u32[]{:S(2)}) collective-permute-start(bf16[5,128,128]{2,1,0:T(8,128)(2,1)S(1)} %get-tuple-element.21), channel_id=1, source_target_pairs={{1,4},{4,1},{5,8},{8,5},{9,12},{12,9},{3,6},{6,3},{7,10},{10,7},{1... | collective-permute-start | bytes 491528 | tf_op jit(solution)/shard_map/ppermute | solution.py:42
  10.9 1.0 %copy-start.3 = (f32[8,128,128]{2,1,0:T(8,128)S(1)}, f32[8,128,128]{2,1,0:T(8,128)}, u32[]{:S(2)}) copy-start(f32[8,128,128]{2,1,0:T(8,128)} %refs_2_.1) | copy-start | bytes 1572868
  12.0 2.0 %copy-start.5 = (bf16[3,3,128,128]{3,2,1,0:T(8,128)(2,1)S(1)}, bf16[3,3,128,128]{3,2,1,0:T(8,128)(2,1)}, u32[]{:S(2)}) copy-start(bf16[3,3,128,128]{3,2,1,0:T(8,128)(2,1)} %one.1) | copy-start | bytes 884740
  12.0 2.0 %copy-start.6 = (bf16[3,3,128,128]{3,2,1,0:T(8,128)(2,1)S(1)}, bf16[3,3,128,128]{3,2,1,0:T(8,128)(2,1)}, u32[]{:S(2)}) copy-start(bf16[3,3,128,128]{3,2,1,0:T(8,128)(2,1)} %two.1) | copy-start | bytes 884740
  12.0 2.0 %copy-start.9 = (bf16[3,128]{1,0:T(4,128)(2,1)S(1)}, bf16[3,128]{1,0:T(4,128)(2,1)}, u32[]{:S(2)}) copy-start(bf16[3,128]{1,0:T(4,128)(2,1)} %rgb.1) | copy-start | bytes 2308
  12.0 3.6 %copy-start.4 = (f32[8,128,128]{2,1,0:T(8,128)S(1)}, f32[8,128,128]{2,1,0:T(8,128)}, u32[]{:S(2)}) copy-start(f32[8,128,128]{2,1,0:T(8,128)} %refs_2_.1) | copy-start | bytes 1572868
  12.1 3.5 %copy-start.1 = (f32[8,128,128]{2,1,0:T(8,128)S(1)}, f32[8,128,128]{2,1,0:T(8,128)}, u32[]{:S(2)}) copy-start(f32[8,128,128]{2,1,0:T(8,128)} %refs_0_.1) | copy-start | bytes 1572868
  12.2 3.5 %collective-permute-start.2 = (bf16[256,128]{1,0:T(8,128)(2,1)S(1)}, bf16[256,128]{1,0:T(8,128)(2,1)S(1)}, u32[]{:S(2)}, u32[]{:S(2)}) collective-permute-start(bf16[256,128]{1,0:T(8,128)(2,1)S(1)} %pack_columns.1), channel_id=1, source_target_pairs={{0,2},{2,0},{1,3},{3,1},{4,6},{6,4},{5,7},{7,5},{8,10},{10,8},{9,1... | collective-permute-start | bytes 196616 | tf_op jit(solution)/shard_map/ppermute | solution.py:42
  15.6 0.7 %copy-start.10 = (f32[128]{0:T(128)S(1)}, f32[128]{0:T(128)}, u32[]{:S(2)}) copy-start(f32[128]{0:T(128)} %param.16) | copy-start | bytes 1540
  15.6 0.7 %copy-start.11 = (f32[128]{0:T(128)S(1)}, f32[128]{0:T(128)}, u32[]{:S(2)}) copy-start(f32[128]{0:T(128)} %param.18) | copy-start | bytes 1540
  22.2 4.8 %collective-permute-start.3 = (bf16[4,11,16,128]{3,2,1,0:T(8,128)(2,1)S(1)}, bf16[4,11,16,128]{3,2,1,0:T(8,128)(2,1)S(1)}, u32[]{:S(2)}, u32[]{:S(2)}) collective-permute-start(bf16[4,11,16,128]{3,2,1,0:T(8,128)(2,1)S(1)} %get-tuple-element.29), channel_id=1, source_target_pairs={{0,1},{1,0},{4,5},{5,4},{8,9},{9,8},{12,13},{13,12},{2,3},{3,2},{6... | collective-permute-start | bytes 540680 | tf_op jit(solution)/shard_map/ppermute | solution.py:42
  22.3 7.9 %collective-permute-start.4 = (bf16[4,11,16,128]{3,2,1,0:T(8,128)(2,1)S(1)}, bf16[4,11,16,128]{3,2,1,0:T(8,128)(2,1)S(1)}, u32[]{:S(2)}, u32[]{:S(2)}) collective-permute-start(bf16[4,11,16,128]{3,2,1,0:T(8,128)(2,1)S(1)} %get-tuple-element.30), channel_id=1, source_target_pairs={{1,4},{4,1},{5,8},{8,5},{9,12},{12,9},{3,6},{6,3},{7,10},{10,7},{1... | collective-permute-start | bytes 540680 | tf_op jit(solution)/shard_map/ppermute | solution.py:42

commit v2 on v0

v2 whole, which is shorter than its diff:
```python
import functools
import math

import jax
import jax.numpy as jnp
from jax import lax
from jax.experimental import pallas as pl
from jax.experimental.pallas import tpu as pltpu
from jax.sharding import PartitionSpec as P

STEPS = 2

BETA_ONE = 0.6
BETA_TWO = 0.9
LEARN_RATE = 0.4
EPSILON = 1e-08

ROWS = ("row", "cores")
STRIPS = 16
SIDE = 8
EDGE = 4
PLANES = 7
VMEM = pl.BlockSpec(memory_space=pltpu.VMEM)
HBM = pl.BlockSpec(memory_space=pltpu.HBM)
F32 = jnp.float32
BF16 = jnp.bfloat16


def row_place():
    cores = lax.axis_size("cores")
    return lax.axis_index("row") * cores + lax.axis_index("cores")


def pairs(count, parity):
    chosen = []
    for low in range(parity, count - 1, 2):
        chosen += [(low, low + 1), (low + 1, low)]
    return chosen


def swap(block, axes, parity):
    return lax.ppermute(block, axes, pairs(lax.axis_size(axes), parity))


def call(kernel, out_shape, in_specs, out_specs, scratch, cost, name, aliases=None):
    return pl.pallas_call(
        kernel,
        out_shape=out_shape,
        in_specs=in_specs,
        out_specs=out_specs,
        scratch_shapes=scratch,
        compiler_params=pltpu.CompilerParams(vmem_limit_bytes=24 << 20),
        cost_estimate=pl.CostEstimate(flops=cost[0], bytes_accessed=cost[1], transcendentals=0),
        input_output_aliases=aliases or {},
        name=name,
    )


def shape(dims, dtype):
    return jax.ShapeDtypeStruct(dims, dtype)


def pick_row(index, height):
    odd = lax.rem(row_place(), 2) == 1
    return jnp.where(odd, height - 1 - index, index)


def pick_partner_row(index, height):
    odd = lax.rem(row_place(), 2) == 1
    return jnp.where(odd, index, height - 1 - index)


def piece_counts(height):
    return height, height + 2, height * EDGE // SIDE


def pack_columns(sides, latent, first, second, target, mask, *rest):
    outs, rest = rest[:sides], rest[sides:]
    turned, ends, aim, known, planes, flat, sem = rest
    height, breadth = latent.shape[0], latent.shape[1]
    copies = []
    for number, source in enumerate((latent, first, second)):
        for end, start in enumerate((0, breadth - SIDE)):
            copy = pltpu.make_async_copy(
                source.at[:, pl.ds(start, SIDE)], ends.at[number, end], sem.at[number, end]
            )
            copy.start()
            copies.append(copy)
    early = [
        pltpu.make_async_copy(target, aim, sem.at[3, 0]),
        pltpu.make_async_copy(mask, known, sem.at[3, 1]),
    ]
    for copy in early:
        copy.start()
    planes[...] = jnp.zeros_like(planes)
    for copy in early:
        copy.wait()
    keep = known[...].astype(F32)
    for color in range(3):
        wanted = keep * aim[color]
        high = wanted.astype(BF16).astype(F32)
        planes[pl.ds(color, height, stride=PLANES), :] = high
        planes[pl.ds(color + 3, height, stride=PLANES), :] = wanted - high
    planes[pl.ds(6, height, stride=PLANES), :] = keep
    swapped = planes[...].T
    turned[...] = swapped.astype(BF16)
    for copy in copies:
        copy.wait()
    col_even = lax.rem(lax.axis_index("col"), 2) == 0
    _, at_low, step = piece_counts(height)
    for side, out in enumerate(outs):
        right = col_even if side == 0 else jnp.logical_not(col_even)
        flat[height] = jnp.where(right, swapped[breadth - SIDE :], swapped[:SIDE])
        flat[height + 1] = jnp.zeros(flat.shape[1:], F32)
        for row in range(height):
            source = pick_row(row, height)
            own = [jnp.where(right, ends[n, 1, source], ends[n, 0, source]) for n in range(3)]
            flat[row] = own[0]
            own[0] = own[0] - own[0].astype(BF16).astype(F32)
            for number, piece in enumerate(own):
                near = jnp.where(right, piece[SIDE - EDGE :], piece[:EDGE])
                at = EDGE * row
                flat[at_low + number * step + at // SIDE, at % SIDE : at % SIDE + EDGE] = near
        out[...] = flat[...].astype(BF16)


def pack_weights(one, two, rgb, bias_one, bias_two, *refs):
    ahead_one, ahead_two, back_one, back_two, colors, bias, held = refs
    size = one.shape[2]
    odd = lax.rem(row_place(), 2) == 1
    for kernel, ahead, back in ((one, ahead_one, back_one), (two, ahead_two, back_two)):
        for row in range(4):
            for col in range(3):
                at = (row * 3 + col) * size
                for out in range(2):
                    tap = row - out
                    if 0 <= tap <= 2:
                        front = kernel[jnp.where(odd, 2 - tap, tap), col]
                        rear = kernel[jnp.where(odd, tap, 2 - tap), 2 - col]
                        rear = rear.astype(F32).T.astype(BF16)
                    else:
                        front = rear = jnp.zeros((size, size), BF16)
                    ahead[at : at + size, out * size : (out + 1) * size] = front
                    back[at : at + size, out * size : (out + 1) * size] = rear
    held[...] = jnp.zeros_like(held)
    held[0:3] = rgb[...].astype(F32)
    held[3:6] = rgb[...].astype(F32)
    colors[...] = held[...].astype(BF16)
    bias[0] = jnp.broadcast_to(bias_one[...], bias.shape[1:])
    bias[1] = jnp.broadcast_to(bias_two[...], bias.shape[1:])


def put(dest, row, value, strip):
    dest[row, 1 : strip + 1] = value.astype(BF16).reshape(strip, STRIPS, -1)
    dest[row, 0] = pltpu.roll(value[(strip - 1) * STRIPS :], 1, 0).astype(BF16)
    dest[row, strip + 1] = pltpu.roll(value[:STRIPS], STRIPS - 1, 0).astype(BF16)


def widen(dest, source, strip):
    for row in range(EDGE):
        dest[row, 1 : strip + 1] = source[row]
        dest[row, 0] = pltpu.roll(source[row, strip - 1].astype(F32), 1, 0).astype(BF16)
        dest[row, strip + 1] = pltpu.roll(source[row, 0].astype(F32), STRIPS - 1, 0).astype(BF16)


def strips_of(source, row, strip):
    return jnp.concatenate(
        [source[row, pl.ds(j, STRIPS, stride=strip), :] for j in range(strip)], axis=0
    )


def fill_sides(sides, held, pieces, spread, rows):
    breadth = held.shape[1] - 2 * SIDE
    col_even = lax.rem(lax.axis_index("col"), 2) == 0
    for side in range(2):
        right = col_even if side == 0 else jnp.logical_not(col_even)
        spot = pl.ds(pl.multiple_of(jnp.where(right, SIDE + breadth, 0), SIDE), SIDE)
        for row in range(rows):
            if side < sides:
                held[row, spot] = spread(pieces[side], row, right)
            else:
                held[row, spot] = jnp.zeros((SIDE, held.shape[2]), F32)


def nearest(pieces, number, height, row, right):
    _, at_low, step = piece_counts(height)
    at = EDGE * row
    piece = pieces[at_low + number * step + at // SIDE].astype(F32)
    piece = piece[at % SIDE : at % SIDE + EDGE]
    blank = jnp.zeros((SIDE - EDGE, piece.shape[1]), F32)
    return jnp.where(
        right,
        jnp.concatenate([piece, blank], axis=0),
        jnp.concatenate([blank, piece], axis=0),
    )


def pack_rows(sides, latent, turned, *rest):
    pieces, rest = rest[:sides], rest[sides:]
    own, lines, near, far, spots, inside, held, turn = rest
    height, breadth, size = latent.shape
    strip = own.shape[1] - 2
    for row in range(height):
        held[row, SIDE : SIDE + breadth] = latent[pick_row(row, height)]
    fill_sides(
        sides,
        held,
        pieces,
        lambda piece, row, right: piece[row].astype(F32) + nearest(piece, 0, height, row, right),
        height,
    )
    turn[0, SIDE : SIDE + breadth] = turned[...].astype(F32)
    fill_sides(sides, turn, pieces, lambda piece, row, right: piece[height].astype(F32), 1)
    spot = strips_of(turn, 0, strip).astype(BF16).reshape(strip, STRIPS, size)
    spots[...] = spot
    near[EDGE] = spot
    far[EDGE] = spot
    for row in range(height):
        line = strips_of(held, row, strip)
        lines[row] = line
        put(own, row, line, strip)
        short = line.astype(BF16).reshape(strip, STRIPS, size)
        if row < EDGE:
            far[EDGE - 1 - row] = short
        if row >= height - EDGE:
            near[height - 1 - row] = short
    col = lax.axis_index("col")
    base = col * breadth - SIDE
    total = lax.axis_size("col") * breadth
    for j in range(strip):
        at = lax.broadcasted_iota(jnp.int32, (STRIPS, size), 0) * strip + (j + base)
        inside[j * STRIPS : (j + 1) * STRIPS] = ((at >= 0) & (at < total)).astype(F32)


def aim_rows(aims, known, spots):
    size = aims.shape[2]
    lane_in = lax.broadcasted_iota(jnp.int32, (size, 2 * size), 0)
    lane_out = lax.broadcasted_iota(jnp.int32, (size, 2 * size), 1)
    color = lax.rem(lane_out, 3)
    aimed = (lane_out < 6) & ((lane_in == color) | (lane_in == color + 3))
    masked = (lane_out >= size) & (lane_out < size + 6) & (lane_in == 6)
    chosen = (aimed | masked).astype(F32).astype(BF16)
    for row, (spot, source) in enumerate(spots):
        value = pltpu.roll(spot, lax.rem(size - PLANES * source, size), 1)
        both = jnp.dot(value.astype(BF16), chosen, preferred_element_type=F32)
        aims[row] = both[:, :size]
        known[row] = both[:, size:]


def conv_pair(rows, first, weights, strip):
    taps = []
    for down in range(4):
        source, at = rows[first + down]
        for across in range(3):
            taps.append(source[at, across : across + strip].reshape(strip * STRIPS, -1))
    return jnp.dot(jnp.concatenate(taps, axis=1), weights[...], preferred_element_type=F32)


def sigma_of(value):
    return 0.5 * jnp.tanh(0.5 * value) + 0.5


def gradient(firsts, rows, weights, aims, known, inside, emit):
    wide, hidden, slope, grad_two, grad_one = rows
    ahead_one, ahead_two, back_one, back_two, colors, bias = weights
    pixels, size = inside.shape
    strip = pixels // STRIPS
    place, count = row_place(), lax.axis_size("row") * lax.axis_size("cores")
    odd = lax.rem(place, 2) == 1
    there = jnp.where(odd, place < count - 1, place > 0).astype(F32)
    columns = inside[...]
    halves = lambda both: (both[:, :size], both[:, size:])

    for first in firsts[0]:
        for half, summed in enumerate(halves(conv_pair(wide, first - 1, ahead_one, strip))):
            row = first + half
            value = summed + bias[0, :1]
            sigma = sigma_of(value)
            hid = value * sigma
            keep = columns * there if row < EDGE else columns
            put(*hidden[row], hid * keep, strip)
            if row in slope:
                held, at = slope[row]
                held[at] = (sigma + hid * (1.0 - sigma)) * keep

    lane = lax.broadcasted_iota(jnp.int32, (2 * pixels, size), 1)
    for number, first in enumerate(firsts[1]):
        both = conv_pair(hidden, first - 1, ahead_two, strip)
        value = jnp.concatenate(halves(both), axis=0) + bias[1, :1]
        sigma = sigma_of(value)
        hid = value * sigma
        color = lax.dot_general(
            hid.astype(BF16), colors[...], (((1,), (1,)), ((), ())), preferred_element_type=F32
        )
        spot = slice(2 * number, 2 * number + 2)
        residual = known[spot].reshape(2 * pixels, -1) * color - aims[spot].reshape(2 * pixels, -1)
        rest = residual - residual.astype(BF16).astype(F32)
        split = jnp.where(lane < 3, residual, rest).astype(BF16)
        spread = jnp.dot(split, colors[...], preferred_element_type=F32)
        result = spread * (sigma + hid * (1.0 - sigma))
        for half in range(2):
            put(*grad_two[first + half], result[half * pixels : (half + 1) * pixels], strip)

    for first in firsts[2]:
        for half, summed in enumerate(halves(conv_pair(grad_two, first - 1, back_two, strip))):
            held, at = slope[first + half]
            put(*grad_one[first + half], summed * held[at], strip)

    for first in firsts[3]:
        for half, summed in enumerate(halves(conv_pair(grad_one, first - 1, back_one, strip))):
            emit(first + half - EDGE, summed)


def adam(current, first, second, grad):
    first = BETA_ONE * first + (1.0 - BETA_ONE) * grad
    second = BETA_TWO * second + (1.0 - BETA_TWO) * grad * grad
    return current - LEARN_RATE * first / (jnp.sqrt(second) + EPSILON), first, second


def place_rows(*parts):
    rows = {}
    for first, last, held, at in parts:
        for row in range(first, last):
            rows[row] = (held, at + row - first)
    return rows


def near_firsts(height):
    return [range(5 + n, height + 7 - n, 2) for n in range(4)]


def far_firsts():
    return [range(1 + n, 5 + n, 2) for n in range(4)]


def near_rows(height, own, halo, passed, scratch):
    hidden, slope, grad_two, grad_one = scratch
    hidden_out, slope_out, two_out, one_out = passed
    return (
        {**own, **place_rows((height + 4, height + 8, halo, 0))},
        place_rows((5, 7, hidden_out, 0), (7, height + 7, hidden, 0)),
        place_rows((5, 7, slope_out, 0), (7, height + 5, slope, 0)),
        place_rows((6, 8, two_out, 0), (8, height + 6, grad_two, 0)),
        place_rows((7, 9, one_out, 0), (9, height + 5, grad_one, 0)),
    )


def far_rows(own, halo, passed, scratch):
    hidden, slope, grad_two, grad_one = scratch
    hidden_in, slope_in, two_in, one_in = passed
    return (
        {**own, **place_rows((0, 4, halo, 0))},
        place_rows((1, 5, hidden, 0), (5, 7, hidden_in, 0)),
        place_rows((3, 5, slope, 0), (5, 7, slope_in, 0)),
        place_rows((2, 6, grad_two, 0), (6, 8, two_in, 0)),
        place_rows((3, 7, grad_one, 0), (7, 9, one_in, 0)),
    )


def flat_spot(spots):
    return spots[...].reshape(-1, spots.shape[-1]).astype(F32)


def first_near(sides, own, lines, moment_one, moment_two, near, spots, inside, *refs):
    pieces, refs = refs[:sides], refs[sides:]
    weights, refs = refs[:6], refs[6:]
    passed, refs = refs[:4], refs[4:]
    (new, near_out, z_out, m_out, v_out, m_rest, v_rest, aims, known), refs = refs[:9], refs[9:]
    halo, m_held, v_held, *scratch = refs
    height, breadth = moment_one.shape[:2]
    strip = own.shape[1] - 2
    widen(halo, near, strip)
    mine, theirs = flat_spot(spots), flat_spot(near.at[EDGE])
    aim_rows(
        aims,
        known,
        [(mine, pick_row(row, height)) for row in range(2, height)]
        + [(theirs, pick_partner_row(row, height)) for row in (height - 1, height - 2)],
    )
    for number, (held, moment) in enumerate(((m_held, moment_one), (v_held, moment_two))):
        for row in range(height):
            held[row, SIDE : SIDE + breadth] = moment[pick_row(row, height)]
        fill_sides(
            sides,
            held,
            pieces,
            lambda piece, row, right: nearest(piece, number + 1, height, row, right),
            height,
        )
    for row in range(EDGE):
        m_rest[row] = strips_of(m_held, row, strip)
        v_rest[row] = strips_of(v_held, row, strip)

    def emit(row, grad):
        current, first, second = adam(
            lines[row], strips_of(m_held, row, strip), strips_of(v_held, row, strip), grad
        )
        current = current * inside[...]
        at = row - EDGE
        z_out[at] = current
        m_out[at] = first
        v_out[at] = second
        put(new, at, current, strip)
        if row >= height - EDGE:
            near_out[height - 1 - row] = current.astype(BF16).reshape(near_out.shape[1:])

    rows = near_rows(height, place_rows((4, height + 4, own, 0)), halo, passed, scratch)
    gradient(near_firsts(height), rows, weights, aims, known, inside, emit)


def first_far(own, lines, m_rest, v_rest, far, spots, inside, *refs):
    passed, refs = refs[:4], refs[4:]
    weights, refs = refs[:6], refs[6:]
    (new, far_out, z_out, m_out, v_out, aims, known), refs = refs[:7], refs[7:]
    halo, *scratch = refs
    height = own.shape[0]
    strip = own.shape[1] - 2
    widen(halo, far, strip)
    mine, theirs = flat_spot(spots), flat_spot(far.at[EDGE])
    aim_rows(
        aims,
        known,
        [(theirs, pick_partner_row(row, height)) for row in (1, 0)]
        + [(mine, pick_row(row, height)) for row in range(2)],
    )

    def emit(row, grad):
        current, first, second = adam(lines[row], m_rest[row], v_rest[row], grad)
        current = current * inside[...]
        z_out[row] = current
        m_out[row] = first
        v_out[row] = second
        put(new, row, current, strip)
        far_out[EDGE - 1 - row] = current.astype(BF16).reshape(far_out.shape[1:])

    rows = far_rows(place_rows((4, 8, own, 0)), halo, passed, scratch)
    gradient(far_firsts(), rows, weights, aims, known, inside, emit)


def send_rows(outs, helds, sem, height, strip):
    copies = []
    breadth = outs[0].shape[1]

    def send(row, at, values):
        for number, (held, out, value) in enumerate(zip(helds, outs, values)):
            for j in range(strip):
                held[at, pl.ds(j, STRIPS, stride=strip), :] = value[j * STRIPS : (j + 1) * STRIPS]
            copy = pltpu.make_async_copy(
                held.at[at, pl.ds(SIDE, breadth)],
                out.at[pick_row(row, height)],
                sem.at[number, at],
            )
            copy.start()
            copies.append(copy)

    return send, copies


def last_near(low, high, near, z_in, m_in, v_in, aims, known, inside, *refs):
    weights, refs = refs[:6], refs[6:]
    passed, refs = refs[:4], refs[4:]
    outs, refs = refs[:3], refs[3:]
    helds, refs = refs[:3], refs[3:]
    halo, *scratch, sem = refs
    height = EDGE + high.shape[0]
    strip = low.shape[1] - 2
    widen(halo, near, strip)
    send, copies = send_rows(outs, helds, sem, height, strip)

    def emit(row, grad):
        at = row - EDGE
        send(row, at, adam(z_in[at], m_in[at], v_in[at], grad))

    own = place_rows((4, 8, low, 0), (8, height + 4, high, 0))
    rows = near_rows(height, own, halo, passed, scratch)
    gradient(near_firsts(height), rows, weights, aims, known, inside, emit)
    for copy in copies:
        copy.wait()


def last_far(low, far, z_in, m_in, v_in, aims, known, inside, *refs):
    passed, refs = refs[:4], refs[4:]
    weights, refs = refs[:6], refs[6:]
    outs, refs = refs[3:6], refs[6:]
    helds, refs = refs[:3], refs[3:]
    halo, *scratch, sem = refs
    height = outs[0].shape[0]
    strip = low.shape[1] - 2
    widen(halo, far, strip)
    send, copies = send_rows(outs, helds, sem, height, strip)

    def emit(row, grad):
        send(row, row, adam(z_in[row], m_in[row], v_in[row], grad))

    rows = far_rows(place_rows((4, 8, low, 0)), halo, passed, scratch)
    gradient(far_firsts(), rows, weights, aims, known, inside, emit)
    for copy in copies:
        copy.wait()


def body(
    latent,
    moment_one,
    moment_two,
    hole_mask,
    target_rgb,
    kernel_one,
    bias_one,
    kernel_two,
    bias_two,
    rgb_weight,
):
    height, breadth, size = latent.shape
    strip = (breadth + 2 * SIDE) // STRIPS
    assert strip * STRIPS == breadth + 2 * SIDE and height % 2 == 0 and height >= 8
    assert height * PLANES <= size and breadth == size and lax.axis_size("cores") == 2
    pixels = strip * STRIPS
    sides = 1 if lax.axis_size("col") == 2 else 2
    dma = pltpu.SemaphoreType.DMA
    _, at_low, step = piece_counts(height)
    block = (at_low + 3 * step, SIDE, size)
    tall = lambda rows: shape((rows, strip + 2, STRIPS, size), BF16)
    short = lambda rows: shape((rows, strip, STRIPS, size), BF16)
    lines_of = lambda rows: shape((rows, pixels, size), F32)
    vmem = lambda like: pltpu.VMEM(like.shape, like.dtype)
    work = 2 * 12 * 2 * pixels * size * size

    *columns, turned = call(
        functools.partial(pack_columns, sides),
        [shape(block, BF16)] * sides + [shape((breadth, size), BF16)],
        [HBM] * 5,
        [VMEM] * (sides + 1),
        [
            pltpu.VMEM((3, 2, height, SIDE, size), F32),
            pltpu.VMEM(target_rgb.shape, F32),
            pltpu.VMEM(hole_mask.shape, jnp.int32),
            pltpu.VMEM((size, breadth), F32),
            pltpu.VMEM(block, F32),
            dma((4, 2)),
        ],
        (10**6, 10**6),
        "pack_columns",
    )(latent, moment_one, moment_two, target_rgb, hole_mask)
    columns = [swap(piece, "col", side) for side, piece in enumerate(columns)]

    matrix = shape((12 * size, 2 * size), BF16)
    weights = call(
        pack_weights,
        [matrix] * 4 + [shape((size, size), BF16), shape((2, 8, size), F32)],
        [VMEM] * 5,
        [VMEM] * 6,
        [pltpu.VMEM((size, size), F32)],
        (10**6, 4 * 10**6),
        "pack_weights",
    )(kernel_one, kernel_two, rgb_weight, bias_one[None], bias_two[None])

    own, lines, near, far, spots, inside = call(
        functools.partial(pack_rows, sides),
        [tall(height), lines_of(height), short(EDGE + 1), short(EDGE + 1)]
        + [shape((strip, STRIPS, size), BF16), shape((pixels, size), F32)],
        [VMEM] * (2 + sides),
        [VMEM] * 6,
        [vmem(lines_of(height)), vmem(lines_of(1))],
        (10**6, 4 * 10**6),
        "pack_rows",
    )(latent, turned, *columns)
    near = swap(near, ROWS, 0)
    far = swap(far, ROWS, 1)

    passed = [tall(2), lines_of(2), tall(2), tall(2)]
    near_scratch = [
        vmem(tall(height)),
        vmem(lines_of(height - 2)),
        vmem(tall(height - 2)),
        vmem(tall(height - 4)),
    ]
    far_scratch = [vmem(tall(4)), vmem(lines_of(2)), vmem(tall(4)), vmem(tall(4))]
    near_work = (2 * (height - 1) + 0) * work, 10**7
    far_work = 8 * work, 10**7
    rest, some = height - EDGE, EDGE

    *results, near_next, z_high, m_high, v_high, m_rest, v_rest, aims_near, known_near = call(
        functools.partial(first_near, sides),
        passed
        + [tall(rest), short(EDGE), lines_of(rest), lines_of(rest), lines_of(rest)]
        + [lines_of(some), lines_of(some), lines_of(height), lines_of(height)],
        [VMEM] * (7 + sides + 6),
        [VMEM] * 13,
        [vmem(tall(EDGE)), vmem(lines_of(height)), vmem(lines_of(height))] + near_scratch,
        near_work,
        "first_near",
    )(own, lines, moment_one, moment_two, near, spots, inside, *columns, *weights)
    *handed, high = results
    near_next = swap(near_next, ROWS, 0)

    low, far_next, z_low, m_low, v_low, aims_far, known_far = call(
        first_far,
        [tall(some), short(EDGE), lines_of(some), lines_of(some), lines_of(some)]
        + [lines_of(4), lines_of(4)],
        [VMEM] * (7 + 4 + 6),
        [VMEM] * 7,
        [vmem(tall(EDGE))] + far_scratch,
        far_work,
        "first_far",
    )(own, lines, m_rest, v_rest, far, spots, inside, *handed, *weights)
    far_next = swap(far_next, ROWS, 1)

    out = shape(latent.shape, F32)
    results = call(
        last_near,
        passed + [out] * 3,
        [VMEM] * (9 + 6),
        [VMEM] * 4 + [HBM] * 3,
        [vmem(lines_of(rest))] * 3 + [vmem(tall(EDGE))] + near_scratch + [dma((3, rest))],
        near_work,
        "last_near",
    )(low, high, near_next, z_high, m_high, v_high, aims_near, known_near, inside, *weights)
    handed, outs = results[:4], results[4:]
    return call(
        last_far,
        [out] * 3,
        [VMEM] * (8 + 4 + 6) + [HBM] * 3,
        [HBM] * 3,
        [vmem(lines_of(some))] * 3 + [vmem(tall(EDGE))] + far_scratch + [dma((3, some))],
        far_work,
        "last_far",
        {18: 0, 19: 1, 20: 2},
    )(low, far_next, z_low, m_low, v_low, aims_far, known_far, inside, *handed, *weights, *outs)


def solution(mesh):
    tile = P(("parts", "row", "cores"), "col", None)
    return jax.shard_map(
        body,
        mesh=mesh,
        in_specs=(
            tile,
            tile,
            tile,
            P(("parts", "row", "cores"), "col"),
            P(None, ("parts", "row", "cores"), "col"),
            P(),
            P(),
            P(),
            P(),
            P(),
        ),
        out_specs=(tile, tile, tile),
        check_vma=False,
    )
```

time: 148 us -> 32.7 us (0.22)
  the two profiles are of different devices: /device:TPU:26 before, /device:TPU:1 now
where the time goes in v2:
time: 32.7 us; the launch traced here: 32.3 us
  Pallas kernels  14.6 us (45%)
  starting transfers between devices  11 us (34%)
  local copies, waits for them, and re-layouts  4.54 us (14%)
  waiting for transfers between devices  1.45 us (4%)
  between operations  0.78 us (2%)
    ppermute x5, starting transfers between devices, swap(): return lax.ppermute(block, axes, pairs(lax.axis_size(axes), parity))  11 us
    unnamed x24, local copies, waits for them, and re-layouts  4.54 us
    pallas_call x1, Pallas kernels, body(): call(last_near, passed + [out] * 3, [VMEM] * (9 + 6), [VMEM] * 4 + [HBM]...  4.23 us
    pallas_call x1, Pallas kernels, body(): call(functools.partial(first_near, sides), passed + [tall(rest), short(ED...  3.57 us
    pallas_call x1, Pallas kernels, body(): call(last_far, [out] * 3, [VMEM] * (8 + 4 + 6) + [HBM] * 3, [HBM] * 3, [v...  3.25 us
    pallas_call x1, Pallas kernels, body(): call(first_far, [tall(some), short(EDGE), lines_of(some), lines_of(some),...  2.47 us
    ppermute x5, waiting for transfers between devices, swap(): return lax.ppermute(block, axes, pairs(lax.axis_size(axes), parity))  1.45 us
  transfers between devices with their start and end apart: 5, of which 1 were waited for; matrix products, arithmetic and copies ran while one was open for 0% of the time, Pallas kernels for 34%

profile of v2, /device:TPU:1, one launch (start us, length us, event | category | flops | bytes accessed | tf_op | source)
XLA Modules:
  0.0 32.3 jit_solution(12796354381915769800)
XLA Ops:
  0.6 0.0 copy-start
  0.6 1.0 %copy-done = f32[8,128,128]{2,1,0:T(8,128)S(1)} copy-done((f32[8,128,128]{2,1,0:T(8,128)S(1)}, f32[8,128,128]{2,1,0:T(8,128)}, u32[]{:S(2)}) %copy-start) | copy-done | bytes 524312
  1.7 0.0 copy-start.1
  1.7 1.0 %copy-done.1 = f32[8,128,128]{2,1,0:T(8,128)S(1)} copy-done((f32[8,128,128]{2,1,0:T(8,128)S(1)}, f32[8,128,128]{2,1,0:T(8,128)}, u32[]{:S(2)}) %copy-start.1) | copy-done | bytes 524312
  2.7 0.0 copy-start.3
  2.7 1.0 %copy-done.3 = f32[8,128,128]{2,1,0:T(8,128)S(1)} copy-done((f32[8,128,128]{2,1,0:T(8,128)S(1)}, f32[8,128,128]{2,1,0:T(8,128)}, u32[]{:S(2)}) %copy-start.3) | copy-done | bytes 524312
  3.8 0.0 copy-start.7
  3.8 0.7 %copy-done.7 = f32[3,8,128]{2,1,0:T(8,128)S(1)} copy-done((f32[3,8,128]{2,1,0:T(8,128)S(1)}, f32[3,8,128]{2,1,0:T(8,128)}, u32[]{:S(2)}) %copy-start.7) | copy-done | bytes 12312
  4.5 0.0 copy-start.8
  4.5 0.7 %copy-done.8 = s32[8,128]{1,0:T(8,128)S(1)} copy-done((s32[8,128]{1,0:T(8,128)S(1)}, s32[8,128]{1,0:T(8,128)}, u32[]{:S(2)}) %copy-start.8) | copy-done | bytes 4120
  5.2 0.0 copy-start.5
  5.2 0.0 copy-start.6
  5.2 0.0 copy-start.9
  5.2 0.0 copy-start.10
  5.2 0.0 copy-start.11
  5.2 0.3 pack_columns.1
  5.5 2.1 %collective-permute-start = (bf16[22,8,128]{2,1,0:T(8,128)(2,1)S(1)}, bf16[22,8,128]{2,1,0:T(8,128)(2,1)S(1)}, u32[]{:S(2)}, u32[]{:S(2)}) collective-permute-start(bf16[22,8,128]{2,1,0:T(8,128)(2,1)S(1)} %get-tuple-element.45), channel_id=1, source_target_pairs={{0,2},{2,0},{1,3},{3,1},{4,6},{6,4},{5,7},{7,5},{8,10},{10,8},{9,1... | collective-permute-start | bytes 135176 | tf_op jit(solution)/shard_map/ppermute | solution.py:42
  7.6 1.4 %collective-permute-done.rest_0_.refs_0_ = bf16[22,8,128]{2,1,0:T(8,128)(2,1)S(1)} collective-permute-done((bf16[22,8,128]{2,1,0:T(8,128)(2,1)S(1)}, bf16[22,8,128]{2,1,0:T(8,128)(2,1)S(1)}, u32[]{:S(2)}, u32[]{:S(2)}) %collective-permute-start) | collective-permute-done | bytes 45088 | tf_op jit(solution)/shard_map/ppermute | solution.py:42
  9.0 0.0 copy-start.2
  9.0 0.0 copy-start.4
  9.0 0.1 pack_rows.1
  9.2 1.6 %collective-permute-start.1 = (bf16[5,9,16,128]{3,2,1,0:T(8,128)(2,1)S(1)}, bf16[5,9,16,128]{3,2,1,0:T(8,128)(2,1)S(1)}, u32[]{:S(2)}, u32[]{:S(2)}) collective-permute-start(bf16[5,9,16,128]{3,2,1,0:T(8,128)(2,1)S(1)} %get-tuple-element.48), channel_id=1, source_target_pairs={{0,1},{1,0},{4,5},{5,4},{8,9},{9,8},{12,13},{13,12},{2,3},{3,2},{6... | collective-permute-start | bytes 552968 | tf_op jit(solution)/shard_map/ppermute | solution.py:42
  10.8 0.0 copy-done.5
  10.8 0.0 copy-done.6
  10.8 0.0 copy-done.9
  10.8 0.0 copy-done.10
  10.8 0.0 copy-done.11
  10.8 0.6 %pack_weights.1 = (bf16[1536,256]{1,0:T(8,128)(2,1)S(1)}, bf16[1536,256]{1,0:T(8,128)(2,1)S(1)}, bf16[1536,256]{1,0:T(8,128)(2,1)S(1)}, bf16[1536,256]{1,0:T(8,1...) custom-call(bf16[3,3,128,128]{3,2,1,0:T(8,128)(2,1)S(1)} %copy-done.5, ...), custom_call_target="tpu_custom_call" | custom-call | flops 1000000 | bytes 4000000 | tf_op jit(solution)/shard_map/pack_weights/pallas_call | solution.py:547
  11.4 3.7 %collective-permute-start.2 = (bf16[5,9,16,128]{3,2,1,0:T(8,128)(2,1)S(1)}, bf16[5,9,16,128]{3,2,1,0:T(8,128)(2,1)S(1)}, u32[]{:S(2)}, u32[]{:S(2)}) collective-permute-start(bf16[5,9,16,128]{3,2,1,0:T(8,128)(2,1)S(1)} %get-tuple-element.59), channel_id=1, source_target_pairs={{1,4},{4,1},{5,8},{8,5},{9,12},{12,9},{3,6},{6,3},{7,10},{10,7},{1... | collective-permute-start | bytes 552968 | tf_op jit(solution)/shard_map/ppermute | solution.py:42
  15.1 0.0 collective-permute-done.1.near
  15.1 0.0 copy-done.2
  15.1 0.0 copy-done.4
  15.1 3.6 %first_near.1 = (bf16[2,11,16,128]{3,2,1,0:T(8,128)(2,1)S(1)}, f32[2,144,128]{2,1,0:T(8,128)S(1)}, bf16[2,11,16,128]{3,2,1,0:T(8,128)(2,1)S(1)}, bf16[2,11,16,12...) custom-call(bf16[8,11,16,128]{3,2,1,0:T(8,128)(2,1)S(1)} %get-tuple-, ...), custom_call_target="tpu_custom_call" | custom-call | flops 1585446912 | bytes 10000000 | tf_op jit(solution)/shard_map/first_near/pallas_call | solution.py:582
  18.7 0.1 collective-permute-start.4
  18.8 0.0 collective-permute-done.2.far
  18.8 2.5 %first_far.1 = (bf16[4,11,16,128]{3,2,1,0:T(8,128)(2,1)S(1)}, bf16[4,9,16,128]{3,2,1,0:T(8,128)(2,1)S(1)}, f32[4,144,128]{2,1,0:T(8,128)S(1)}, f32[4,144,128]{2,...) custom-call(bf16[8,11,16,128]{3,2,1,0:T(8,128)(2,1)S(1)} %get-tuple-element.46., ...), custom_call_target="tpu_custom_call" | custom-call | flops 905969664 | bytes 10000000 | tf_op jit(solution)/shard_map/first_far/pallas_call | solution.py:596
  21.3 3.6 %collective-permute-start.3 = (bf16[4,9,16,128]{3,2,1,0:T(8,128)(2,1)S(1)}, bf16[4,9,16,128]{3,2,1,0:T(8,128)(2,1)S(1)}, u32[]{:S(2)}, u32[]{:S(2)}) collective-permute-start(bf16[4,9,16,128]{3,2,1,0:T(8,128)(2,1)S(1)} %get-tuple-element.65), channel_id=1, source_target_pairs={{1,4},{4,1},{5,8},{8,5},{9,12},{12,9},{3,6},{6,3},{7,10},{10,7},{1... | collective-permute-start | bytes 442376 | tf_op jit(solution)/shard_map/ppermute | solution.py:42
  24.8 0.0 collective-permute-done.4.near
  24.9 4.2 %last_near.1 = (bf16[2,11,16,128]{3,2,1,0:T(8,128)(2,1)S(1)}, f32[2,144,128]{2,1,0:T(8,128)S(1)}, bf16[2,11,16,128]{3,2,1,0:T(8,128)(2,1)S(1)}, bf16[2,11,16,128...) custom-call(bf16[4,11,16,128]{3,2,1,0:T(8,128)(2,1)S(1)} %get-tuple-element.64.l, ...), custom_call_target="tpu_custom_call" | custom-call | flops 1585446912 | bytes 10000000 | tf_op jit(solution)/shard_map/last_near/pallas_call | solution.py:609
  29.1 0.0 collective-permute-done.3.far
  29.1 3.2 %last_far.1 = (f32[8,128,128]{2,1,0:T(8,128)}, f32[8,128,128]{2,1,0:T(8,128)}, f32[8,128,128]{2,1,0:T(8,128)}) custom-call(bf16[4,11,16,128]{3,2,1,0:T(8,128)(2,1)S(1)} %get-tuple-element.64.low, bf16[4,9,16,128]{3,2,1,0:T(8,128)(2,1)S(1)} %collective-permute-done.3.far, ...), custom_call_target="tpu_custom_call", output_to_operand_aliasing={{0}: (18, {}), {1}: (19, {}), {2}: (20, {})} | custom-call | flops 905969664 | bytes 10000000 | tf_op jit(solution)/shard_map/last_far/pallas_call | solution.py:619
Async XLA Ops:
  0.6 1.0 %copy-start = (f32[8,128,128]{2,1,0:T(8,128)S(1)}, f32[8,128,128]{2,1,0:T(8,128)}, u32[]{:S(2)}) copy-start(f32[8,128,128]{2,1,0:T(8,128)} %latent.3) | copy-start | bytes 1572868
  1.7 1.0 %copy-start.1 = (f32[8,128,128]{2,1,0:T(8,128)S(1)}, f32[8,128,128]{2,1,0:T(8,128)}, u32[]{:S(2)}) copy-start(f32[8,128,128]{2,1,0:T(8,128)} %moment_one.1) | copy-start | bytes 1572868
  2.7 1.0 %copy-start.3 = (f32[8,128,128]{2,1,0:T(8,128)S(1)}, f32[8,128,128]{2,1,0:T(8,128)}, u32[]{:S(2)}) copy-start(f32[8,128,128]{2,1,0:T(8,128)} %moment_two.1) | copy-start | bytes 1572868
  3.8 0.7 %copy-start.7 = (f32[3,8,128]{2,1,0:T(8,128)S(1)}, f32[3,8,128]{2,1,0:T(8,128)}, u32[]{:S(2)}) copy-start(f32[3,8,128]{2,1,0:T(8,128)} %target.1) | copy-start | bytes 36868
  4.5 0.7 %copy-start.8 = (s32[8,128]{1,0:T(8,128)S(1)}, s32[8,128]{1,0:T(8,128)}, u32[]{:S(2)}) copy-start(s32[8,128]{1,0:T(8,128)} %mask.1) | copy-start | bytes 12292
  5.2 5.6 %copy-start.5 = (bf16[3,3,128,128]{3,2,1,0:T(8,128)(2,1)S(1)}, bf16[3,3,128,128]{3,2,1,0:T(8,128)(2,1)}, u32[]{:S(2)}) copy-start(bf16[3,3,128,128]{3,2,1,0:T(8,128)(2,1)} %one.1) | copy-start | bytes 884740
  5.2 5.6 %copy-start.6 = (bf16[3,3,128,128]{3,2,1,0:T(8,128)(2,1)S(1)}, bf16[3,3,128,128]{3,2,1,0:T(8,128)(2,1)}, u32[]{:S(2)}) copy-start(bf16[3,3,128,128]{3,2,1,0:T(8,128)(2,1)} %two.1) | copy-start | bytes 884740
  5.2 5.6 %copy-start.9 = (bf16[3,128]{1,0:T(4,128)(2,1)S(1)}, bf16[3,128]{1,0:T(4,128)(2,1)}, u32[]{:S(2)}) copy-start(bf16[3,128]{1,0:T(4,128)(2,1)} %rgb.1) | copy-start | bytes 2308
  5.2 5.6 %copy-start.10 = (f32[128]{0:T(128)S(1)}, f32[128]{0:T(128)}, u32[]{:S(2)}) copy-start(f32[128]{0:T(128)} %param.16) | copy-start | bytes 1540
  5.2 5.6 %copy-start.11 = (f32[128]{0:T(128)S(1)}, f32[128]{0:T(128)}, u32[]{:S(2)}) copy-start(f32[128]{0:T(128)} %param.18) | copy-start | bytes 1540
  5.5 3.5 %collective-permute-start = (bf16[22,8,128]{2,1,0:T(8,128)(2,1)S(1)}, bf16[22,8,128]{2,1,0:T(8,128)(2,1)S(1)}, u32[]{:S(2)}, u32[]{:S(2)}) collective-permute-start(bf16[22,8,128]{2,1,0:T(8,128)(2,1)S(1)} %get-tuple-element.45), channel_id=1, source_target_pairs={{0,2},{2,0},{1,3},{3,1},{4,6},{6,4},{5,7},{7,5},{8,10},{10,8},{9,1... | collective-permute-start | bytes 135176 | tf_op jit(solution)/shard_map/ppermute | solution.py:42
  9.0 6.1 %copy-start.2 = (f32[8,128,128]{2,1,0:T(8,128)S(1)}, f32[8,128,128]{2,1,0:T(8,128)}, u32[]{:S(2)}) copy-start(f32[8,128,128]{2,1,0:T(8,128)} %moment_one.1) | copy-start | bytes 1572868
  9.0 6.1 %copy-start.4 = (f32[8,128,128]{2,1,0:T(8,128)S(1)}, f32[8,128,128]{2,1,0:T(8,128)}, u32[]{:S(2)}) copy-start(f32[8,128,128]{2,1,0:T(8,128)} %moment_two.1) | copy-start | bytes 1572868
  9.2 5.9 %collective-permute-start.1 = (bf16[5,9,16,128]{3,2,1,0:T(8,128)(2,1)S(1)}, bf16[5,9,16,128]{3,2,1,0:T(8,128)(2,1)S(1)}, u32[]{:S(2)}, u32[]{:S(2)}) collective-permute-start(bf16[5,9,16,128]{3,2,1,0:T(8,128)(2,1)S(1)} %get-tuple-element.48), channel_id=1, source_target_pairs={{0,1},{1,0},{4,5},{5,4},{8,9},{9,8},{12,13},{13,12},{2,3},{3,2},{6... | collective-permute-start | bytes 552968 | tf_op jit(solution)/shard_map/ppermute | solution.py:42
  11.4 7.4 %collective-permute-start.2 = (bf16[5,9,16,128]{3,2,1,0:T(8,128)(2,1)S(1)}, bf16[5,9,16,128]{3,2,1,0:T(8,128)(2,1)S(1)}, u32[]{:S(2)}, u32[]{:S(2)}) collective-permute-start(bf16[5,9,16,128]{3,2,1,0:T(8,128)(2,1)S(1)} %get-tuple-element.59), channel_id=1, source_target_pairs={{1,4},{4,1},{5,8},{8,5},{9,12},{12,9},{3,6},{6,3},{7,10},{10,7},{1... | collective-permute-start | bytes 552968 | tf_op jit(solution)/shard_map/ppermute | solution.py:42
  18.7 6.2 %collective-permute-start.4 = (bf16[4,9,16,128]{3,2,1,0:T(8,128)(2,1)S(1)}, bf16[4,9,16,128]{3,2,1,0:T(8,128)(2,1)S(1)}, u32[]{:S(2)}, u32[]{:S(2)}) collective-permute-start(bf16[4,9,16,128]{3,2,1,0:T(8,128)(2,1)S(1)} %get-tuple-element.72), channel_id=1, source_target_pairs={{0,1},{1,0},{4,5},{5,4},{8,9},{9,8},{12,13},{13,12},{2,3},{3,2},{6... | collective-permute-start | bytes 442376 | tf_op jit(solution)/shard_map/ppermute | solution.py:42
  21.3 7.8 %collective-permute-start.3 = (bf16[4,9,16,128]{3,2,1,0:T(8,128)(2,1)S(1)}, bf16[4,9,16,128]{3,2,1,0:T(8,128)(2,1)S(1)}, u32[]{:S(2)}, u32[]{:S(2)}) collective-permute-start(bf16[4,9,16,128]{3,2,1,0:T(8,128)(2,1)S(1)} %get-tuple-element.65), channel_id=1, source_target_pairs={{1,4},{4,1},{5,8},{8,5},{9,12},{12,9},{3,6},{6,3},{7,10},{10,7},{1... | collective-permute-start | bytes 442376 | tf_op jit(solution)/shard_map/ppermute | solution.py:42

commit v3 on v2

--- a/solution.py
+++ b/solution.py
@@ -42,20 +42,24 @@
     return lax.ppermute(block, axes, pairs(lax.axis_size(axes), parity))
 
 
-def call(kernel, out_shape, in_specs, out_specs, scratch, cost, name, aliases=None):
+def call(kernel, out_shape, in_specs, out_specs, scratch, cost, name, aliases=None, limit=24 << 20):
     return pl.pallas_call(
         kernel,
         out_shape=out_shape,
         in_specs=in_specs,
         out_specs=out_specs,
         scratch_shapes=scratch,
-        compiler_params=pltpu.CompilerParams(vmem_limit_bytes=24 << 20),
+        compiler_params=pltpu.CompilerParams(vmem_limit_bytes=limit),
         cost_estimate=pl.CostEstimate(flops=cost[0], bytes_accessed=cost[1], transcendentals=0),
         input_output_aliases=aliases or {},
         name=name,
     )
 
 
+def in_hbm(array):
+    return pltpu.with_memory_space_constraint(array, pltpu.HBM)
+
+
 def shape(dims, dtype):
     return jax.ShapeDtypeStruct(dims, dtype)
 
@@ -76,21 +80,17 @@
 
 def pack_columns(sides, latent, first, second, target, mask, *rest):
     outs, rest = rest[:sides], rest[sides:]
-    turned, ends, aim, known, planes, flat, sem = rest
+    turned, *inner, aim, known, planes, flat, sem = rest
     height, breadth = latent.shape[0], latent.shape[1]
-    copies = []
-    for number, source in enumerate((latent, first, second)):
-        for end, start in enumerate((0, breadth - SIDE)):
-            copy = pltpu.make_async_copy(
-                source.at[:, pl.ds(start, SIDE)], ends.at[number, end], sem.at[number, end]
-            )
-            copy.start()
-            copies.append(copy)
     early = [
-        pltpu.make_async_copy(target, aim, sem.at[3, 0]),
-        pltpu.make_async_copy(mask, known, sem.at[3, 1]),
+        pltpu.make_async_copy(target, aim, sem.at[3]),
+        pltpu.make_async_copy(mask, known, sem.at[4]),
     ]
-    for copy in early:
+    copies = [
+        pltpu.make_async_copy(source, dest, sem.at[number])
+        for number, (source, dest) in enumerate(zip((latent, first, second), inner))
+    ]
+    for copy in early + copies:
         copy.start()
     planes[...] = jnp.zeros_like(planes)
     for copy in early:
@@ -114,7 +114,10 @@
         flat[height + 1] = jnp.zeros(flat.shape[1:], F32)
         for row in range(height):
             source = pick_row(row, height)
-            own = [jnp.where(right, ends[n, 1, source], ends[n, 0, source]) for n in range(3)]
+            own = [
+                jnp.where(right, block[source, breadth - SIDE :], block[source, :SIDE])
+                for block in inner
+            ]
             flat[row] = own[0]
             own[0] = own[0] - own[0].astype(BF16).astype(F32)
             for number, piece in enumerate(own):
@@ -437,60 +440,57 @@
     gradient(far_firsts(), rows, weights, aims, known, inside, emit)
 
 
-def send_rows(outs, helds, sem, height, strip):
-    copies = []
-    breadth = outs[0].shape[1]
-
-    def send(row, at, values):
-        for number, (held, out, value) in enumerate(zip(helds, outs, values)):
-            for j in range(strip):
-                held[at, pl.ds(j, STRIPS, stride=strip), :] = value[j * STRIPS : (j + 1) * STRIPS]
-            copy = pltpu.make_async_copy(
-                held.at[at, pl.ds(SIDE, breadth)],
-                out.at[pick_row(row, height)],
-                sem.at[number, at],
-            )
-            copy.start()
-            copies.append(copy)
-
-    return send, copies
+def keep_row(held, at, value, strip):
+    for j in range(strip):
+        held[at, pl.ds(j, STRIPS, stride=strip), :] = value[j * STRIPS : (j + 1) * STRIPS]
 
 
 def last_near(low, high, near, z_in, m_in, v_in, aims, known, inside, *refs):
     weights, refs = refs[:6], refs[6:]
     passed, refs = refs[:4], refs[4:]
-    outs, refs = refs[:3], refs[3:]
     helds, refs = refs[:3], refs[3:]
-    halo, *scratch, sem = refs
+    halo, *scratch = refs
     height = EDGE + high.shape[0]
     strip = low.shape[1] - 2
     widen(halo, near, strip)
-    send, copies = send_rows(outs, helds, sem, height, strip)
 
     def emit(row, grad):
         at = row - EDGE
-        send(row, at, adam(z_in[at], m_in[at], v_in[at], grad))
+        for held, value in zip(helds, adam(z_in[at], m_in[at], v_in[at], grad)):
+            keep_row(held, at, value, strip)
 
     own = place_rows((4, 8, low, 0), (8, height + 4, high, 0))
     rows = near_rows(height, own, halo, passed, scratch)
     gradient(near_firsts(height), rows, weights, aims, known, inside, emit)
-    for copy in copies:
-        copy.wait()
 
 
 def last_far(low, far, z_in, m_in, v_in, aims, known, inside, *refs):
     passed, refs = refs[:4], refs[4:]
     weights, refs = refs[:6], refs[6:]
-    outs, refs = refs[3:6], refs[6:]
-    helds, refs = refs[:3], refs[3:]
+    ready, outs, helds, refs = refs[:3], refs[3:6], refs[6:9], refs[9:]
     halo, *scratch, sem = refs
-    height = outs[0].shape[0]
+    height, breadth = outs[0].shape[:2]
     strip = low.shape[1] - 2
+    copies = []
+
+    def send(row, number, held, at):
+        copy = pltpu.make_async_copy(
+            held.at[at, pl.ds(SIDE, breadth)],
+            outs[number].at[pick_row(row, height)],
+            sem.at[number, row],
+        )
+        copy.start()
+        copies.append(copy)
+
+    for row in range(EDGE, height):
+        for number in range(3):
+            send(row, number, ready[number], row - EDGE)
     widen(halo, far, strip)
-    send, copies = send_rows(outs, helds, sem, height, strip)
 
     def emit(row, grad):
-        send(row, row, adam(z_in[row], m_in[row], v_in[row], grad))
+        for number, value in enumerate(adam(z_in[row], m_in[row], v_in[row], grad)):
+            keep_row(helds[number], row, value, strip)
+            send(row, number, helds[number], row)
 
     rows = far_rows(place_rows((4, 8, low, 0)), halo, passed, scratch)
     gradient(far_firsts(), rows, weights, aims, known, inside, emit)
@@ -525,22 +525,23 @@
     vmem = lambda like: pltpu.VMEM(like.shape, like.dtype)
     work = 2 * 12 * 2 * pixels * size * size
 
-    *columns, turned = call(
+    *columns, turned, latent, moment_one, moment_two = call(
         functools.partial(pack_columns, sides),
-        [shape(block, BF16)] * sides + [shape((breadth, size), BF16)],
+        [shape(block, BF16)] * sides
+        + [shape((breadth, size), BF16)]
+        + [shape(latent.shape, F32)] * 3,
         [HBM] * 5,
-        [VMEM] * (sides + 1),
+        [VMEM] * (sides + 4),
         [
-            pltpu.VMEM((3, 2, height, SIDE, size), F32),
             pltpu.VMEM(target_rgb.shape, F32),
             pltpu.VMEM(hole_mask.shape, jnp.int32),
             pltpu.VMEM((size, breadth), F32),
             pltpu.VMEM(block, F32),
-            dma((4, 2)),
+            dma((5,)),
         ],
         (10**6, 10**6),
         "pack_columns",
-    )(latent, moment_one, moment_two, target_rgb, hole_mask)
+    )(*map(in_hbm, (latent, moment_one, moment_two, target_rgb, hole_mask)))
     columns = [swap(piece, "col", side) for side, piece in enumerate(columns)]
 
     matrix = shape((12 * size, 2 * size), BF16)
@@ -554,6 +555,7 @@
         "pack_weights",
     )(kernel_one, kernel_two, rgb_weight, bias_one[None], bias_two[None])
 
+    columns, weights = lax.optimization_barrier((columns, weights))
     own, lines, near, far, spots, inside = call(
         functools.partial(pack_rows, sides),
         [tall(height), lines_of(height), short(EDGE + 1), short(EDGE + 1)]
@@ -608,24 +610,23 @@
     out = shape(latent.shape, F32)
     results = call(
         last_near,
-        passed + [out] * 3,
+        passed + [lines_of(rest)] * 3,
         [VMEM] * (9 + 6),
-        [VMEM] * 4 + [HBM] * 3,
-        [vmem(lines_of(rest))] * 3 + [vmem(tall(EDGE))] + near_scratch + [dma((3, rest))],
+        [VMEM] * 7,
+        [vmem(tall(EDGE))] + near_scratch,
         near_work,
         "last_near",
     )(low, high, near_next, z_high, m_high, v_high, aims_near, known_near, inside, *weights)
-    handed, outs = results[:4], results[4:]
+    handed, ready = results[:4], results[4:]
     return call(
         last_far,
         [out] * 3,
-        [VMEM] * (8 + 4 + 6) + [HBM] * 3,
+        [VMEM] * (8 + 4 + 6 + 3),
         [HBM] * 3,
-        [vmem(lines_of(some))] * 3 + [vmem(tall(EDGE))] + far_scratch + [dma((3, some))],
+        [vmem(lines_of(some))] * 3 + [vmem(tall(EDGE))] + far_scratch + [dma((3, height))],
         far_work,
         "last_far",
-        {18: 0, 19: 1, 20: 2},
-    )(low, far_next, z_low, m_low, v_low, aims_far, known_far, inside, *handed, *weights, *outs)
+    )(low, far_next, z_low, m_low, v_low, aims_far, known_far, inside, *handed, *weights, *ready)
 
 
 def solution(mesh):

time: 32.7 us -> 27.9 us (0.85)
  local copies, waits for them, and re-layouts: 4.54 us -> 0.67 us
  waiting for transfers between devices: 1.45 us -> 0.17 us
  Pallas kernels: 14.6 us -> 15.1 us
    unnamed x24 -> x10, local copies, waits for them, and re-layouts: 4.54 us -> 0.67 us
    ppermute x5, waiting for transfers between devices: 1.45 us -> 0.17 us  [swap(): return lax.ppermute(block, axes, pairs(lax.axis_size(axes), parity))]
    pallas_call x1, Pallas kernels: 0.31 us -> 1.53 us  [body(): call(functools.partial(pack_columns, sides), [shape(block, BF16)] * sides...]
    pallas_call x2, Pallas kernels: 7.48 us -> 6.82 us  [the longest x1 3.47 us: body(): call(last_far, [out] * 3, [VMEM] * (8 + 4 + 6 + 3), [HBM] * 3, [vmem(line...]
  transfers between devices with their start and end apart: 5 -> 5, of which waited for: 1 -> 1; matrix products, arithmetic and copies ran while one was open for 0% -> 0% of each run, Pallas kernels for 34% -> 36%
where the time goes in v3:
time: 27.9 us; the launch traced here: 27.7 us
  Pallas kernels  15.1 us (54%)
  starting transfers between devices  11 us (39%)
  between operations  0.76 us (3%)
  local copies, waits for them, and re-layouts  0.67 us (2%)
    ppermute x5, starting transfers between devices, swap(): return lax.ppermute(block, axes, pairs(lax.axis_size(axes), parity))  11 us
    pallas_call x1, Pallas kernels, body(): call(functools.partial(first_near, sides), passed + [tall(rest), short(ED...  3.55 us
    pallas_call x1, Pallas kernels, body(): call(last_far, [out] * 3, [VMEM] * (8 + 4 + 6 + 3), [HBM] * 3, [vmem(line...  3.47 us
    pallas_call x1, Pallas kernels, body(): call(last_near, passed + [lines_of(rest)] * 3, [VMEM] * (9 + 6), [VMEM] *...  3.36 us
    pallas_call x1, Pallas kernels, body(): call(first_far, [tall(some), short(EDGE), lines_of(some), lines_of(some),...  2.48 us
    pallas_call x1, Pallas kernels, body(): call(functools.partial(pack_columns, sides), [shape(block, BF16)] * sides...  1.53 us
    unnamed x10, local copies, waits for them, and re-layouts  0.67 us
    pallas_call x1, Pallas kernels, body(): call(pack_weights, [matrix] * 4 + [shape((size, size), BF16), shape((2, 8...  0.58 us
  transfers between devices with their start and end apart: 5, of which 1 were waited for; matrix products, arithmetic and copies ran while one was open for 0% of the time, Pallas kernels for 36%

profile of v3, /device:TPU:1, one launch (start us, length us, event | category | flops | bytes accessed | tf_op | source)
XLA Modules:
  0.0 27.7 jit_solution(2306977593159284999)
XLA Ops:
  0.6 0.0 copy-start.1
  0.6 0.0 copy-start
  0.7 0.0 copy-start.4
  0.7 1.5 %pack_columns.1 = (bf16[22,8,128]{2,1,0:T(8,128)(2,1)S(1)}, bf16[128,128]{1,0:T(8,128)(2,1)S(1)}, f32[8,128,128]{2,1,0:T(8,128)S(1)}, f32[8,128,128]{2,1,0:T(8,128)S(1)}, f32[8,128,128]{2,1,0:T(8,128)S(1)}) custom-call(f32[8,128,128]{2,1,0:T(8,128)} %latent.1, f32[8,128,128]{2,1,0:T(8,128)} %first.1, f32[8,128,128]{2,1,0:T(8,128)} %second.1, ...), custom_call_target="tpu_custom_call" | custom-call | flops 1000000 | bytes 1000000 | tf_op jit(solution)/shard_map/pack_columns/pallas_call | solution.py:528
  2.2 2.1 %collective-permute-start = (bf16[22,8,128]{2,1,0:T(8,128)(2,1)S(1)}, bf16[22,8,128]{2,1,0:T(8,128)(2,1)S(1)}, u32[]{:S(2)}, u32[]{:S(2)}) collective-permute-start(bf16[22,8,128]{2,1,0:T(8,128)(2,1)S(1)} %get-tuple-element.56), channel_id=1, source_target_pairs={{0,2},{2,0},{1,3},{3,1},{4,6},{6,4},{5,7},{7,5},{8,10},{10,8},{9,1... | collective-permute-start | bytes 135176 | tf_op jit(solution)/shard_map/ppermute | solution.py:42
  4.3 0.0 copy-start.2
  4.3 0.0 copy-start.3
  4.3 0.0 copy-done.1
  4.3 0.0 copy-done
  4.3 0.0 copy-done.4
  4.3 0.7 %copy-done.2 = bf16[3,128]{1,0:T(4,128)(2,1)S(1)} copy-done((bf16[3,128]{1,0:T(4,128)(2,1)S(1)}, bf16[3,128]{1,0:T(4,128)(2,1)}, u32[]{:S(2)}) %copy-start.2) | copy-done | bytes 792
  5.0 0.0 copy-done.3
  5.0 0.6 %pack_weights.1 = (bf16[1536,256]{1,0:T(8,128)(2,1)S(1)}, bf16[1536,256]{1,0:T(8,128)(2,1)S(1)}, bf16[1536,256]{1,0:T(8,128)(2,1)S(1)}, bf16[1536,256]{1,0:T(8,1...) custom-call(bf16[3,3,128,128]{3,2,1,0:T(8,128)(2,1)S(1)} %copy-done, ...), custom_call_target="tpu_custom_call" | custom-call | flops 1000000 | bytes 4000000 | tf_op jit(solution)/shard_map/pack_weights/pallas_call | solution.py:548
  5.6 0.2 collective-permute-done.rest_0_.refs_0_
  5.7 0.1 pack_rows.1
  5.9 1.6 %collective-permute-start.1 = (bf16[5,9,16,128]{3,2,1,0:T(8,128)(2,1)S(1)}, bf16[5,9,16,128]{3,2,1,0:T(8,128)(2,1)S(1)}, u32[]{:S(2)}, u32[]{:S(2)}) collective-permute-start(bf16[5,9,16,128]{3,2,1,0:T(8,128)(2,1)S(1)} %get-tuple-element.68), channel_id=1, source_target_pairs={{0,1},{1,0},{4,5},{5,4},{8,9},{9,8},{12,13},{13,12},{2,3},{3,2},{6... | collective-permute-start | bytes 552968 | tf_op jit(solution)/shard_map/ppermute | solution.py:42
  7.5 3.6 %collective-permute-start.2 = (bf16[5,9,16,128]{3,2,1,0:T(8,128)(2,1)S(1)}, bf16[5,9,16,128]{3,2,1,0:T(8,128)(2,1)S(1)}, u32[]{:S(2)}, u32[]{:S(2)}) collective-permute-start(bf16[5,9,16,128]{3,2,1,0:T(8,128)(2,1)S(1)} %get-tuple-element.79), channel_id=1, source_target_pairs={{1,4},{4,1},{5,8},{8,5},{9,12},{12,9},{3,6},{6,3},{7,10},{10,7},{1... | collective-permute-start | bytes 552968 | tf_op jit(solution)/shard_map/ppermute | solution.py:42
  11.1 0.0 collective-permute-done.1.near
  11.1 3.5 %first_near.1 = (bf16[2,11,16,128]{3,2,1,0:T(8,128)(2,1)S(1)}, f32[2,144,128]{2,1,0:T(8,128)S(1)}, bf16[2,11,16,128]{3,2,1,0:T(8,128)(2,1)S(1)}, bf16[2,11,16,12...) custom-call(bf16[8,11,16,128]{3,2,1,0:T(8,128)(2,1)S(1)} %get-tuple-, ...), custom_call_target="tpu_custom_call" | custom-call | flops 1585446912 | bytes 10000000 | tf_op jit(solution)/shard_map/first_near/pallas_call | solution.py:584
  14.7 0.1 collective-permute-start.4
  14.8 0.0 collective-permute-done.2.far
  14.8 2.5 %first_far.1 = (bf16[4,11,16,128]{3,2,1,0:T(8,128)(2,1)S(1)}, bf16[4,9,16,128]{3,2,1,0:T(8,128)(2,1)S(1)}, f32[4,144,128]{2,1,0:T(8,128)S(1)}, f32[4,144,128]{2,...) custom-call(bf16[8,11,16,128]{3,2,1,0:T(8,128)(2,1)S(1)} %get-tuple-element.64., ...), custom_call_target="tpu_custom_call" | custom-call | flops 905969664 | bytes 10000000 | tf_op jit(solution)/shard_map/first_far/pallas_call | solution.py:598
  17.3 3.6 %collective-permute-start.3 = (bf16[4,9,16,128]{3,2,1,0:T(8,128)(2,1)S(1)}, bf16[4,9,16,128]{3,2,1,0:T(8,128)(2,1)S(1)}, u32[]{:S(2)}, u32[]{:S(2)}) collective-permute-start(bf16[4,9,16,128]{3,2,1,0:T(8,128)(2,1)S(1)} %get-tuple-element.85), channel_id=1, source_target_pairs={{1,4},{4,1},{5,8},{8,5},{9,12},{12,9},{3,6},{6,3},{7,10},{10,7},{1... | collective-permute-start | bytes 442376 | tf_op jit(solution)/shard_map/ppermute | solution.py:42
  20.8 0.0 collective-permute-done.4.near
  20.9 3.4 %last_near.1 = (bf16[2,11,16,128]{3,2,1,0:T(8,128)(2,1)S(1)}, f32[2,144,128]{2,1,0:T(8,128)S(1)}, bf16[2,11,16,128]{3,2,1,0:T(8,128)(2,1)S(1)}, bf16[2,11,16,128...) custom-call(bf16[4,11,16,128]{3,2,1,0:T(8,128)(2,1)S(1)} %get-tuple-, ...), custom_call_target="tpu_custom_call" | custom-call | flops 1585446912 | bytes 10000000 | tf_op jit(solution)/shard_map/last_near/pallas_call | solution.py:611
  24.2 0.0 collective-permute-done.3.far
  24.2 3.5 %last_far.1 = (f32[8,128,128]{2,1,0:T(8,128)}, f32[8,128,128]{2,1,0:T(8,128)}, f32[8,128,128]{2,1,0:T(8,128)}) custom-call(bf16[4,11,16,128]{3,2,1,0:T(8,128)(2,1)S(1)} %get-tuple-element.84.low, bf16[4,9,16,128]{3,2,1,0:T(8,128)(2,1)S(1)} %collective-permute-done.3.far, f32[4,144,128]{2,1,0:T(8,128)S(1)} %get-tuple-element.86.z_in, ...), custom_call_target="tpu_custom_call" | custom-call | flops 905969664 | bytes 10000000 | tf_op jit(solution)/shard_map/last_far/pallas_call | solution.py:621
Async XLA Ops:
  0.6 3.7 %copy-start.1 = (bf16[3,3,128,128]{3,2,1,0:T(8,128)(2,1)S(1)}, bf16[3,3,128,128]{3,2,1,0:T(8,128)(2,1)}, u32[]{:S(2)}) copy-start(bf16[3,3,128,128]{3,2,1,0:T(8,128)(2,1)} %two.1) | copy-start | bytes 884740
  0.6 3.7 %copy-start = (bf16[3,3,128,128]{3,2,1,0:T(8,128)(2,1)S(1)}, bf16[3,3,128,128]{3,2,1,0:T(8,128)(2,1)}, u32[]{:S(2)}) copy-start(bf16[3,3,128,128]{3,2,1,0:T(8,128)(2,1)} %one.1) | copy-start | bytes 884740
  0.7 3.7 %copy-start.4 = (f32[128]{0:T(128)S(1)}, f32[128]{0:T(128)}, u32[]{:S(2)}) copy-start(f32[128]{0:T(128)} %param.18) | copy-start | bytes 1540
  2.2 3.5 %collective-permute-start = (bf16[22,8,128]{2,1,0:T(8,128)(2,1)S(1)}, bf16[22,8,128]{2,1,0:T(8,128)(2,1)S(1)}, u32[]{:S(2)}, u32[]{:S(2)}) collective-permute-start(bf16[22,8,128]{2,1,0:T(8,128)(2,1)S(1)} %get-tuple-element.56), channel_id=1, source_target_pairs={{0,2},{2,0},{1,3},{3,1},{4,6},{6,4},{5,7},{7,5},{8,10},{10,8},{9,1... | collective-permute-start | bytes 135176 | tf_op jit(solution)/shard_map/ppermute | solution.py:42
  4.3 0.7 %copy-start.2 = (bf16[3,128]{1,0:T(4,128)(2,1)S(1)}, bf16[3,128]{1,0:T(4,128)(2,1)}, u32[]{:S(2)}) copy-start(bf16[3,128]{1,0:T(4,128)(2,1)} %rgb.1) | copy-start | bytes 2308
  4.3 0.7 %copy-start.3 = (f32[128]{0:T(128)S(1)}, f32[128]{0:T(128)}, u32[]{:S(2)}) copy-start(f32[128]{0:T(128)} %param.16) | copy-start | bytes 1540
  5.9 5.3 %collective-permute-start.1 = (bf16[5,9,16,128]{3,2,1,0:T(8,128)(2,1)S(1)}, bf16[5,9,16,128]{3,2,1,0:T(8,128)(2,1)S(1)}, u32[]{:S(2)}, u32[]{:S(2)}) collective-permute-start(bf16[5,9,16,128]{3,2,1,0:T(8,128)(2,1)S(1)} %get-tuple-element.68), channel_id=1, source_target_pairs={{0,1},{1,0},{4,5},{5,4},{8,9},{9,8},{12,13},{13,12},{2,3},{3,2},{6... | collective-permute-start | bytes 552968 | tf_op jit(solution)/shard_map/ppermute | solution.py:42
  7.5 7.3 %collective-permute-start.2 = (bf16[5,9,16,128]{3,2,1,0:T(8,128)(2,1)S(1)}, bf16[5,9,16,128]{3,2,1,0:T(8,128)(2,1)S(1)}, u32[]{:S(2)}, u32[]{:S(2)}) collective-permute-start(bf16[5,9,16,128]{3,2,1,0:T(8,128)(2,1)S(1)} %get-tuple-element.79), channel_id=1, source_target_pairs={{1,4},{4,1},{5,8},{8,5},{9,12},{12,9},{3,6},{6,3},{7,10},{10,7},{1... | collective-permute-start | bytes 552968 | tf_op jit(solution)/shard_map/ppermute | solution.py:42
  14.7 6.2 %collective-permute-start.4 = (bf16[4,9,16,128]{3,2,1,0:T(8,128)(2,1)S(1)}, bf16[4,9,16,128]{3,2,1,0:T(8,128)(2,1)S(1)}, u32[]{:S(2)}, u32[]{:S(2)}) collective-permute-start(bf16[4,9,16,128]{3,2,1,0:T(8,128)(2,1)S(1)} %get-tuple-element.92), channel_id=1, source_target_pairs={{0,1},{1,0},{4,5},{5,4},{8,9},{9,8},{12,13},{13,12},{2,3},{3,2},{6... | collective-permute-start | bytes 442376 | tf_op jit(solution)/shard_map/ppermute | solution.py:42
  17.3 7.0 %collective-permute-start.3 = (bf16[4,9,16,128]{3,2,1,0:T(8,128)(2,1)S(1)}, bf16[4,9,16,128]{3,2,1,0:T(8,128)(2,1)S(1)}, u32[]{:S(2)}, u32[]{:S(2)}) collective-permute-start(bf16[4,9,16,128]{3,2,1,0:T(8,128)(2,1)S(1)} %get-tuple-element.85), channel_id=1, source_target_pairs={{1,4},{4,1},{5,8},{8,5},{9,12},{12,9},{3,6},{6,3},{7,10},{10,7},{1... | collective-permute-start | bytes 442376 | tf_op jit(solution)/shard_map/ppermute | solution.py:42

commit v4 on v3

--- a/solution.py
+++ b/solution.py
@@ -40,6 +40,31 @@
 
 def swap(block, axes, parity):
     return lax.ppermute(block, axes, pairs(lax.axis_size(axes), parity))
+
+
+def swap_near(block):
+    return swap(block, ROWS, 0)
+
+
+def swap_far(block):
+    rows, cols, cores = (lax.axis_size(name) for name in ("row", "col", "cores"))
+    count = rows * cores
+
+    def index(place, col):
+        return (place // cores * cols + col) * cores + place % cores
+
+    chosen = []
+    for col in range(cols):
+        chosen += [(index(a, col), index(b, col)) for a, b in pairs(count, 1)]
+    for place in (0, count - 1):
+        chosen += [(index(place, a), index(place, b)) for a, b in pairs(cols, 0)]
+    return lax.ppermute(block, ("row", "col", "cores"), sorted(chosen))
+
+
+def far_there():
+    place, count = row_place(), lax.axis_size("row") * lax.axis_size("cores")
+    odd = lax.rem(place, 2) == 1
+    return jnp.where(odd, place < count - 1, place > 0).astype(F32)
 
 
 def call(kernel, out_shape, in_specs, out_specs, scratch, cost, name, aliases=None, limit=24 << 20):
@@ -80,15 +105,18 @@
 
 def pack_columns(sides, latent, first, second, target, mask, *rest):
     outs, rest = rest[:sides], rest[sides:]
-    turned, *inner, aim, known, planes, flat, sem = rest
+    turned, ends, aim, known, planes, flat, sem = rest
     height, breadth = latent.shape[0], latent.shape[1]
     early = [
-        pltpu.make_async_copy(target, aim, sem.at[3]),
-        pltpu.make_async_copy(mask, known, sem.at[4]),
+        pltpu.make_async_copy(target, aim, sem.at[3, 0]),
+        pltpu.make_async_copy(mask, known, sem.at[3, 1]),
     ]
     copies = [
-        pltpu.make_async_copy(source, dest, sem.at[number])
-        for number, (source, dest) in enumerate(zip((latent, first, second), inner))
+        pltpu.make_async_copy(
+            source.at[:, pl.ds(start, SIDE)], ends.at[number, end], sem.at[number, end]
+        )
+        for number, source in enumerate((latent, first, second))
+        for end, start in enumerate((0, breadth - SIDE))
     ]
     for copy in early + copies:
         copy.start()
@@ -114,10 +142,7 @@
         flat[height + 1] = jnp.zeros(flat.shape[1:], F32)
         for row in range(height):
             source = pick_row(row, height)
-            own = [
-                jnp.where(right, block[source, breadth - SIDE :], block[source, :SIDE])
-                for block in inner
-            ]
+            own = [jnp.where(right, ends[n, 1, source], ends[n, 0, source]) for n in range(3)]
             flat[row] = own[0]
             own[0] = own[0] - own[0].astype(BF16).astype(F32)
             for number, piece in enumerate(own):
@@ -128,8 +153,16 @@
 
 
 def pack_weights(one, two, rgb, bias_one, bias_two, *refs):
-    ahead_one, ahead_two, back_one, back_two, colors, bias, held = refs
+    given, loaded, refs = refs[:3], refs[10:13], refs[3:10] + refs[13:]
+    ahead_one, ahead_two, back_one, back_two, colors, spread, bias, held, sem = refs
+    copies = [
+        pltpu.make_async_copy(source, dest, sem.at[number])
+        for number, (source, dest) in enumerate(zip(given, loaded))
+    ]
+    for copy in copies:
+        copy.start()
     size = one.shape[2]
+    half = jnp.asarray(0.5, BF16)
     odd = lax.rem(row_place(), 2) == 1
     for kernel, ahead, back in ((one, ahead_one, back_one), (two, ahead_two, back_two)):
         for row in range(4):
@@ -138,32 +171,48 @@
                 for out in range(2):
                     tap = row - out
                     if 0 <= tap <= 2:
-                        front = kernel[jnp.where(odd, 2 - tap, tap), col]
+                        front = kernel[jnp.where(odd, 2 - tap, tap), col] * half
                         rear = kernel[jnp.where(odd, tap, 2 - tap), 2 - col]
                         rear = rear.astype(F32).T.astype(BF16)
+                        if kernel is two:
+                            rear = rear * half
                     else:
                         front = rear = jnp.zeros((size, size), BF16)
                     ahead[at : at + size, out * size : (out + 1) * size] = front
                     back[at : at + size, out * size : (out + 1) * size] = rear
     held[...] = jnp.zeros_like(held)
-    held[0:3] = rgb[...].astype(F32)
-    held[3:6] = rgb[...].astype(F32)
+    for at in (0, size):
+        held[at : at + 3, at : at + size] = rgb[...].astype(F32)
+        held[at + 3 : at + 6, at : at + size] = rgb[...].astype(F32)
     colors[...] = held[...].astype(BF16)
-    bias[0] = jnp.broadcast_to(bias_one[...], bias.shape[1:])
-    bias[1] = jnp.broadcast_to(bias_two[...], bias.shape[1:])
-
-
-def put(dest, row, value, strip):
-    dest[row, 1 : strip + 1] = value.astype(BF16).reshape(strip, STRIPS, -1)
-    dest[row, 0] = pltpu.roll(value[(strip - 1) * STRIPS :], 1, 0).astype(BF16)
-    dest[row, strip + 1] = pltpu.roll(value[:STRIPS], STRIPS - 1, 0).astype(BF16)
-
-
-def widen(dest, source, strip):
+    spread[...] = (0.5 * held[...]).astype(BF16)
+    for number, given in enumerate((bias_one, bias_two)):
+        for at in (0, size):
+            bias[number, :, at : at + size] = jnp.broadcast_to(0.5 * given[...], (8, size))
+    for copy in copies:
+        copy.wait()
+
+
+def put(dest, row, value, strip, keep=None):
+    low, high = value[:STRIPS], value[(strip - 1) * STRIPS :]
+    value = value.astype(BF16)
+    if keep is not None:
+        value = value * keep
+        low = low * keep[:STRIPS].astype(F32)
+        high = high * keep[(strip - 1) * STRIPS :].astype(F32)
+    dest[row, 1 : strip + 1] = value.reshape(strip, STRIPS, -1)
+    dest[row, 0] = pltpu.roll(high, 1, 0).astype(BF16)
+    dest[row, strip + 1] = pltpu.roll(low, STRIPS - 1, 0).astype(BF16)
+
+
+def widen(dest, source, strip, there=None):
     for row in range(EDGE):
-        dest[row, 1 : strip + 1] = source[row]
-        dest[row, 0] = pltpu.roll(source[row, strip - 1].astype(F32), 1, 0).astype(BF16)
-        dest[row, strip + 1] = pltpu.roll(source[row, 0].astype(F32), STRIPS - 1, 0).astype(BF16)
+        value, low, high = source[row], source[row, 0].astype(F32), source[row, strip - 1].astype(F32)
+        if there is not None:
+            value, low, high = value * there.astype(BF16), low * there, high * there
+        dest[row, 1 : strip + 1] = value
+        dest[row, 0] = pltpu.roll(high, 1, 0).astype(BF16)
+        dest[row, strip + 1] = pltpu.roll(low, STRIPS - 1, 0).astype(BF16)
 
 
 def strips_of(source, row, strip):
@@ -236,18 +285,22 @@
 
 
 def aim_rows(aims, known, spots):
-    size = aims.shape[2]
+    size = aims.shape[2] // 2
     lane_in = lax.broadcasted_iota(jnp.int32, (size, 2 * size), 0)
     lane_out = lax.broadcasted_iota(jnp.int32, (size, 2 * size), 1)
     color = lax.rem(lane_out, 3)
     aimed = (lane_out < 6) & ((lane_in == color) | (lane_in == color + 3))
     masked = (lane_out >= size) & (lane_out < size + 6) & (lane_in == 6)
     chosen = (aimed | masked).astype(F32).astype(BF16)
-    for row, (spot, source) in enumerate(spots):
+
+    def aim(row, spot, source):
         value = pltpu.roll(spot, lax.rem(size - PLANES * source, size), 1)
         both = jnp.dot(value.astype(BF16), chosen, preferred_element_type=F32)
-        aims[row] = both[:, :size]
-        known[row] = both[:, size:]
+        lanes = slice(row % 2 * size, (row % 2 + 1) * size)
+        aims[row // 2, :, lanes] = both[:, :size]
+        known[row // 2, :, lanes] = both[:, size:]
+
+    return [functools.partial(aim, row, *spot) for row, spot in enumerate(spots)]
 
 
 def conv_pair(rows, first, weights, strip):
@@ -256,68 +309,111 @@
         source, at = rows[first + down]
         for across in range(3):
             taps.append(source[at, across : across + strip].reshape(strip * STRIPS, -1))
-    return jnp.dot(jnp.concatenate(taps, axis=1), weights[...], preferred_element_type=F32)
+    half = weights.shape[0] // 2
+    parts = [
+        jnp.dot(
+            jnp.concatenate(taps[6 * part : 6 * part + 6], axis=1),
+            weights[half * part : half * (part + 1)],
+            preferred_element_type=F32,
+        )
+        for part in range(2)
+    ]
+    return parts[0] + parts[1]
 
 
 def sigma_of(value):
     return 0.5 * jnp.tanh(0.5 * value) + 0.5
 
 
-def gradient(firsts, rows, weights, aims, known, inside, emit):
+def gradient(order, rows, weights, aims, known, inside, emit, beside=(), parts=True):
     wide, hidden, slope, grad_two, grad_one = rows
-    ahead_one, ahead_two, back_one, back_two, colors, bias = weights
+    ahead_one, ahead_two, back_one, back_two, colors, spread, bias = weights
     pixels, size = inside.shape
     strip = pixels // STRIPS
-    place, count = row_place(), lax.axis_size("row") * lax.axis_size("cores")
-    odd = lax.rem(place, 2) == 1
-    there = jnp.where(odd, place < count - 1, place > 0).astype(F32)
-    columns = inside[...]
-    halves = lambda both: (both[:, :size], both[:, size:])
-
-    for first in firsts[0]:
-        for half, summed in enumerate(halves(conv_pair(wide, first - 1, ahead_one, strip))):
+    there = far_there()
+    low = min(first for stage, first in filter(None, order) if stage == 1)
+
+    def keep_of(row):
+        return (inside[...] * there if row < EDGE else inside[...]).astype(BF16)
+
+    def half_of(both, half):
+        return both[:, half * size : (half + 1) * size]
+
+    def gate(both, number):
+        value = both + bias[number, :1]
+        twice = jnp.tanh(value) + 1.0
+        hid = value * twice
+        return hid, twice + hid * (2.0 - twice)
+
+    def ahead_first(first):
+        both = conv_pair(wide, first - 1, ahead_one, strip)
+        yield
+        hid, twice = gate(both, 0)
+        for half in range(2):
             row = first + half
-            value = summed + bias[0, :1]
-            sigma = sigma_of(value)
-            hid = value * sigma
-            keep = columns * there if row < EDGE else columns
-            put(*hidden[row], hid * keep, strip)
+            put(*hidden[row], half_of(hid, half), strip, keep_of(row))
             if row in slope:
                 held, at = slope[row]
-                held[at] = (sigma + hid * (1.0 - sigma)) * keep
-
-    lane = lax.broadcasted_iota(jnp.int32, (2 * pixels, size), 1)
-    for number, first in enumerate(firsts[1]):
+                held[at] = half_of(twice, half)
+
+    def ahead_second(first):
+        number = (first - low) // 2
         both = conv_pair(hidden, first - 1, ahead_two, strip)
-        value = jnp.concatenate(halves(both), axis=0) + bias[1, :1]
-        sigma = sigma_of(value)
-        hid = value * sigma
+        yield
+        hid, twice = gate(both, 1)
         color = lax.dot_general(
             hid.astype(BF16), colors[...], (((1,), (1,)), ((), ())), preferred_element_type=F32
         )
-        spot = slice(2 * number, 2 * number + 2)
-        residual = known[spot].reshape(2 * pixels, -1) * color - aims[spot].reshape(2 * pixels, -1)
+        if parts:
+            yield
+        residual = known[number] * color - aims[number]
         rest = residual - residual.astype(BF16).astype(F32)
-        split = jnp.where(lane < 3, residual, rest).astype(BF16)
-        spread = jnp.dot(split, colors[...], preferred_element_type=F32)
-        result = spread * (sigma + hid * (1.0 - sigma))
+        lane = lax.broadcasted_iota(jnp.int32, (pixels, 2 * size), 1)
+        split = jnp.where(lax.rem(lane, size) < 3, residual, rest).astype(BF16)
+        back = jnp.dot(split, spread[...], preferred_element_type=F32)
+        if parts:
+            yield
+        result = back * twice
         for half in range(2):
-            put(*grad_two[first + half], result[half * pixels : (half + 1) * pixels], strip)
-
-    for first in firsts[2]:
-        for half, summed in enumerate(halves(conv_pair(grad_two, first - 1, back_two, strip))):
-            held, at = slope[first + half]
-            put(*grad_one[first + half], summed * held[at], strip)
-
-    for first in firsts[3]:
-        for half, summed in enumerate(halves(conv_pair(grad_one, first - 1, back_one, strip))):
-            emit(first + half - EDGE, summed)
+            put(*grad_two[first + half], half_of(result, half), strip)
+
+    def back_second(first):
+        both = conv_pair(grad_two, first - 1, back_two, strip)
+        yield
+        for half in range(2):
+            row = first + half
+            held, at = slope[row]
+            put(*grad_one[row], half_of(both, half) * held[at], strip, keep_of(row))
+
+    def back_first(first):
+        both = conv_pair(grad_one, first - 1, back_one, strip)
+        yield
+        for half in range(2):
+            emit(first + half - EDGE, half_of(both, half))
+
+    stages = (ahead_first, ahead_second, back_second, back_first)
+    beside = list(beside)
+    active = []
+    slots = list(order)
+    while slots or active:
+        started = None
+        if slots:
+            item = slots.pop(0)
+            if item is not None:
+                started = stages[item[0]](item[1])
+                next(started)
+        if beside:
+            beside.pop(0)()
+        active = [task for task in active if next(task, active) is None]
+        if started is not None:
+            active.append(started)
 
 
 def adam(current, first, second, grad):
     first = BETA_ONE * first + (1.0 - BETA_ONE) * grad
     second = BETA_TWO * second + (1.0 - BETA_TWO) * grad * grad
-    return current - LEARN_RATE * first / (jnp.sqrt(second) + EPSILON), first, second
+    root = second * lax.rsqrt(jnp.maximum(second, 1e-30))
+    return current - (LEARN_RATE * first) / (root + EPSILON), first, second
 
 
 def place_rows(*parts):
@@ -328,12 +424,28 @@
     return rows
 
 
-def near_firsts(height):
-    return [range(5 + n, height + 7 - n, 2) for n in range(4)]
-
-
-def far_firsts():
-    return [range(1 + n, 5 + n, 2) for n in range(4)]
+def near_order(height):
+    firsts = [list(range(5 + n, height + 7 - n, 2)) for n in range(4)]
+    delay = (2, 4, 2)
+    done, order = {}, []
+    while any(firsts):
+        slot = len(order)
+        for stage in (3, 2, 1, 0):
+            if not firsts[stage]:
+                continue
+            first = firsts[stage][0]
+            needs = [(stage - 1, first - 1), (stage - 1, first + 1)] if stage else []
+            if all(done.get(need, slot) + delay[stage - 1] <= slot for need in needs):
+                done[stage, first] = slot
+                order.append((stage, firsts[stage].pop(0)))
+                break
+        else:
+            order.append(None)
+    return order
+
+
+def far_order():
+    return [(0, 3), (0, 1), (1, 4), (1, 2), (2, 5), (2, 3), (3, 6), (3, 4)]
 
 
 def near_rows(height, own, halo, passed, scratch):
@@ -360,13 +472,21 @@
     )
 
 
+def pair_up(tasks):
+    def both(one, two):
+        one()
+        two()
+
+    return [functools.partial(both, *tasks[at : at + 2]) for at in range(0, len(tasks), 2)]
+
+
 def flat_spot(spots):
     return spots[...].reshape(-1, spots.shape[-1]).astype(F32)
 
 
 def first_near(sides, own, lines, moment_one, moment_two, near, spots, inside, *refs):
     pieces, refs = refs[:sides], refs[sides:]
-    weights, refs = refs[:6], refs[6:]
+    weights, refs = refs[:7], refs[7:]
     passed, refs = refs[:4], refs[4:]
     (new, near_out, z_out, m_out, v_out, m_rest, v_rest, aims, known), refs = refs[:9], refs[9:]
     halo, m_held, v_held, *scratch = refs
@@ -374,7 +494,7 @@
     strip = own.shape[1] - 2
     widen(halo, near, strip)
     mine, theirs = flat_spot(spots), flat_spot(near.at[EDGE])
-    aim_rows(
+    tasks = aim_rows(
         aims,
         known,
         [(mine, pick_row(row, height)) for row in range(2, height)]
@@ -408,19 +528,19 @@
             near_out[height - 1 - row] = current.astype(BF16).reshape(near_out.shape[1:])
 
     rows = near_rows(height, place_rows((4, height + 4, own, 0)), halo, passed, scratch)
-    gradient(near_firsts(height), rows, weights, aims, known, inside, emit)
+    gradient(near_order(height), rows, weights, aims, known, inside, emit, pair_up(tasks))
 
 
 def first_far(own, lines, m_rest, v_rest, far, spots, inside, *refs):
     passed, refs = refs[:4], refs[4:]
-    weights, refs = refs[:6], refs[6:]
+    weights, refs = refs[:7], refs[7:]
     (new, far_out, z_out, m_out, v_out, aims, known), refs = refs[:7], refs[7:]
     halo, *scratch = refs
     height = own.shape[0]
     strip = own.shape[1] - 2
-    widen(halo, far, strip)
-    mine, theirs = flat_spot(spots), flat_spot(far.at[EDGE])
-    aim_rows(
+    widen(halo, far, strip, far_there())
+    mine, theirs = flat_spot(spots), flat_spot(far.at[EDGE]) * far_there()
+    tasks = aim_rows(
         aims,
         known,
         [(theirs, pick_partner_row(row, height)) for row in (1, 0)]
@@ -437,7 +557,7 @@
         far_out[EDGE - 1 - row] = current.astype(BF16).reshape(far_out.shape[1:])
 
     rows = far_rows(place_rows((4, 8, own, 0)), halo, passed, scratch)
-    gradient(far_firsts(), rows, weights, aims, known, inside, emit)
+    gradient(far_order(), rows, weights, aims, known, inside, emit, pair_up(tasks), False)
 
 
 def keep_row(held, at, value, strip):
@@ -446,7 +566,7 @@
 
 
 def last_near(low, high, near, z_in, m_in, v_in, aims, known, inside, *refs):
-    weights, refs = refs[:6], refs[6:]
+    weights, refs = refs[:7], refs[7:]
     passed, refs = refs[:4], refs[4:]
     helds, refs = refs[:3], refs[3:]
     halo, *scratch = refs
@@ -461,12 +581,12 @@
 
     own = place_rows((4, 8, low, 0), (8, height + 4, high, 0))
     rows = near_rows(height, own, halo, passed, scratch)
-    gradient(near_firsts(height), rows, weights, aims, known, inside, emit)
+    gradient(near_order(height), rows, weights, aims, known, inside, emit)
 
 
 def last_far(low, far, z_in, m_in, v_in, aims, known, inside, *refs):
     passed, refs = refs[:4], refs[4:]
-    weights, refs = refs[:6], refs[6:]
+    weights, refs = refs[:7], refs[7:]
     ready, outs, helds, refs = refs[:3], refs[3:6], refs[6:9], refs[9:]
     halo, *scratch, sem = refs
     height, breadth = outs[0].shape[:2]
@@ -485,7 +605,7 @@
     for row in range(EDGE, height):
         for number in range(3):
             send(row, number, ready[number], row - EDGE)
-    widen(halo, far, strip)
+    widen(halo, far, strip, far_there())
 
     def emit(row, grad):
         for number, value in enumerate(adam(z_in[row], m_in[row], v_in[row], grad)):
@@ -493,7 +613,7 @@
             send(row, number, helds[number], row)
 
     rows = far_rows(place_rows((4, 8, low, 0)), halo, passed, scratch)
-    gradient(far_firsts(), rows, weights, aims, known, inside, emit)
+    gradient(far_order(), rows, weights, aims, known, inside, emit, (), False)
     for copy in copies:
         copy.wait()
 
@@ -522,38 +642,41 @@
     tall = lambda rows: shape((rows, strip + 2, STRIPS, size), BF16)
     short = lambda rows: shape((rows, strip, STRIPS, size), BF16)
     lines_of = lambda rows: shape((rows, pixels, size), F32)
+    aims_of = lambda rows: shape((rows // 2, pixels, 2 * size), F32)
     vmem = lambda like: pltpu.VMEM(like.shape, like.dtype)
     work = 2 * 12 * 2 * pixels * size * size
 
-    *columns, turned, latent, moment_one, moment_two = call(
+    given = tuple(map(in_hbm, (latent, moment_one, moment_two)))
+    *columns, turned = call(
         functools.partial(pack_columns, sides),
         [shape(block, BF16)] * sides
-        + [shape((breadth, size), BF16)]
-        + [shape(latent.shape, F32)] * 3,
+        + [shape((breadth, size), BF16)],
         [HBM] * 5,
-        [VMEM] * (sides + 4),
+        [VMEM] * (sides + 1),
         [
+            pltpu.VMEM((3, 2, height, SIDE, size), F32),
             pltpu.VMEM(target_rgb.shape, F32),
             pltpu.VMEM(hole_mask.shape, jnp.int32),
             pltpu.VMEM((size, breadth), F32),
             pltpu.VMEM(block, F32),
-            dma((5,)),
+            dma((4, 2)),
         ],
         (10**6, 10**6),
         "pack_columns",
-    )(*map(in_hbm, (latent, moment_one, moment_two, target_rgb, hole_mask)))
+    )(*given, in_hbm(target_rgb), in_hbm(hole_mask))
     columns = [swap(piece, "col", side) for side, piece in enumerate(columns)]
 
     matrix = shape((12 * size, 2 * size), BF16)
-    weights = call(
+    *weights, latent, moment_one, moment_two = call(
         pack_weights,
-        [matrix] * 4 + [shape((size, size), BF16), shape((2, 8, size), F32)],
-        [VMEM] * 5,
-        [VMEM] * 6,
-        [pltpu.VMEM((size, size), F32)],
+        [matrix] * 4 + [shape((2 * size, 2 * size), BF16)] * 2 + [shape((2, 8, 2 * size), F32)]
+        + [shape(latent.shape, F32)] * 3,
+        [VMEM] * 5 + [HBM] * 3,
+        [VMEM] * 10,
+        [pltpu.VMEM((2 * size, 2 * size), F32), dma((3,))],
         (10**6, 4 * 10**6),
         "pack_weights",
-    )(kernel_one, kernel_two, rgb_weight, bias_one[None], bias_two[None])
+    )(kernel_one, kernel_two, rgb_weight, bias_one[None], bias_two[None], *given)
 
     columns, weights = lax.optimization_barrier((columns, weights))
     own, lines, near, far, spots, inside = call(
@@ -566,8 +689,8 @@
         (10**6, 4 * 10**6),
         "pack_rows",
     )(latent, turned, *columns)
-    near = swap(near, ROWS, 0)
-    far = swap(far, ROWS, 1)
+    near = swap_near(near)
+    far = swap_far(far)
 
     passed = [tall(2), lines_of(2), tall(2), tall(2)]
     near_scratch = [
@@ -585,33 +708,33 @@
         functools.partial(first_near, sides),
         passed
         + [tall(rest), short(EDGE), lines_of(rest), lines_of(rest), lines_of(rest)]
-        + [lines_of(some), lines_of(some), lines_of(height), lines_of(height)],
-        [VMEM] * (7 + sides + 6),
+        + [lines_of(some), lines_of(some), aims_of(height), aims_of(height)],
+        [VMEM] * (7 + sides + 7),
         [VMEM] * 13,
         [vmem(tall(EDGE)), vmem(lines_of(height)), vmem(lines_of(height))] + near_scratch,
         near_work,
         "first_near",
     )(own, lines, moment_one, moment_two, near, spots, inside, *columns, *weights)
     *handed, high = results
-    near_next = swap(near_next, ROWS, 0)
+    near_next = swap_near(near_next)
 
     low, far_next, z_low, m_low, v_low, aims_far, known_far = call(
         first_far,
         [tall(some), short(EDGE), lines_of(some), lines_of(some), lines_of(some)]
-        + [lines_of(4), lines_of(4)],
-        [VMEM] * (7 + 4 + 6),
+        + [aims_of(4), aims_of(4)],
+        [VMEM] * (7 + 4 + 7),
         [VMEM] * 7,
         [vmem(tall(EDGE))] + far_scratch,
         far_work,
         "first_far",
     )(own, lines, m_rest, v_rest, far, spots, inside, *handed, *weights)
-    far_next = swap(far_next, ROWS, 1)
+    far_next = swap_far(far_next)
 
     out = shape(latent.shape, F32)
     results = call(
         last_near,
         passed + [lines_of(rest)] * 3,
-        [VMEM] * (9 + 6),
+        [VMEM] * (9 + 7),
         [VMEM] * 7,
         [vmem(tall(EDGE))] + near_scratch,
         near_work,
@@ -621,7 +744,7 @@
     return call(
         last_far,
         [out] * 3,
-        [VMEM] * (8 + 4 + 6 + 3),
+        [VMEM] * (8 + 4 + 7 + 3),
         [HBM] * 3,
         [vmem(lines_of(some))] * 3 + [vmem(tall(EDGE))] + far_scratch + [dma((3, height))],
         far_work,

time: 27.9 us -> 22.5 us (0.81)
  the two profiles are of different devices: /device:TPU:1 before, /device:TPU:0 now
where the time goes in v4:
time: 22.5 us; the launch traced here: 22.3 us
  Pallas kernels  13.3 us (59%)
  starting transfers between devices  7.39 us (33%)
  between operations  0.73 us (3%)
  local copies, waits for them, and re-layouts  0.67 us (3%)
  waiting for transfers between devices  0.28 us (1%)
    ppermute x2, starting transfers between devices, swap_far(): return lax.ppermute(block, ('row', 'col', 'cores'), sorted(chosen))  4.02 us
    ppermute x3, starting transfers between devices, swap(): return lax.ppermute(block, axes, pairs(lax.axis_size(axes), parity))  3.37 us
    pallas_call x1, Pallas kernels, body(): call(functools.partial(first_near, sides), passed + [tall(rest), short(ED...  3.19 us
    pallas_call x1, Pallas kernels, body(): call(last_near, passed + [lines_of(rest)] * 3, [VMEM] * (9 + 7), [VMEM] *...  3.05 us
    pallas_call x1, Pallas kernels, body(): call(last_far, [out] * 3, [VMEM] * (8 + 4 + 7 + 3), [HBM] * 3, [vmem(line...  2.68 us
    pallas_call x1, Pallas kernels, body(): call(first_far, [tall(some), short(EDGE), lines_of(some), lines_of(some),...  1.74 us
    pallas_call x1, Pallas kernels, body(): call(pack_weights, [matrix] * 4 + [shape((2 * size, 2 * size), BF16)] * 2...  1.4 us
    pallas_call x1, Pallas kernels, body(): call(functools.partial(pack_columns, sides), [shape(block, BF16)] * sides...  1.04 us
  transfers between devices with their start and end apart: 5, of which 2 were waited for; matrix products, arithmetic and copies ran while one was open for 0% of the time, Pallas kernels for 42%

profile of v4, /device:TPU:0, one launch (start us, length us, event | category | flops | bytes accessed | tf_op | source)
XLA Modules:
  0.0 22.3 jit_solution(5055689515297246489)
XLA Ops:
  0.6 0.0 copy-start.1
  0.6 0.0 copy-start
  0.7 0.0 copy-start.4
  0.7 1.0 %pack_columns.1 = (bf16[22,8,128]{2,1,0:T(8,128)(2,1)S(1)}, bf16[128,128]{1,0:T(8,128)(2,1)S(1)}) custom-call(f32[8,128,128]{2,1,0:T(8,128)} %latent.1, f32[8,128,128]{2,1,0:T(8,128)} %first.1, f32[8,128,128]{2,1,0:T(8,128)} %second.1, f32[3,8,128]{2,1,0:T(8,128)} %target.1, s32[8,128]{1,0:T(8,128)} %mask.1), custom_call_target="tpu_custom_call" | custom-call | flops 1000000 | bytes 1000000 | tf_op jit(solution)/shard_map/pack_columns/pallas_call | solution.py:650
  1.7 3.0 %collective-permute-start = (bf16[22,8,128]{2,1,0:T(8,128)(2,1)S(1)}, bf16[22,8,128]{2,1,0:T(8,128)(2,1)S(1)}, u32[]{:S(2)}, u32[]{:S(2)}) collective-permute-start(bf16[22,8,128]{2,1,0:T(8,128)(2,1)S(1)} %get-tuple-element.58), channel_id=1, source_target_pairs={{0,2},{2,0},{1,3},{3,1},{4,6},{6,4},{5,7},{7,5},{8,10},{10,8},{9,1... | collective-permute-start | bytes 135176 | tf_op jit(solution)/shard_map/ppermute | solution.py:42
  4.7 0.0 copy-start.2
  4.7 0.0 copy-start.3
  4.7 0.0 copy-done.1
  4.8 0.0 copy-done
  4.8 0.0 copy-done.4
  4.8 0.7 %copy-done.2 = bf16[3,128]{1,0:T(4,128)(2,1)S(1)} copy-done((bf16[3,128]{1,0:T(4,128)(2,1)S(1)}, bf16[3,128]{1,0:T(4,128)(2,1)}, u32[]{:S(2)}) %copy-start.2) | copy-done | bytes 792
  5.4 0.0 copy-done.3
  5.4 1.4 %pack_weights.1 = (bf16[1536,256]{1,0:T(8,128)(2,1)S(1)}, bf16[1536,256]{1,0:T(8,128)(2,1)S(1)}, bf16[1536,256]{1,0:T(8,128)(2,1)S(1)}, bf16[1536,256]{1,0:T(8,1...) custom-call(bf16[3,3,128,128]{3,2,1,0:T(8,128)(2,1)S(1)} %copy-done,, ...), custom_call_target="tpu_custom_call" | custom-call | flops 1000000 | bytes 4000000 | tf_op jit(solution)/shard_map/pack_weights/pallas_call | solution.py:670
  6.8 0.0 collective-permute-done.rest_0_.refs_0_
  6.8 0.2 pack_rows.1
  7.0 0.1 collective-permute-start.1
  7.1 2.0 %collective-permute-start.2 = (bf16[5,9,16,128]{3,2,1,0:T(8,128)(2,1)S(1)}, bf16[5,9,16,128]{3,2,1,0:T(8,128)(2,1)S(1)}, u32[]{:S(2)}, u32[]{:S(2)}) collective-permute-start(bf16[5,9,16,128]{3,2,1,0:T(8,128)(2,1)S(1)} %get-tuple-element.83), channel_id=1, source_target_pairs={{0,2},{1,4},{2,0},{3,6},{4,1},{5,8},{6,3},{7,10},{8,5},{9,12},{10,... | collective-permute-start | bytes 552968 | tf_op jit(solution)/shard_map/ppermute | solution.py:61
  9.1 0.0 collective-permute-done.1.near
  9.1 3.2 %first_near.1 = (bf16[2,11,16,128]{3,2,1,0:T(8,128)(2,1)S(1)}, f32[2,144,128]{2,1,0:T(8,128)S(1)}, bf16[2,11,16,128]{3,2,1,0:T(8,128)(2,1)S(1)}, bf16[2,11,16,12...) custom-call(bf16[8,11,16,128]{3,2,1,0:T(8,128)(2,1)S(1)} %get-tuple-, ...), custom_call_target="tpu_custom_call" | custom-call | flops 1585446912 | bytes 10000000 | tf_op jit(solution)/shard_map/first_near/pallas_call | solution.py:707
  12.3 0.3 %collective-permute-start.4 = (bf16[4,9,16,128]{3,2,1,0:T(8,128)(2,1)S(1)}, bf16[4,9,16,128]{3,2,1,0:T(8,128)(2,1)S(1)}, u32[]{:S(2)}, u32[]{:S(2)}) collective-permute-start(bf16[4,9,16,128]{3,2,1,0:T(8,128)(2,1)S(1)} %get-tuple-element.96), channel_id=1, source_target_pairs={{0,1},{1,0},{4,5},{5,4},{8,9},{9,8},{12,13},{13,12},{2,3},{3,2},{6... | collective-permute-start | bytes 442376 | tf_op jit(solution)/shard_map/ppermute | solution.py:42
  12.5 0.1 collective-permute-done.2.far
  12.7 1.7 %first_far.1 = (bf16[4,11,16,128]{3,2,1,0:T(8,128)(2,1)S(1)}, bf16[4,9,16,128]{3,2,1,0:T(8,128)(2,1)S(1)}, f32[4,144,128]{2,1,0:T(8,128)S(1)}, f32[4,144,128]{2,...) custom-call(bf16[8,11,16,128]{3,2,1,0:T(8,128)(2,1)S(1)} %get-tuple-element.67., ...), custom_call_target="tpu_custom_call" | custom-call | flops 905969664 | bytes 10000000 | tf_op jit(solution)/shard_map/first_far/pallas_call | solution.py:721
  14.4 2.0 %collective-permute-start.3 = (bf16[4,9,16,128]{3,2,1,0:T(8,128)(2,1)S(1)}, bf16[4,9,16,128]{3,2,1,0:T(8,128)(2,1)S(1)}, u32[]{:S(2)}, u32[]{:S(2)}) collective-permute-start(bf16[4,9,16,128]{3,2,1,0:T(8,128)(2,1)S(1)} %get-tuple-element.89), channel_id=1, source_target_pairs={{0,2},{1,4},{2,0},{3,6},{4,1},{5,8},{6,3},{7,10},{8,5},{9,12},{10,... | collective-permute-start | bytes 442376 | tf_op jit(solution)/shard_map/ppermute | solution.py:61
  16.4 0.0 collective-permute-done.4.near
  16.4 3.0 %last_near.1 = (bf16[2,11,16,128]{3,2,1,0:T(8,128)(2,1)S(1)}, f32[2,144,128]{2,1,0:T(8,128)S(1)}, bf16[2,11,16,128]{3,2,1,0:T(8,128)(2,1)S(1)}, bf16[2,11,16,128...) custom-call(bf16[4,11,16,128]{3,2,1,0:T(8,128)(2,1)S(1)} %get-tuple-, ...), custom_call_target="tpu_custom_call" | custom-call | flops 1585446912 | bytes 10000000 | tf_op jit(solution)/shard_map/last_near/pallas_call | solution.py:734
  19.5 0.1 collective-permute-done.3.far
  19.6 2.7 %last_far.1 = (f32[8,128,128]{2,1,0:T(8,128)}, f32[8,128,128]{2,1,0:T(8,128)}, f32[8,128,128]{2,1,0:T(8,128)}) custom-call(bf16[4,11,16,128]{3,2,1,0:T(8,128)(2,1)S(1)} %get-tuple-element.88.low, bf16[4,9,16,128]{3,2,1,0:T(8,128)(2,1)S(1)} %collective-permute-done.3.far, f32[4,144,128]{2,1,0:T(8,128)S(1)} %get-tuple-element.90.z_in, ...), custom_call_target="tpu_custom_call" | custom-call | flops 905969664 | bytes 10000000 | tf_op jit(solution)/shard_map/last_far/pallas_call | solution.py:744
Async XLA Ops:
  0.6 4.1 %copy-start.1 = (bf16[3,3,128,128]{3,2,1,0:T(8,128)(2,1)S(1)}, bf16[3,3,128,128]{3,2,1,0:T(8,128)(2,1)}, u32[]{:S(2)}) copy-start(bf16[3,3,128,128]{3,2,1,0:T(8,128)(2,1)} %two.1) | copy-start | bytes 884740
  0.6 4.1 %copy-start = (bf16[3,3,128,128]{3,2,1,0:T(8,128)(2,1)S(1)}, bf16[3,3,128,128]{3,2,1,0:T(8,128)(2,1)}, u32[]{:S(2)}) copy-start(bf16[3,3,128,128]{3,2,1,0:T(8,128)(2,1)} %one.1) | copy-start | bytes 884740
  0.7 4.1 %copy-start.4 = (f32[128]{0:T(128)S(1)}, f32[128]{0:T(128)}, u32[]{:S(2)}) copy-start(f32[128]{0:T(128)} %param.18) | copy-start | bytes 1540
  1.7 5.1 %collective-permute-start = (bf16[22,8,128]{2,1,0:T(8,128)(2,1)S(1)}, bf16[22,8,128]{2,1,0:T(8,128)(2,1)S(1)}, u32[]{:S(2)}, u32[]{:S(2)}) collective-permute-start(bf16[22,8,128]{2,1,0:T(8,128)(2,1)S(1)} %get-tuple-element.58), channel_id=1, source_target_pairs={{0,2},{2,0},{1,3},{3,1},{4,6},{6,4},{5,7},{7,5},{8,10},{10,8},{9,1... | collective-permute-start | bytes 135176 | tf_op jit(solution)/shard_map/ppermute | solution.py:42
  4.7 0.7 %copy-start.2 = (bf16[3,128]{1,0:T(4,128)(2,1)S(1)}, bf16[3,128]{1,0:T(4,128)(2,1)}, u32[]{:S(2)}) copy-start(bf16[3,128]{1,0:T(4,128)(2,1)} %rgb.1) | copy-start | bytes 2308
  4.7 0.7 %copy-start.3 = (f32[128]{0:T(128)S(1)}, f32[128]{0:T(128)}, u32[]{:S(2)}) copy-start(f32[128]{0:T(128)} %param.16) | copy-start | bytes 1540
  7.0 2.1 %collective-permute-start.1 = (bf16[5,9,16,128]{3,2,1,0:T(8,128)(2,1)S(1)}, bf16[5,9,16,128]{3,2,1,0:T(8,128)(2,1)S(1)}, u32[]{:S(2)}, u32[]{:S(2)}) collective-permute-start(bf16[5,9,16,128]{3,2,1,0:T(8,128)(2,1)S(1)} %get-tuple-element.71), channel_id=1, source_target_pairs={{0,1},{1,0},{4,5},{5,4},{8,9},{9,8},{12,13},{13,12},{2,3},{3,2},{6... | collective-permute-start | bytes 552968 | tf_op jit(solution)/shard_map/ppermute | solution.py:42
  7.1 5.6 %collective-permute-start.2 = (bf16[5,9,16,128]{3,2,1,0:T(8,128)(2,1)S(1)}, bf16[5,9,16,128]{3,2,1,0:T(8,128)(2,1)S(1)}, u32[]{:S(2)}, u32[]{:S(2)}) collective-permute-start(bf16[5,9,16,128]{3,2,1,0:T(8,128)(2,1)S(1)} %get-tuple-element.83), channel_id=1, source_target_pairs={{0,2},{1,4},{2,0},{3,6},{4,1},{5,8},{6,3},{7,10},{8,5},{9,12},{10,... | collective-permute-start | bytes 552968 | tf_op jit(solution)/shard_map/ppermute | solution.py:61
  12.3 4.2 %collective-permute-start.4 = (bf16[4,9,16,128]{3,2,1,0:T(8,128)(2,1)S(1)}, bf16[4,9,16,128]{3,2,1,0:T(8,128)(2,1)S(1)}, u32[]{:S(2)}, u32[]{:S(2)}) collective-permute-start(bf16[4,9,16,128]{3,2,1,0:T(8,128)(2,1)S(1)} %get-tuple-element.96), channel_id=1, source_target_pairs={{0,1},{1,0},{4,5},{5,4},{8,9},{9,8},{12,13},{13,12},{2,3},{3,2},{6... | collective-permute-start | bytes 442376 | tf_op jit(solution)/shard_map/ppermute | solution.py:42
  14.4 5.2 %collective-permute-start.3 = (bf16[4,9,16,128]{3,2,1,0:T(8,128)(2,1)S(1)}, bf16[4,9,16,128]{3,2,1,0:T(8,128)(2,1)S(1)}, u32[]{:S(2)}, u32[]{:S(2)}) collective-permute-start(bf16[4,9,16,128]{3,2,1,0:T(8,128)(2,1)S(1)} %get-tuple-element.89), channel_id=1, source_target_pairs={{0,2},{1,4},{2,0},{3,6},{4,1},{5,8},{6,3},{7,10},{8,5},{9,12},{10,... | collective-permute-start | bytes 442376 | tf_op jit(solution)/shard_map/ppermute | solution.py:61

commit v5 on v4

--- a/solution.py
+++ b/solution.py
@@ -153,12 +153,17 @@
 
 
 def pack_weights(one, two, rgb, bias_one, bias_two, *refs):
-    given, loaded, refs = refs[:3], refs[10:13], refs[3:10] + refs[13:]
-    ahead_one, ahead_two, back_one, back_two, colors, spread, bias, held, sem = refs
+    given, refs = refs[:1], refs[1:]
+    matrices, loaded, refs = refs[:7], refs[7 : 7 + 1], refs[7 + 1 :]
+    ahead_one, ahead_two, back_one, back_two, colors, spread, bias = matrices
+    held, *small, sem = refs
     copies = [
         pltpu.make_async_copy(source, dest, sem.at[number])
-        for number, (source, dest) in enumerate(zip(given, loaded))
+        for number, (source, dest) in enumerate(
+            zip((rgb, bias_one, bias_two, *given), (*small, *loaded))
+        )
     ]
+    rgb, bias_one, bias_two = small
     for copy in copies:
         copy.start()
     size = one.shape[2]
@@ -181,6 +186,8 @@
                     ahead[at : at + size, out * size : (out + 1) * size] = front
                     back[at : at + size, out * size : (out + 1) * size] = rear
     held[...] = jnp.zeros_like(held)
+    for copy in copies[:3]:
+        copy.wait()
     for at in (0, size):
         held[at : at + 3, at : at + size] = rgb[...].astype(F32)
         held[at + 3 : at + 6, at : at + size] = rgb[...].astype(F32)
@@ -189,7 +196,7 @@
     for number, given in enumerate((bias_one, bias_two)):
         for at in (0, size):
             bias[number, :, at : at + size] = jnp.broadcast_to(0.5 * given[...], (8, size))
-    for copy in copies:
+    for copy in copies[3:]:
         copy.wait()
 
 
@@ -303,35 +310,38 @@
     return [functools.partial(aim, row, *spot) for row, spot in enumerate(spots)]
 
 
-def conv_pair(rows, first, weights, strip):
+def conv_pairs(rows, firsts, weights, strip, count):
     taps = []
     for down in range(4):
-        source, at = rows[first + down]
         for across in range(3):
-            taps.append(source[at, across : across + strip].reshape(strip * STRIPS, -1))
-    half = weights.shape[0] // 2
+            parts = []
+            for first in firsts:
+                source, at = rows[first - 1 + down]
+                parts.append(source[at, across : across + strip].reshape(strip * STRIPS, -1))
+            taps.append(jnp.concatenate(parts, axis=0) if len(parts) > 1 else parts[0])
+    size = weights.shape[0] // count
     parts = [
         jnp.dot(
-            jnp.concatenate(taps[6 * part : 6 * part + 6], axis=1),
-            weights[half * part : half * (part + 1)],
+            jnp.concatenate(taps[len(taps) // count * part : len(taps) // count * (part + 1)], axis=1),
+            weights[size * part : size * (part + 1)],
             preferred_element_type=F32,
         )
-        for part in range(2)
+        for part in range(count)
     ]
-    return parts[0] + parts[1]
-
-
-def sigma_of(value):
-    return 0.5 * jnp.tanh(0.5 * value) + 0.5
-
-
-def gradient(order, rows, weights, aims, known, inside, emit, beside=(), parts=True):
+    total = parts[0]
+    for part in parts[1:]:
+        total = total + part
+    pixels = strip * STRIPS
+    return [total[at * pixels : (at + 1) * pixels] for at in range(len(firsts))]
+
+
+def gradient(order, rows, weights, aims, known, inside, emit, beside=(), parts=False, cuts=1):
     wide, hidden, slope, grad_two, grad_one = rows
     ahead_one, ahead_two, back_one, back_two, colors, spread, bias = weights
     pixels, size = inside.shape
     strip = pixels // STRIPS
     there = far_there()
-    low = min(first for stage, first in filter(None, order) if stage == 1)
+    low = min(min(firsts) for stage, firsts in filter(None, order) if stage == 1)
 
     def keep_of(row):
         return (inside[...] * there if row < EDGE else inside[...]).astype(BF16)
@@ -345,51 +355,56 @@
         hid = value * twice
         return hid, twice + hid * (2.0 - twice)
 
-    def ahead_first(first):
-        both = conv_pair(wide, first - 1, ahead_one, strip)
+    def ahead_first(firsts):
+        results = conv_pairs(wide, firsts, ahead_one, strip, cuts)
         yield
-        hid, twice = gate(both, 0)
-        for half in range(2):
-            row = first + half
-            put(*hidden[row], half_of(hid, half), strip, keep_of(row))
-            if row in slope:
+        for first, both in zip(firsts, results):
+            hid, twice = gate(both, 0)
+            for half in range(2):
+                row = first + half
+                put(*hidden[row], half_of(hid, half), strip, keep_of(row))
+                if row in slope:
+                    held, at = slope[row]
+                    held[at] = half_of(twice, half)
+
+    lane = lax.rem(lax.broadcasted_iota(jnp.int32, (pixels, 2 * size), 1), size)
+
+    def ahead_second(firsts):
+        results = conv_pairs(hidden, firsts, ahead_two, strip, cuts)
+        yield
+        for first, both in zip(firsts, results):
+            number = (first - low) // 2
+            hid, twice = gate(both, 1)
+            color = lax.dot_general(
+                hid.astype(BF16), colors[...], (((1,), (1,)), ((), ())), preferred_element_type=F32
+            )
+            if parts:
+                yield
+            residual = known[number] * color - aims[number]
+            rest = residual - residual.astype(BF16).astype(F32)
+            split = jnp.where(lane < 3, residual, rest).astype(BF16)
+            back = jnp.dot(split, spread[...], preferred_element_type=F32)
+            if parts:
+                yield
+            result = back * twice
+            for half in range(2):
+                put(*grad_two[first + half], half_of(result, half), strip)
+
+    def back_second(firsts):
+        results = conv_pairs(grad_two, firsts, back_two, strip, cuts)
+        yield
+        for first, both in zip(firsts, results):
+            for half in range(2):
+                row = first + half
                 held, at = slope[row]
-                held[at] = half_of(twice, half)
-
-    def ahead_second(first):
-        number = (first - low) // 2
-        both = conv_pair(hidden, first - 1, ahead_two, strip)
+                put(*grad_one[row], half_of(both, half) * held[at], strip, keep_of(row))
+
+    def back_first(firsts):
+        results = conv_pairs(grad_one, firsts, back_one, strip, cuts)
         yield
-        hid, twice = gate(both, 1)
-        color = lax.dot_general(
-            hid.astype(BF16), colors[...], (((1,), (1,)), ((), ())), preferred_element_type=F32
-        )
-        if parts:
-            yield
-        residual = known[number] * color - aims[number]
-        rest = residual - residual.astype(BF16).astype(F32)
-        lane = lax.broadcasted_iota(jnp.int32, (pixels, 2 * size), 1)
-        split = jnp.where(lax.rem(lane, size) < 3, residual, rest).astype(BF16)
-        back = jnp.dot(split, spread[...], preferred_element_type=F32)
-        if parts:
-            yield
-        result = back * twice
-        for half in range(2):
-            put(*grad_two[first + half], half_of(result, half), strip)
-
-    def back_second(first):
-        both = conv_pair(grad_two, first - 1, back_two, strip)
-        yield
-        for half in range(2):
-            row = first + half
-            held, at = slope[row]
-            put(*grad_one[row], half_of(both, half) * held[at], strip, keep_of(row))
-
-    def back_first(first):
-        both = conv_pair(grad_one, first - 1, back_one, strip)
-        yield
-        for half in range(2):
-            emit(first + half - EDGE, half_of(both, half))
+        for first, both in zip(firsts, results):
+            for half in range(2):
+                emit(first + half - EDGE, half_of(both, half))
 
     stages = (ahead_first, ahead_second, back_second, back_first)
     beside = list(beside)
@@ -411,9 +426,13 @@
 
 def adam(current, first, second, grad):
     first = BETA_ONE * first + (1.0 - BETA_ONE) * grad
-    second = BETA_TWO * second + (1.0 - BETA_TWO) * grad * grad
-    root = second * lax.rsqrt(jnp.maximum(second, 1e-30))
+    second = BETA_TWO * second + ((1.0 - BETA_TWO) * grad) * grad
+    root = second * lax.rsqrt(second)
     return current - (LEARN_RATE * first) / (root + EPSILON), first, second
+
+
+def floored(second):
+    return jnp.maximum(second, 1e-30)
 
 
 def place_rows(*parts):
@@ -424,28 +443,20 @@
     return rows
 
 
-def near_order(height):
-    firsts = [list(range(5 + n, height + 7 - n, 2)) for n in range(4)]
-    delay = (2, 4, 2)
-    done, order = {}, []
-    while any(firsts):
-        slot = len(order)
-        for stage in (3, 2, 1, 0):
-            if not firsts[stage]:
-                continue
-            first = firsts[stage][0]
-            needs = [(stage - 1, first - 1), (stage - 1, first + 1)] if stage else []
-            if all(done.get(need, slot) + delay[stage - 1] <= slot for need in needs):
-                done[stage, first] = slot
-                order.append((stage, firsts[stage].pop(0)))
-                break
-        else:
-            order.append(None)
-    return order
-
-
-def far_order():
-    return [(0, 3), (0, 1), (1, 4), (1, 2), (2, 5), (2, 3), (3, 6), (3, 4)]
+def first_near_order(height):
+    return [(0, (5, 7)), (0, (9, 11)), (0, (13,)), (1, (6, 8)), (1, (10, 12)), None, (2, (7, 9)), (2, (11,)), (3, (8,)), (3, (10,))]
+
+
+def last_near_order(height):
+    return [(0, (5, 7, 9)), (0, (11, 13)), (1, (6,)), (1, (8,)), (1, (10,)), (1, (12,)), (2, (7,)), (2, (9,)), (2, (11,)), (3, (8,)), (3, (10,))]
+
+
+def first_far_order(height):
+    return [(0, (3,)), (0, (1,)), (1, (4,)), (1, (2,)), (2, (5,)), (2, (3,)), (3, (6,)), (3, (4,))]
+
+
+def last_far_order(height):
+    return [(0, (3,)), (0, (1,)), (1, (4,)), (1, (2,)), (2, (5,)), (2, (3,)), (3, (6,)), (3, (4,))]
 
 
 def near_rows(height, own, halo, passed, scratch):
@@ -512,11 +523,11 @@
         )
     for row in range(EDGE):
         m_rest[row] = strips_of(m_held, row, strip)
-        v_rest[row] = strips_of(v_held, row, strip)
+        v_rest[row] = floored(strips_of(v_held, row, strip))
 
     def emit(row, grad):
         current, first, second = adam(
-            lines[row], strips_of(m_held, row, strip), strips_of(v_held, row, strip), grad
+            lines[row], strips_of(m_held, row, strip), floored(strips_of(v_held, row, strip)), grad
         )
         current = current * inside[...]
         at = row - EDGE
@@ -528,7 +539,7 @@
             near_out[height - 1 - row] = current.astype(BF16).reshape(near_out.shape[1:])
 
     rows = near_rows(height, place_rows((4, height + 4, own, 0)), halo, passed, scratch)
-    gradient(near_order(height), rows, weights, aims, known, inside, emit, pair_up(tasks))
+    gradient(first_near_order(height), rows, weights, aims, known, inside, emit, pair_up(tasks), False, 2)
 
 
 def first_far(own, lines, m_rest, v_rest, far, spots, inside, *refs):
@@ -557,7 +568,7 @@
         far_out[EDGE - 1 - row] = current.astype(BF16).reshape(far_out.shape[1:])
 
     rows = far_rows(place_rows((4, 8, own, 0)), halo, passed, scratch)
-    gradient(far_order(), rows, weights, aims, known, inside, emit, pair_up(tasks), False)
+    gradient(first_far_order(height), rows, weights, aims, known, inside, emit, pair_up(tasks), False, 2)
 
 
 def keep_row(held, at, value, strip):
@@ -581,7 +592,7 @@
 
     own = place_rows((4, 8, low, 0), (8, height + 4, high, 0))
     rows = near_rows(height, own, halo, passed, scratch)
-    gradient(near_order(height), rows, weights, aims, known, inside, emit)
+    gradient(last_near_order(height), rows, weights, aims, known, inside, emit, (), False, 2)
 
 
 def last_far(low, far, z_in, m_in, v_in, aims, known, inside, *refs):
@@ -613,7 +624,7 @@
             send(row, number, helds[number], row)
 
     rows = far_rows(place_rows((4, 8, low, 0)), halo, passed, scratch)
-    gradient(far_order(), rows, weights, aims, known, inside, emit, (), False)
+    gradient(last_far_order(height), rows, weights, aims, known, inside, emit, (), False, 2)
     for copy in copies:
         copy.wait()
 
@@ -667,16 +678,27 @@
     columns = [swap(piece, "col", side) for side, piece in enumerate(columns)]
 
     matrix = shape((12 * size, 2 * size), BF16)
-    *weights, latent, moment_one, moment_two = call(
+    *weights, latent = call(
         pack_weights,
         [matrix] * 4 + [shape((2 * size, 2 * size), BF16)] * 2 + [shape((2, 8, 2 * size), F32)]
-        + [shape(latent.shape, F32)] * 3,
-        [VMEM] * 5 + [HBM] * 3,
-        [VMEM] * 10,
-        [pltpu.VMEM((2 * size, 2 * size), F32), dma((3,))],
+        + [shape(latent.shape, F32)],
+        [VMEM] * 2 + [HBM] * 4,
+        [VMEM] * 8,
+        [
+            pltpu.VMEM((2 * size, 2 * size), F32),
+            pltpu.VMEM(rgb_weight.shape, BF16),
+            pltpu.VMEM((1, size), F32),
+            pltpu.VMEM((1, size), F32),
+            dma((4,)),
+        ],
         (10**6, 4 * 10**6),
         "pack_weights",
-    )(kernel_one, kernel_two, rgb_weight, bias_one[None], bias_two[None], *given)
+    )(
+        kernel_one,
+        kernel_two,
+        *map(in_hbm, (rgb_weight, bias_one[None], bias_two[None])),
+        given[0],
+    )
 
     columns, weights = lax.optimization_barrier((columns, weights))
     own, lines, near, far, spots, inside = call(

time: 22.5 us -> 22.4 us (level)
  waiting for transfers between devices: 0.28 us -> 1.17 us
  local copies, waits for them, and re-layouts: 0.67 us -> 0.02 us
  Pallas kernels: 13.3 us -> 12.8 us
    ppermute x3, waiting for transfers between devices: 0.01 us -> 0.81 us  [swap(): return lax.ppermute(block, axes, pairs(lax.axis_size(axes), parity))]
    unnamed x10 -> x8, local copies, waits for them, and re-layouts: 0.67 us -> 0.02 us
  transfers between devices with their start and end apart: 5 -> 5, of which waited for: 2 -> 3; matrix products, arithmetic and copies ran while one was open for 0% -> 0% of each run, Pallas kernels for 42% -> 40%
where the time goes in v5:
time: 22.4 us; the launch traced here: 22.3 us
  Pallas kernels  12.8 us (57%)
  starting transfers between devices  7.54 us (34%)
  waiting for transfers between devices  1.17 us (5%)
  between operations  0.71 us (3%)
    ppermute x2, starting transfers between devices, swap_far(): return lax.ppermute(block, ('row', 'col', 'cores'), sorted(chosen))  4.17 us
    ppermute x3, starting transfers between devices, swap(): return lax.ppermute(block, axes, pairs(lax.axis_size(axes), parity))  3.37 us
    pallas_call x1, Pallas kernels, body(): call(functools.partial(first_near, sides), passed + [tall(rest), short(ED...  3.11 us
    pallas_call x1, Pallas kernels, body(): call(last_near, passed + [lines_of(rest)] * 3, [VMEM] * (9 + 7), [VMEM] *...  2.88 us
    pallas_call x1, Pallas kernels, body(): call(last_far, [out] * 3, [VMEM] * (8 + 4 + 7 + 3), [HBM] * 3, [vmem(line...  2.71 us
    pallas_call x1, Pallas kernels, body(): call(first_far, [tall(some), short(EDGE), lines_of(some), lines_of(some),...  1.75 us
    pallas_call x1, Pallas kernels, body(): call(pack_weights, [matrix] * 4 + [shape((2 * size, 2 * size), BF16)] * 2...  1.19 us
    pallas_call x1, Pallas kernels, body(): call(functools.partial(pack_columns, sides), [shape(block, BF16)] * sides...  1.04 us
  transfers between devices with their start and end apart: 5, of which 3 were waited for; matrix products, arithmetic and copies ran while one was open for 0% of the time, Pallas kernels for 40%

profile of v5, /device:TPU:0, one launch (start us, length us, event | category | flops | bytes accessed | tf_op | source)
XLA Modules:
  0.0 22.3 jit_solution(8253863462792467668)
XLA Ops:
  0.6 0.0 copy-start.3
  0.6 0.0 copy-start.2
  0.7 1.0 %pack_columns.1 = (bf16[22,8,128]{2,1,0:T(8,128)(2,1)S(1)}, bf16[128,128]{1,0:T(8,128)(2,1)S(1)}) custom-call(f32[8,128,128]{2,1,0:T(8,128)} %latent.1, f32[8,128,128]{2,1,0:T(8,128)} %moment_one.1, f32[8,128,128]{2,1,0:T(8,128)} %moment_two.1, f32[3,8,128]{2,1,0:T(8,128)} %target.1, s32[8,128]{1,0:T(8,128)} %mask.1), custom_call_target="tpu_custom_call" | custom-call | flops 1000000 | bytes 1000000 | tf_op jit(solution)/shard_map/pack_columns/pallas_call | solution.py:661
  1.7 3.0 %collective-permute-start = (bf16[22,8,128]{2,1,0:T(8,128)(2,1)S(1)}, bf16[22,8,128]{2,1,0:T(8,128)(2,1)S(1)}, u32[]{:S(2)}, u32[]{:S(2)}) collective-permute-start(bf16[22,8,128]{2,1,0:T(8,128)(2,1)S(1)} %get-tuple-element.56), channel_id=1, source_target_pairs={{0,2},{2,0},{1,3},{3,1},{4,6},{6,4},{5,7},{7,5},{8,10},{10,8},{9,1... | collective-permute-start | bytes 135176 | tf_op jit(solution)/shard_map/ppermute | solution.py:42
  4.7 0.0 copy-done.3
  4.7 0.0 copy-done.2
  4.7 0.0 copy-start.1
  4.7 1.2 %pack_weights.1 = (bf16[1536,256]{1,0:T(8,128)(2,1)S(1)}, bf16[1536,256]{1,0:T(8,128)(2,1)S(1)}, bf16[1536,256]{1,0:T(8,128)(2,1)S(1)}, bf16[1536,256]{1,0:T(8,1...) custom-call(bf16[3,3,128,128]{3,2,1,0:T(8,128)(2,1)S(1)} %copy-done., ...), custom_call_target="tpu_custom_call" | custom-call | flops 1000000 | bytes 4000000 | tf_op jit(solution)/shard_map/pack_weights/pallas_call | solution.py:681
  5.9 0.0 copy-start
  6.0 0.8 %collective-permute-done.rest_0_.refs_0_ = bf16[22,8,128]{2,1,0:T(8,128)(2,1)S(1)} collective-permute-done((bf16[22,8,128]{2,1,0:T(8,128)(2,1)S(1)}, bf16[22,8,128]{2,1,0:T(8,128)(2,1)S(1)}, u32[]{:S(2)}, u32[]{:S(2)}) %collective-permute-start) | collective-permute-done | bytes 45088 | tf_op jit(solution)/shard_map/ppermute | solution.py:42
  6.8 0.1 pack_rows.1
  6.9 0.1 collective-permute-start.1
  7.0 2.1 %collective-permute-start.2 = (bf16[5,9,16,128]{3,2,1,0:T(8,128)(2,1)S(1)}, bf16[5,9,16,128]{3,2,1,0:T(8,128)(2,1)S(1)}, u32[]{:S(2)}, u32[]{:S(2)}) collective-permute-start(bf16[5,9,16,128]{3,2,1,0:T(8,128)(2,1)S(1)} %get-tuple-element.79), channel_id=1, source_target_pairs={{0,2},{1,4},{2,0},{3,6},{4,1},{5,8},{6,3},{7,10},{8,5},{9,12},{10,... | collective-permute-start | bytes 552968 | tf_op jit(solution)/shard_map/ppermute | solution.py:61
  9.1 0.0 collective-permute-done.1.near
  9.1 0.0 copy-done.1
  9.1 0.0 copy-done
  9.1 3.1 %first_near.1 = (bf16[2,11,16,128]{3,2,1,0:T(8,128)(2,1)S(1)}, f32[2,144,128]{2,1,0:T(8,128)S(1)}, bf16[2,11,16,128]{3,2,1,0:T(8,128)(2,1)S(1)}, bf16[2,11,16,12...) custom-call(bf16[8,11,16,128]{3,2,1,0:T(8,128)(2,1)S(1)} %get-tuple-, ...), custom_call_target="tpu_custom_call" | custom-call | flops 1585446912 | bytes 10000000 | tf_op jit(solution)/shard_map/first_near/pallas_call | solution.py:729
  12.2 0.3 %collective-permute-start.4 = (bf16[4,9,16,128]{3,2,1,0:T(8,128)(2,1)S(1)}, bf16[4,9,16,128]{3,2,1,0:T(8,128)(2,1)S(1)}, u32[]{:S(2)}, u32[]{:S(2)}) collective-permute-start(bf16[4,9,16,128]{3,2,1,0:T(8,128)(2,1)S(1)} %get-tuple-element.92), channel_id=1, source_target_pairs={{0,1},{1,0},{4,5},{5,4},{8,9},{9,8},{12,13},{13,12},{2,3},{3,2},{6... | collective-permute-start | bytes 442376 | tf_op jit(solution)/shard_map/ppermute | solution.py:42
  12.5 0.1 collective-permute-done.2.far
  12.6 1.7 %first_far.1 = (bf16[4,11,16,128]{3,2,1,0:T(8,128)(2,1)S(1)}, bf16[4,9,16,128]{3,2,1,0:T(8,128)(2,1)S(1)}, f32[4,144,128]{2,1,0:T(8,128)S(1)}, f32[4,144,128]{2,...) custom-call(bf16[8,11,16,128]{3,2,1,0:T(8,128)(2,1)S(1)} %get-tuple-element.65., ...), custom_call_target="tpu_custom_call" | custom-call | flops 905969664 | bytes 10000000 | tf_op jit(solution)/shard_map/first_far/pallas_call | solution.py:743
  14.3 2.1 %collective-permute-start.3 = (bf16[4,9,16,128]{3,2,1,0:T(8,128)(2,1)S(1)}, bf16[4,9,16,128]{3,2,1,0:T(8,128)(2,1)S(1)}, u32[]{:S(2)}, u32[]{:S(2)}) collective-permute-start(bf16[4,9,16,128]{3,2,1,0:T(8,128)(2,1)S(1)} %get-tuple-element.85), channel_id=1, source_target_pairs={{0,2},{1,4},{2,0},{3,6},{4,1},{5,8},{6,3},{7,10},{8,5},{9,12},{10,... | collective-permute-start | bytes 442376 | tf_op jit(solution)/shard_map/ppermute | solution.py:61
  16.4 0.0 collective-permute-done.4.near
  16.4 2.9 %last_near.1 = (bf16[2,11,16,128]{3,2,1,0:T(8,128)(2,1)S(1)}, f32[2,144,128]{2,1,0:T(8,128)S(1)}, bf16[2,11,16,128]{3,2,1,0:T(8,128)(2,1)S(1)}, bf16[2,11,16,128...) custom-call(bf16[4,11,16,128]{3,2,1,0:T(8,128)(2,1)S(1)} %get-tuple-, ...), custom_call_target="tpu_custom_call" | custom-call | flops 1585446912 | bytes 10000000 | tf_op jit(solution)/shard_map/last_near/pallas_call | solution.py:756
  19.3 0.2 %collective-permute-done.3.far = bf16[4,9,16,128]{3,2,1,0:T(8,128)(2,1)S(1)} collective-permute-done((bf16[4,9,16,128]{3,2,1,0:T(8,128)(2,1)S(1)}, bf16[4,9,16,128]{3,2,1,0:T(8,128)(2,1)S(1)}, u32[]{:S(2)}, u32[]{:S(2)}) %collective-permute-start.3) | collective-permute-done | bytes 147488 | tf_op jit(solution)/shard_map/ppermute | solution.py:61
  19.6 2.7 %last_far.1 = (f32[8,128,128]{2,1,0:T(8,128)}, f32[8,128,128]{2,1,0:T(8,128)}, f32[8,128,128]{2,1,0:T(8,128)}) custom-call(bf16[4,11,16,128]{3,2,1,0:T(8,128)(2,1)S(1)} %get-tuple-element.84.low, bf16[4,9,16,128]{3,2,1,0:T(8,128)(2,1)S(1)} %collective-permute-done.3.far, f32[4,144,128]{2,1,0:T(8,128)S(1)} %get-tuple-element.86.z_in, ...), custom_call_target="tpu_custom_call" | custom-call | flops 905969664 | bytes 10000000 | tf_op jit(solution)/shard_map/last_far/pallas_call | solution.py:766
Async XLA Ops:
  0.6 4.1 %copy-start.3 = (bf16[3,3,128,128]{3,2,1,0:T(8,128)(2,1)S(1)}, bf16[3,3,128,128]{3,2,1,0:T(8,128)(2,1)}, u32[]{:S(2)}) copy-start(bf16[3,3,128,128]{3,2,1,0:T(8,128)(2,1)} %two.1) | copy-start | bytes 884740
  0.6 4.1 %copy-start.2 = (bf16[3,3,128,128]{3,2,1,0:T(8,128)(2,1)S(1)}, bf16[3,3,128,128]{3,2,1,0:T(8,128)(2,1)}, u32[]{:S(2)}) copy-start(bf16[3,3,128,128]{3,2,1,0:T(8,128)(2,1)} %one.1) | copy-start | bytes 884740
  1.7 5.1 %collective-permute-start = (bf16[22,8,128]{2,1,0:T(8,128)(2,1)S(1)}, bf16[22,8,128]{2,1,0:T(8,128)(2,1)S(1)}, u32[]{:S(2)}, u32[]{:S(2)}) collective-permute-start(bf16[22,8,128]{2,1,0:T(8,128)(2,1)S(1)} %get-tuple-element.56), channel_id=1, source_target_pairs={{0,2},{2,0},{1,3},{3,1},{4,6},{6,4},{5,7},{7,5},{8,10},{10,8},{9,1... | collective-permute-start | bytes 135176 | tf_op jit(solution)/shard_map/ppermute | solution.py:42
  4.7 4.3 %copy-start.1 = (f32[8,128,128]{2,1,0:T(8,128)S(1)}, f32[8,128,128]{2,1,0:T(8,128)}, u32[]{:S(2)}) copy-start(f32[8,128,128]{2,1,0:T(8,128)} %moment_two.1) | copy-start | bytes 1572868
  5.9 3.1 %copy-start = (f32[8,128,128]{2,1,0:T(8,128)S(1)}, f32[8,128,128]{2,1,0:T(8,128)}, u32[]{:S(2)}) copy-start(f32[8,128,128]{2,1,0:T(8,128)} %moment_one.1) | copy-start | bytes 1572868
  6.9 2.2 %collective-permute-start.1 = (bf16[5,9,16,128]{3,2,1,0:T(8,128)(2,1)S(1)}, bf16[5,9,16,128]{3,2,1,0:T(8,128)(2,1)S(1)}, u32[]{:S(2)}, u32[]{:S(2)}) collective-permute-start(bf16[5,9,16,128]{3,2,1,0:T(8,128)(2,1)S(1)} %get-tuple-element.67), channel_id=1, source_target_pairs={{0,1},{1,0},{4,5},{5,4},{8,9},{9,8},{12,13},{13,12},{2,3},{3,2},{6... | collective-permute-start | bytes 552968 | tf_op jit(solution)/shard_map/ppermute | solution.py:42
  7.0 5.6 %collective-permute-start.2 = (bf16[5,9,16,128]{3,2,1,0:T(8,128)(2,1)S(1)}, bf16[5,9,16,128]{3,2,1,0:T(8,128)(2,1)S(1)}, u32[]{:S(2)}, u32[]{:S(2)}) collective-permute-start(bf16[5,9,16,128]{3,2,1,0:T(8,128)(2,1)S(1)} %get-tuple-element.79), channel_id=1, source_target_pairs={{0,2},{1,4},{2,0},{3,6},{4,1},{5,8},{6,3},{7,10},{8,5},{9,12},{10,... | collective-permute-start | bytes 552968 | tf_op jit(solution)/shard_map/ppermute | solution.py:61
  12.2 4.2 %collective-permute-start.4 = (bf16[4,9,16,128]{3,2,1,0:T(8,128)(2,1)S(1)}, bf16[4,9,16,128]{3,2,1,0:T(8,128)(2,1)S(1)}, u32[]{:S(2)}, u32[]{:S(2)}) collective-permute-start(bf16[4,9,16,128]{3,2,1,0:T(8,128)(2,1)S(1)} %get-tuple-element.92), channel_id=1, source_target_pairs={{0,1},{1,0},{4,5},{5,4},{8,9},{9,8},{12,13},{13,12},{2,3},{3,2},{6... | collective-permute-start | bytes 442376 | tf_op jit(solution)/shard_map/ppermute | solution.py:42
  14.3 5.2 %collective-permute-start.3 = (bf16[4,9,16,128]{3,2,1,0:T(8,128)(2,1)S(1)}, bf16[4,9,16,128]{3,2,1,0:T(8,128)(2,1)S(1)}, u32[]{:S(2)}, u32[]{:S(2)}) collective-permute-start(bf16[4,9,16,128]{3,2,1,0:T(8,128)(2,1)S(1)} %get-tuple-element.85), channel_id=1, source_target_pairs={{0,2},{1,4},{2,0},{3,6},{4,1},{5,8},{6,3},{7,10},{8,5},{9,12},{10,... | collective-permute-start | bytes 442376 | tf_op jit(solution)/shard_map/ppermute | solution.py:61

commit v6 on v5

--- a/solution.py
+++ b/solution.py
@@ -105,7 +105,7 @@
 
 def pack_columns(sides, latent, first, second, target, mask, *rest):
     outs, rest = rest[:sides], rest[sides:]
-    turned, ends, aim, known, planes, flat, sem = rest
+    turned, close, away, ends, aim, known, planes, flat, sem = rest
     height, breadth = latent.shape[0], latent.shape[1]
     early = [
         pltpu.make_async_copy(target, aim, sem.at[3, 0]),
@@ -132,6 +132,11 @@
     planes[pl.ds(6, height, stride=PLANES), :] = keep
     swapped = planes[...].T
     turned[...] = swapped.astype(BF16)
+    odd = lax.rem(row_place(), 2) == 1
+    start = (height - 2) * PLANES
+    low, high = planes[:STRIPS], planes[start : start + STRIPS]
+    close[...] = jnp.where(odd, low, high).astype(BF16)
+    away[...] = jnp.where(odd, high, low).astype(BF16)
     for copy in copies:
         copy.wait()
     col_even = lax.rem(lax.axis_index("col"), 2) == 0
@@ -144,8 +149,7 @@
             source = pick_row(row, height)
             own = [jnp.where(right, ends[n, 1, source], ends[n, 0, source]) for n in range(3)]
             flat[row] = own[0]
-            own[0] = own[0] - own[0].astype(BF16).astype(F32)
-            for number, piece in enumerate(own):
+            for number, piece in enumerate(own[1:]):
                 near = jnp.where(right, piece[SIDE - EDGE :], piece[:EDGE])
                 at = EDGE * row
                 flat[at_low + number * step + at // SIDE, at % SIDE : at % SIDE + EDGE] = near
@@ -214,7 +218,9 @@
 
 def widen(dest, source, strip, there=None):
     for row in range(EDGE):
-        value, low, high = source[row], source[row, 0].astype(F32), source[row, strip - 1].astype(F32)
+        at = row * strip
+        value = source[at : at + strip]
+        low, high = source[at].astype(F32), source[at + strip - 1].astype(F32)
         if there is not None:
             value, low, high = value * there.astype(BF16), low * there, high * there
         dest[row, 1 : strip + 1] = value
@@ -254,7 +260,7 @@
     )
 
 
-def pack_rows(sides, latent, turned, *rest):
+def pack_rows(sides, latent, turned, close, away, *rest):
     pieces, rest = rest[:sides], rest[sides:]
     own, lines, near, far, spots, inside, held, turn = rest
     height, breadth, size = latent.shape
@@ -265,24 +271,26 @@
         sides,
         held,
         pieces,
-        lambda piece, row, right: piece[row].astype(F32) + nearest(piece, 0, height, row, right),
+        lambda piece, row, right: piece[row].astype(F32),
         height,
     )
     turn[0, SIDE : SIDE + breadth] = turned[...].astype(F32)
     fill_sides(sides, turn, pieces, lambda piece, row, right: piece[height].astype(F32), 1)
-    spot = strips_of(turn, 0, strip).astype(BF16).reshape(strip, STRIPS, size)
-    spots[...] = spot
-    near[EDGE] = spot
-    far[EDGE] = spot
+    spots[...] = strips_of(turn, 0, strip).astype(BF16).reshape(strip, STRIPS, size)
+    ends = jnp.concatenate([turn[0, :SIDE], turn[0, SIDE + breadth :]], axis=0).astype(BF16)
+    near[EDGE * strip] = close[...]
+    far[EDGE * strip] = away[...]
+    near[EDGE * strip + 1] = ends
+    far[EDGE * strip + 1] = ends
     for row in range(height):
         line = strips_of(held, row, strip)
         lines[row] = line
         put(own, row, line, strip)
         short = line.astype(BF16).reshape(strip, STRIPS, size)
         if row < EDGE:
-            far[EDGE - 1 - row] = short
+            far[(EDGE - 1 - row) * strip : (EDGE - row) * strip] = short
         if row >= height - EDGE:
-            near[height - 1 - row] = short
+            near[(height - 1 - row) * strip : (height - row) * strip] = short
     col = lax.axis_index("col")
     base = col * breadth - SIDE
     total = lax.axis_size("col") * breadth
@@ -301,6 +309,7 @@
     chosen = (aimed | masked).astype(F32).astype(BF16)
 
     def aim(row, spot, source):
+        spot = spot() if callable(spot) else spot
         value = pltpu.roll(spot, lax.rem(size - PLANES * source, size), 1)
         both = jnp.dot(value.astype(BF16), chosen, preferred_element_type=F32)
         lanes = slice(row % 2 * size, (row % 2 + 1) * size)
@@ -483,12 +492,35 @@
     )
 
 
+def once(make):
+    made = []
+
+    def get():
+        if not made:
+            made.append(make())
+        return made[0]
+
+    return get
+
+
 def pair_up(tasks):
     def both(one, two):
         one()
         two()
 
     return [functools.partial(both, *tasks[at : at + 2]) for at in range(0, len(tasks), 2)]
+
+
+def spread_spot(sent, turn, strip, first):
+    breadth = turn.shape[1] - 2 * SIDE
+    size = turn.shape[2]
+    middle = sent[EDGE * strip].astype(F32)
+    rest = jnp.zeros((size - STRIPS, breadth), F32)
+    turn[0, SIDE : SIDE + breadth] = jnp.concatenate([middle, rest], axis=0).T
+    ends = pltpu.roll(sent[EDGE * strip + 1].astype(F32), lax.rem(size - PLANES * first, size), 1)
+    turn[0, :SIDE] = ends[:SIDE]
+    turn[0, SIDE + breadth :] = ends[SIDE:]
+    return strips_of(turn, 0, strip)
 
 
 def flat_spot(spots):
@@ -500,16 +532,17 @@
     weights, refs = refs[:7], refs[7:]
     passed, refs = refs[:4], refs[4:]
     (new, near_out, z_out, m_out, v_out, m_rest, v_rest, aims, known), refs = refs[:9], refs[9:]
-    halo, m_held, v_held, *scratch = refs
+    halo, turn, m_held, v_held, *scratch = refs
     height, breadth = moment_one.shape[:2]
     strip = own.shape[1] - 2
     widen(halo, near, strip)
-    mine, theirs = flat_spot(spots), flat_spot(near.at[EDGE])
+    start = jnp.where(lax.rem(row_place(), 2) == 1, height - 2, 0)
+    mine, theirs = flat_spot(spots), once(lambda: spread_spot(near, turn, strip, start))
     tasks = aim_rows(
         aims,
         known,
         [(mine, pick_row(row, height)) for row in range(2, height)]
-        + [(theirs, pick_partner_row(row, height)) for row in (height - 1, height - 2)],
+        + [(theirs, pick_partner_row(row, height) - start) for row in (height - 1, height - 2)],
     )
     for number, (held, moment) in enumerate(((m_held, moment_one), (v_held, moment_two))):
         for row in range(height):
@@ -518,7 +551,7 @@
             sides,
             held,
             pieces,
-            lambda piece, row, right: nearest(piece, number + 1, height, row, right),
+            lambda piece, row, right: nearest(piece, number, height, row, right),
             height,
         )
     for row in range(EDGE):
@@ -536,7 +569,8 @@
         v_out[at] = second
         put(new, at, current, strip)
         if row >= height - EDGE:
-            near_out[height - 1 - row] = current.astype(BF16).reshape(near_out.shape[1:])
+            short = current.astype(BF16).reshape(strip, *near_out.shape[1:])
+            near_out[(height - 1 - row) * strip : (height - row) * strip] = short
 
     rows = near_rows(height, place_rows((4, height + 4, own, 0)), halo, passed, scratch)
     gradient(first_near_order(height), rows, weights, aims, known, inside, emit, pair_up(tasks), False, 2)
@@ -546,15 +580,17 @@
     passed, refs = refs[:4], refs[4:]
     weights, refs = refs[:7], refs[7:]
     (new, far_out, z_out, m_out, v_out, aims, known), refs = refs[:7], refs[7:]
-    halo, *scratch = refs
+    halo, turn, *scratch = refs
     height = own.shape[0]
     strip = own.shape[1] - 2
     widen(halo, far, strip, far_there())
-    mine, theirs = flat_spot(spots), flat_spot(far.at[EDGE]) * far_there()
+    start = jnp.where(lax.rem(row_place(), 2) == 1, 0, height - 2)
+    mine = flat_spot(spots)
+    theirs = once(lambda: spread_spot(far, turn, strip, start) * far_there())
     tasks = aim_rows(
         aims,
         known,
-        [(theirs, pick_partner_row(row, height)) for row in (1, 0)]
+        [(theirs, pick_partner_row(row, height) - start) for row in (1, 0)]
         + [(mine, pick_row(row, height)) for row in range(2)],
     )
 
@@ -565,10 +601,11 @@
         m_out[row] = first
         v_out[row] = second
         put(new, row, current, strip)
-        far_out[EDGE - 1 - row] = current.astype(BF16).reshape(far_out.shape[1:])
+        short = current.astype(BF16).reshape(strip, *far_out.shape[1:])
+        far_out[(EDGE - 1 - row) * strip : (EDGE - row) * strip] = short
 
     rows = far_rows(place_rows((4, 8, own, 0)), halo, passed, scratch)
-    gradient(first_far_order(height), rows, weights, aims, known, inside, emit, pair_up(tasks), False, 2)
+    gradient(first_far_order(height), rows, weights, aims, known, inside, emit, pair_up(tasks)[::-1], False, 2)
 
 
 def keep_row(held, at, value, strip):
@@ -649,21 +686,22 @@
     sides = 1 if lax.axis_size("col") == 2 else 2
     dma = pltpu.SemaphoreType.DMA
     _, at_low, step = piece_counts(height)
-    block = (at_low + 3 * step, SIDE, size)
+    block = (at_low + 2 * step, SIDE, size)
     tall = lambda rows: shape((rows, strip + 2, STRIPS, size), BF16)
-    short = lambda rows: shape((rows, strip, STRIPS, size), BF16)
+    short = lambda tiles: shape((EDGE * strip + tiles, STRIPS, size), BF16)
     lines_of = lambda rows: shape((rows, pixels, size), F32)
     aims_of = lambda rows: shape((rows // 2, pixels, 2 * size), F32)
     vmem = lambda like: pltpu.VMEM(like.shape, like.dtype)
     work = 2 * 12 * 2 * pixels * size * size
 
     given = tuple(map(in_hbm, (latent, moment_one, moment_two)))
-    *columns, turned = call(
+    *columns, turned, close, away = call(
         functools.partial(pack_columns, sides),
         [shape(block, BF16)] * sides
-        + [shape((breadth, size), BF16)],
+        + [shape((breadth, size), BF16)]
+        + [shape((STRIPS, breadth), BF16)] * 2,
         [HBM] * 5,
-        [VMEM] * (sides + 1),
+        [VMEM] * (sides + 3),
         [
             pltpu.VMEM((3, 2, height, SIDE, size), F32),
             pltpu.VMEM(target_rgb.shape, F32),
@@ -703,14 +741,14 @@
     columns, weights = lax.optimization_barrier((columns, weights))
     own, lines, near, far, spots, inside = call(
         functools.partial(pack_rows, sides),
-        [tall(height), lines_of(height), short(EDGE + 1), short(EDGE + 1)]
+        [tall(height), lines_of(height), short(2), short(2)]
         + [shape((strip, STRIPS, size), BF16), shape((pixels, size), F32)],
-        [VMEM] * (2 + sides),
+        [VMEM] * (4 + sides),
         [VMEM] * 6,
         [vmem(lines_of(height)), vmem(lines_of(1))],
         (10**6, 4 * 10**6),
         "pack_rows",
-    )(latent, turned, *columns)
+    )(latent, turned, close, away, *columns)
     near = swap_near(near)
     far = swap_far(far)
 
@@ -729,11 +767,12 @@
     *results, near_next, z_high, m_high, v_high, m_rest, v_rest, aims_near, known_near = call(
         functools.partial(first_near, sides),
         passed
-        + [tall(rest), short(EDGE), lines_of(rest), lines_of(rest), lines_of(rest)]
+        + [tall(rest), short(0), lines_of(rest), lines_of(rest), lines_of(rest)]
         + [lines_of(some), lines_of(some), aims_of(height), aims_of(height)],
         [VMEM] * (7 + sides + 7),
         [VMEM] * 13,
-        [vmem(tall(EDGE)), vmem(lines_of(height)), vmem(lines_of(height))] + near_scratch,
+        [vmem(tall(EDGE)), vmem(lines_of(1)), vmem(lines_of(height)), vmem(lines_of(height))]
+        + near_scratch,
         near_work,
         "first_near",
     )(own, lines, moment_one, moment_two, near, spots, inside, *columns, *weights)
@@ -742,11 +781,11 @@
 
     low, far_next, z_low, m_low, v_low, aims_far, known_far = call(
         first_far,
-        [tall(some), short(EDGE), lines_of(some), lines_of(some), lines_of(some)]
+        [tall(some), short(0), lines_of(some), lines_of(some), lines_of(some)]
         + [aims_of(4), aims_of(4)],
         [VMEM] * (7 + 4 + 7),
         [VMEM] * 7,
-        [vmem(tall(EDGE))] + far_scratch,
+        [vmem(tall(EDGE)), vmem(lines_of(1))] + far_scratch,
         far_work,
         "first_far",
     )(own, lines, m_rest, v_rest, far, spots, inside, *handed, *weights)

time: 22.4 us -> 22.1 us (0.987)
  transfers between devices with their start and end apart: 5 -> 5, of which waited for: 3 -> 2; matrix products, arithmetic and copies ran while one was open for 0% -> 0% of each run, Pallas kernels for 40% -> 40%
where the time goes in v6:
time: 22.1 us; the launch traced here: 21.9 us
  Pallas kernels  12.6 us (57%)
  starting transfers between devices  7.42 us (34%)
  waiting for transfers between devices  1.12 us (5%)
  between operations  0.71 us (3%)
    ppermute x2, starting transfers between devices, swap_far(): return lax.ppermute(block, ('row', 'col', 'cores'), sorted(chosen))  4.05 us
    ppermute x3, starting transfers between devices, swap(): return lax.ppermute(block, axes, pairs(lax.axis_size(axes), parity))  3.37 us
    pallas_call x1, Pallas kernels, body(): call(functools.partial(first_near, sides), passed + [tall(rest), short(0)...  3.05 us
    pallas_call x1, Pallas kernels, body(): call(last_near, passed + [lines_of(rest)] * 3, [VMEM] * (9 + 7), [VMEM] *...  2.84 us
    pallas_call x1, Pallas kernels, body(): call(last_far, [out] * 3, [VMEM] * (8 + 4 + 7 + 3), [HBM] * 3, [vmem(line...  2.68 us
    pallas_call x1, Pallas kernels, body(): call(first_far, [tall(some), short(0), lines_of(some), lines_of(some), li...  1.7 us
    pallas_call x1, Pallas kernels, body(): call(pack_weights, [matrix] * 4 + [shape((2 * size, 2 * size), BF16)] * 2...  1.19 us
    pallas_call x1, Pallas kernels, body(): call(functools.partial(pack_columns, sides), [shape(block, BF16)] * sides...  1.04 us
  transfers between devices with their start and end apart: 5, of which 2 were waited for; matrix products, arithmetic and copies ran while one was open for 0% of the time, Pallas kernels for 40%

profile of v6, /device:TPU:0, one launch (start us, length us, event | category | flops | bytes accessed | tf_op | source)
XLA Modules:
  0.0 21.9 jit_solution(245026755292710309)
XLA Ops:
  0.6 0.0 copy-start.3
  0.6 0.0 copy-start.2
  0.7 1.0 %pack_columns.1 = (bf16[18,8,128]{2,1,0:T(8,128)(2,1)S(1)}, bf16[128,128]{1,0:T(8,128)(2,1)S(1)}, bf16[16,128]{1,0:T(8,128)(2,1)S(1)}, bf16[16,128]{1,0:T(8,128)(2,1)S(1)}) custom-call(f32[8,128,128]{2,1,0:T(8,128)} %latent.1, f32[8,128,128]{2,1,0:T(8,128)} %moment_one.1, f32[8,128,128]{2,1,0:T(8,128)} %moment_two.1, f32[3,8,128]{2,1,0:T(8,128)} %target.1, ...), custom_call_target="tpu_custom_call" | custom-call | flops 1000000 | bytes 1000000 | tf_op jit(solution)/shard_map/pack_columns/pallas_call | solution.py:698
  1.7 3.0 %collective-permute-start = (bf16[18,8,128]{2,1,0:T(8,128)(2,1)S(1)}, bf16[18,8,128]{2,1,0:T(8,128)(2,1)S(1)}, u32[]{:S(2)}, u32[]{:S(2)}) collective-permute-start(bf16[18,8,128]{2,1,0:T(8,128)(2,1)S(1)} %get-tuple-element.60), channel_id=1, source_target_pairs={{0,2},{2,0},{1,3},{3,1},{4,6},{6,4},{5,7},{7,5},{8,10},{10,8},{9,1... | collective-permute-start | bytes 110600 | tf_op jit(solution)/shard_map/ppermute | solution.py:42
  4.7 0.0 copy-done.3
  4.7 0.0 copy-done.2
  4.7 0.0 copy-start.1
  4.7 1.2 %pack_weights.1 = (bf16[1536,256]{1,0:T(8,128)(2,1)S(1)}, bf16[1536,256]{1,0:T(8,128)(2,1)S(1)}, bf16[1536,256]{1,0:T(8,128)(2,1)S(1)}, bf16[1536,256]{1,0:T(8,1...) custom-call(bf16[3,3,128,128]{3,2,1,0:T(8,128)(2,1)S(1)} %copy-done., ...), custom_call_target="tpu_custom_call" | custom-call | flops 1000000 | bytes 4000000 | tf_op jit(solution)/shard_map/pack_weights/pallas_call | solution.py:719
  5.9 0.0 copy-start
  6.0 0.7 %collective-permute-done.rest_0_.refs_0_ = bf16[18,8,128]{2,1,0:T(8,128)(2,1)S(1)} collective-permute-done((bf16[18,8,128]{2,1,0:T(8,128)(2,1)S(1)}, bf16[18,8,128]{2,1,0:T(8,128)(2,1)S(1)}, u32[]{:S(2)}, u32[]{:S(2)}) %collective-permute-start) | collective-permute-done | bytes 36896 | tf_op jit(solution)/shard_map/ppermute | solution.py:42
  6.7 0.1 pack_rows.1
  6.8 0.1 collective-permute-start.1
  6.9 2.1 %collective-permute-start.2 = (bf16[38,16,128]{2,1,0:T(8,128)(2,1)S(1)}, bf16[38,16,128]{2,1,0:T(8,128)(2,1)S(1)}, u32[]{:S(2)}, u32[]{:S(2)}) collective-permute-start(bf16[38,16,128]{2,1,0:T(8,128)(2,1)S(1)} %get-tuple-element.83), channel_id=1, source_target_pairs={{0,2},{1,4},{2,0},{3,6},{4,1},{5,8},{6,3},{7,10},{8,5},{9,12},{10,... | collective-permute-start | bytes 466952 | tf_op jit(solution)/shard_map/ppermute | solution.py:61
  9.0 0.0 collective-permute-done.1.near
  9.0 0.0 copy-done.1
  9.0 0.0 copy-done
  9.0 3.0 %first_near.1 = (bf16[2,11,16,128]{3,2,1,0:T(8,128)(2,1)S(1)}, f32[2,144,128]{2,1,0:T(8,128)S(1)}, bf16[2,11,16,128]{3,2,1,0:T(8,128)(2,1)S(1)}, bf16[2,11,16,12...) custom-call(bf16[8,11,16,128]{3,2,1,0:T(8,128)(2,1)S(1)} %get-tuple-, ...), custom_call_target="tpu_custom_call" | custom-call | flops 1585446912 | bytes 10000000 | tf_op jit(solution)/shard_map/first_near/pallas_call | solution.py:767
  12.0 0.3 %collective-permute-start.4 = (bf16[36,16,128]{2,1,0:T(8,128)(2,1)S(1)}, bf16[36,16,128]{2,1,0:T(8,128)(2,1)S(1)}, u32[]{:S(2)}, u32[]{:S(2)}) collective-permute-start(bf16[36,16,128]{2,1,0:T(8,128)(2,1)S(1)} %get-tuple-element.96), channel_id=1, source_target_pairs={{0,1},{1,0},{4,5},{5,4},{8,9},{9,8},{12,13},{13,12},{2,3},{3,2},{6... | collective-permute-start | bytes 442376 | tf_op jit(solution)/shard_map/ppermute | solution.py:42
  12.3 0.0 collective-permute-done.2.far
  12.3 1.7 %first_far.1 = (bf16[4,11,16,128]{3,2,1,0:T(8,128)(2,1)S(1)}, bf16[36,16,128]{2,1,0:T(8,128)(2,1)S(1)}, f32[4,144,128]{2,1,0:T(8,128)S(1)}, f32[4,144,128]{2,1,0...) custom-call(bf16[8,11,16,128]{3,2,1,0:T(8,128)(2,1)S(1)} %get-tuple-element.69.own, ...), custom_call_target="tpu_custom_call" | custom-call | flops 905969664 | bytes 10000000 | tf_op jit(solution)/shard_map/first_far/pallas_call | solution.py:782
  14.0 2.0 %collective-permute-start.3 = (bf16[36,16,128]{2,1,0:T(8,128)(2,1)S(1)}, bf16[36,16,128]{2,1,0:T(8,128)(2,1)S(1)}, u32[]{:S(2)}, u32[]{:S(2)}) collective-permute-start(bf16[36,16,128]{2,1,0:T(8,128)(2,1)S(1)} %get-tuple-element.89), channel_id=1, source_target_pairs={{0,2},{1,4},{2,0},{3,6},{4,1},{5,8},{6,3},{7,10},{8,5},{9,12},{10,... | collective-permute-start | bytes 442376 | tf_op jit(solution)/shard_map/ppermute | solution.py:61
  16.0 0.0 collective-permute-done.4.near
  16.0 2.8 %last_near.1 = (bf16[2,11,16,128]{3,2,1,0:T(8,128)(2,1)S(1)}, f32[2,144,128]{2,1,0:T(8,128)S(1)}, bf16[2,11,16,128]{3,2,1,0:T(8,128)(2,1)S(1)}, bf16[2,11,16,128...) custom-call(bf16[4,11,16,128]{3,2,1,0:T(8,128)(2,1)S(1)} %get-tuple-, ...), custom_call_target="tpu_custom_call" | custom-call | flops 1585446912 | bytes 10000000 | tf_op jit(solution)/shard_map/last_near/pallas_call | solution.py:795
  18.8 0.4 %collective-permute-done.3.far = bf16[36,16,128]{2,1,0:T(8,128)(2,1)S(1)} collective-permute-done((bf16[36,16,128]{2,1,0:T(8,128)(2,1)S(1)}, bf16[36,16,128]{2,1,0:T(8,128)(2,1)S(1)}, u32[]{:S(2)}, u32[]{:S(2)}) %collective-permute-start.3) | collective-permute-done | bytes 147488 | tf_op jit(solution)/shard_map/ppermute | solution.py:61
  19.2 2.7 %last_far.1 = (f32[8,128,128]{2,1,0:T(8,128)}, f32[8,128,128]{2,1,0:T(8,128)}, f32[8,128,128]{2,1,0:T(8,128)}) custom-call(bf16[4,11,16,128]{3,2,1,0:T(8,128)(2,1)S(1)} %get-tuple-element.88.low, bf16[36,16,128]{2,1,0:T(8,128)(2,1)S(1)} %collective-permute-done.3.far, f32[4,144,128]{2,1,0:T(8,128)S(1)} %get-tuple-element.90.z_in, ...), custom_call_target="tpu_custom_call" | custom-call | flops 905969664 | bytes 10000000 | tf_op jit(solution)/shard_map/last_far/pallas_call | solution.py:805
Async XLA Ops:
  0.6 4.1 %copy-start.3 = (bf16[3,3,128,128]{3,2,1,0:T(8,128)(2,1)S(1)}, bf16[3,3,128,128]{3,2,1,0:T(8,128)(2,1)}, u32[]{:S(2)}) copy-start(bf16[3,3,128,128]{3,2,1,0:T(8,128)(2,1)} %two.1) | copy-start | bytes 884740
  0.6 4.1 %copy-start.2 = (bf16[3,3,128,128]{3,2,1,0:T(8,128)(2,1)S(1)}, bf16[3,3,128,128]{3,2,1,0:T(8,128)(2,1)}, u32[]{:S(2)}) copy-start(bf16[3,3,128,128]{3,2,1,0:T(8,128)(2,1)} %one.1) | copy-start | bytes 884740
  1.7 5.0 %collective-permute-start = (bf16[18,8,128]{2,1,0:T(8,128)(2,1)S(1)}, bf16[18,8,128]{2,1,0:T(8,128)(2,1)S(1)}, u32[]{:S(2)}, u32[]{:S(2)}) collective-permute-start(bf16[18,8,128]{2,1,0:T(8,128)(2,1)S(1)} %get-tuple-element.60), channel_id=1, source_target_pairs={{0,2},{2,0},{1,3},{3,1},{4,6},{6,4},{5,7},{7,5},{8,10},{10,8},{9,1... | collective-permute-start | bytes 110600 | tf_op jit(solution)/shard_map/ppermute | solution.py:42
  4.7 4.2 %copy-start.1 = (f32[8,128,128]{2,1,0:T(8,128)S(1)}, f32[8,128,128]{2,1,0:T(8,128)}, u32[]{:S(2)}) copy-start(f32[8,128,128]{2,1,0:T(8,128)} %moment_two.1) | copy-start | bytes 1572868
  5.9 3.0 %copy-start = (f32[8,128,128]{2,1,0:T(8,128)S(1)}, f32[8,128,128]{2,1,0:T(8,128)}, u32[]{:S(2)}) copy-start(f32[8,128,128]{2,1,0:T(8,128)} %moment_one.1) | copy-start | bytes 1572868
  6.8 2.2 %collective-permute-start.1 = (bf16[38,16,128]{2,1,0:T(8,128)(2,1)S(1)}, bf16[38,16,128]{2,1,0:T(8,128)(2,1)S(1)}, u32[]{:S(2)}, u32[]{:S(2)}) collective-permute-start(bf16[38,16,128]{2,1,0:T(8,128)(2,1)S(1)} %get-tuple-element.71), channel_id=1, source_target_pairs={{0,1},{1,0},{4,5},{5,4},{8,9},{9,8},{12,13},{13,12},{2,3},{3,2},{6... | collective-permute-start | bytes 466952 | tf_op jit(solution)/shard_map/ppermute | solution.py:42
  6.9 5.4 %collective-permute-start.2 = (bf16[38,16,128]{2,1,0:T(8,128)(2,1)S(1)}, bf16[38,16,128]{2,1,0:T(8,128)(2,1)S(1)}, u32[]{:S(2)}, u32[]{:S(2)}) collective-permute-start(bf16[38,16,128]{2,1,0:T(8,128)(2,1)S(1)} %get-tuple-element.83), channel_id=1, source_target_pairs={{0,2},{1,4},{2,0},{3,6},{4,1},{5,8},{6,3},{7,10},{8,5},{9,12},{10,... | collective-permute-start | bytes 466952 | tf_op jit(solution)/shard_map/ppermute | solution.py:61
  12.0 3.9 %collective-permute-start.4 = (bf16[36,16,128]{2,1,0:T(8,128)(2,1)S(1)}, bf16[36,16,128]{2,1,0:T(8,128)(2,1)S(1)}, u32[]{:S(2)}, u32[]{:S(2)}) collective-permute-start(bf16[36,16,128]{2,1,0:T(8,128)(2,1)S(1)} %get-tuple-element.96), channel_id=1, source_target_pairs={{0,1},{1,0},{4,5},{5,4},{8,9},{9,8},{12,13},{13,12},{2,3},{3,2},{6... | collective-permute-start | bytes 442376 | tf_op jit(solution)/shard_map/ppermute | solution.py:42
  14.0 5.2 %collective-permute-start.3 = (bf16[36,16,128]{2,1,0:T(8,128)(2,1)S(1)}, bf16[36,16,128]{2,1,0:T(8,128)(2,1)S(1)}, u32[]{:S(2)}, u32[]{:S(2)}) collective-permute-start(bf16[36,16,128]{2,1,0:T(8,128)(2,1)S(1)} %get-tuple-element.89), channel_id=1, source_target_pairs={{0,2},{1,4},{2,0},{3,6},{4,1},{5,8},{6,3},{7,10},{8,5},{9,12},{10,... | collective-permute-start | bytes 442376 | tf_op jit(solution)/shard_map/ppermute | solution.py:61

commit v7 on v6

--- a/solution.py
+++ b/solution.py
@@ -107,16 +107,20 @@
     outs, rest = rest[:sides], rest[sides:]
     turned, close, away, ends, aim, known, planes, flat, sem = rest
     height, breadth = latent.shape[0], latent.shape[1]
+    col_even = lax.rem(lax.axis_index("col"), 2) == 0
+    rights = (col_even, jnp.logical_not(col_even))[:sides]
     early = [
         pltpu.make_async_copy(target, aim, sem.at[3, 0]),
         pltpu.make_async_copy(mask, known, sem.at[3, 1]),
     ]
     copies = [
         pltpu.make_async_copy(
-            source.at[:, pl.ds(start, SIDE)], ends.at[number, end], sem.at[number, end]
+            source.at[:, pl.ds(pl.multiple_of(jnp.where(right, breadth - SIDE, 0), SIDE), SIDE)],
+            ends.at[number, side],
+            sem.at[number, side],
         )
         for number, source in enumerate((latent, first, second))
-        for end, start in enumerate((0, breadth - SIDE))
+        for side, right in enumerate(rights)
     ]
     for copy in early + copies:
         copy.start()
@@ -139,15 +143,13 @@
     away[...] = jnp.where(odd, high, low).astype(BF16)
     for copy in copies:
         copy.wait()
-    col_even = lax.rem(lax.axis_index("col"), 2) == 0
     _, at_low, step = piece_counts(height)
-    for side, out in enumerate(outs):
-        right = col_even if side == 0 else jnp.logical_not(col_even)
+    for side, (out, right) in enumerate(zip(outs, rights)):
         flat[height] = jnp.where(right, swapped[breadth - SIDE :], swapped[:SIDE])
         flat[height + 1] = jnp.zeros(flat.shape[1:], F32)
         for row in range(height):
             source = pick_row(row, height)
-            own = [jnp.where(right, ends[n, 1, source], ends[n, 0, source]) for n in range(3)]
+            own = [ends[n, side, source] for n in range(3)]
             flat[row] = own[0]
             for number, piece in enumerate(own[1:]):
                 near = jnp.where(right, piece[SIDE - EDGE :], piece[:EDGE])
@@ -703,7 +705,7 @@
         [HBM] * 5,
         [VMEM] * (sides + 3),
         [
-            pltpu.VMEM((3, 2, height, SIDE, size), F32),
+            pltpu.VMEM((3, sides, height, SIDE, size), F32),
             pltpu.VMEM(target_rgb.shape, F32),
             pltpu.VMEM(hole_mask.shape, jnp.int32),
             pltpu.VMEM((size, breadth), F32),

time: 22.1 us -> 22 us (level)
  no operation moved by 1% of the time
where the time goes in v7:
time: 22 us; the launch traced here: 21.8 us
  Pallas kernels  12.6 us (57%)
  starting transfers between devices  7.42 us (34%)
  waiting for transfers between devices  1.12 us (5%)
  between operations  0.71 us (3%)
    ppermute x2, starting transfers between devices, swap_far(): return lax.ppermute(block, ('row', 'col', 'cores'), sorted(chosen))  4.05 us
    ppermute x3, starting transfers between devices, swap(): return lax.ppermute(block, axes, pairs(lax.axis_size(axes), parity))  3.37 us
    pallas_call x1, Pallas kernels, body(): call(functools.partial(first_near, sides), passed + [tall(rest), short(0)...  3.04 us
    pallas_call x1, Pallas kernels, body(): call(last_near, passed + [lines_of(rest)] * 3, [VMEM] * (9 + 7), [VMEM] *...  2.84 us
    pallas_call x1, Pallas kernels, body(): call(last_far, [out] * 3, [VMEM] * (8 + 4 + 7 + 3), [HBM] * 3, [vmem(line...  2.68 us
    pallas_call x1, Pallas kernels, body(): call(first_far, [tall(some), short(0), lines_of(some), lines_of(some), li...  1.7 us
    pallas_call x1, Pallas kernels, body(): call(pack_weights, [matrix] * 4 + [shape((2 * size, 2 * size), BF16)] * 2...  1.19 us
    pallas_call x1, Pallas kernels, body(): call(functools.partial(pack_columns, sides), [shape(block, BF16)] * sides...  0.98 us
  transfers between devices with their start and end apart: 5, of which 2 were waited for; matrix products, arithmetic and copies ran while one was open for 0% of the time, Pallas kernels for 40%

profile of v7, /device:TPU:0, one launch (start us, length us, event | category | flops | bytes accessed | tf_op | source)
XLA Modules:
  0.0 21.8 jit_solution(17993941828227855048)
XLA Ops:
  0.6 0.0 copy-start.3
  0.6 0.0 copy-start.2
  0.7 1.0 %pack_columns.1 = (bf16[18,8,128]{2,1,0:T(8,128)(2,1)S(1)}, bf16[128,128]{1,0:T(8,128)(2,1)S(1)}, bf16[16,128]{1,0:T(8,128)(2,1)S(1)}, bf16[16,128]{1,0:T(8,128)(2,1)S(1)}) custom-call(f32[8,128,128]{2,1,0:T(8,128)} %latent.1, f32[8,128,128]{2,1,0:T(8,128)} %moment_one.1, f32[8,128,128]{2,1,0:T(8,128)} %moment_two.1, f32[3,8,128]{2,1,0:T(8,128)} %target.1, ...), custom_call_target="tpu_custom_call" | custom-call | flops 1000000 | bytes 1000000 | tf_op jit(solution)/shard_map/pack_columns/pallas_call | solution.py:700
  1.6 3.0 %collective-permute-start = (bf16[18,8,128]{2,1,0:T(8,128)(2,1)S(1)}, bf16[18,8,128]{2,1,0:T(8,128)(2,1)S(1)}, u32[]{:S(2)}, u32[]{:S(2)}) collective-permute-start(bf16[18,8,128]{2,1,0:T(8,128)(2,1)S(1)} %get-tuple-element.60), channel_id=1, source_target_pairs={{0,2},{2,0},{1,3},{3,1},{4,6},{6,4},{5,7},{7,5},{8,10},{10,8},{9,1... | collective-permute-start | bytes 110600 | tf_op jit(solution)/shard_map/ppermute | solution.py:42
  4.7 0.0 copy-done.3
  4.7 0.0 copy-done.2
  4.7 0.0 copy-start.1
  4.7 1.2 %pack_weights.1 = (bf16[1536,256]{1,0:T(8,128)(2,1)S(1)}, bf16[1536,256]{1,0:T(8,128)(2,1)S(1)}, bf16[1536,256]{1,0:T(8,128)(2,1)S(1)}, bf16[1536,256]{1,0:T(8,1...) custom-call(bf16[3,3,128,128]{3,2,1,0:T(8,128)(2,1)S(1)} %copy-done., ...), custom_call_target="tpu_custom_call" | custom-call | flops 1000000 | bytes 4000000 | tf_op jit(solution)/shard_map/pack_weights/pallas_call | solution.py:721
  5.9 0.0 copy-start
  5.9 0.7 %collective-permute-done.rest_0_.refs_0_ = bf16[18,8,128]{2,1,0:T(8,128)(2,1)S(1)} collective-permute-done((bf16[18,8,128]{2,1,0:T(8,128)(2,1)S(1)}, bf16[18,8,128]{2,1,0:T(8,128)(2,1)S(1)}, u32[]{:S(2)}, u32[]{:S(2)}) %collective-permute-start) | collective-permute-done | bytes 36896 | tf_op jit(solution)/shard_map/ppermute | solution.py:42
  6.6 0.1 pack_rows.1
  6.8 0.1 collective-permute-start.1
  6.8 2.1 %collective-permute-start.2 = (bf16[38,16,128]{2,1,0:T(8,128)(2,1)S(1)}, bf16[38,16,128]{2,1,0:T(8,128)(2,1)S(1)}, u32[]{:S(2)}, u32[]{:S(2)}) collective-permute-start(bf16[38,16,128]{2,1,0:T(8,128)(2,1)S(1)} %get-tuple-element.83), channel_id=1, source_target_pairs={{0,2},{1,4},{2,0},{3,6},{4,1},{5,8},{6,3},{7,10},{8,5},{9,12},{10,... | collective-permute-start | bytes 466952 | tf_op jit(solution)/shard_map/ppermute | solution.py:61
  8.9 0.0 collective-permute-done.1.near
  8.9 0.0 copy-done.1
  8.9 0.0 copy-done
  8.9 3.0 %first_near.1 = (bf16[2,11,16,128]{3,2,1,0:T(8,128)(2,1)S(1)}, f32[2,144,128]{2,1,0:T(8,128)S(1)}, bf16[2,11,16,128]{3,2,1,0:T(8,128)(2,1)S(1)}, bf16[2,11,16,12...) custom-call(bf16[8,11,16,128]{3,2,1,0:T(8,128)(2,1)S(1)} %get-tuple-, ...), custom_call_target="tpu_custom_call" | custom-call | flops 1585446912 | bytes 10000000 | tf_op jit(solution)/shard_map/first_near/pallas_call | solution.py:769
  12.0 0.3 %collective-permute-start.4 = (bf16[36,16,128]{2,1,0:T(8,128)(2,1)S(1)}, bf16[36,16,128]{2,1,0:T(8,128)(2,1)S(1)}, u32[]{:S(2)}, u32[]{:S(2)}) collective-permute-start(bf16[36,16,128]{2,1,0:T(8,128)(2,1)S(1)} %get-tuple-element.96), channel_id=1, source_target_pairs={{0,1},{1,0},{4,5},{5,4},{8,9},{9,8},{12,13},{13,12},{2,3},{3,2},{6... | collective-permute-start | bytes 442376 | tf_op jit(solution)/shard_map/ppermute | solution.py:42
  12.2 0.0 collective-permute-done.2.far
  12.2 1.7 %first_far.1 = (bf16[4,11,16,128]{3,2,1,0:T(8,128)(2,1)S(1)}, bf16[36,16,128]{2,1,0:T(8,128)(2,1)S(1)}, f32[4,144,128]{2,1,0:T(8,128)S(1)}, f32[4,144,128]{2,1,0...) custom-call(bf16[8,11,16,128]{3,2,1,0:T(8,128)(2,1)S(1)} %get-tuple-element.69.own, ...), custom_call_target="tpu_custom_call" | custom-call | flops 905969664 | bytes 10000000 | tf_op jit(solution)/shard_map/first_far/pallas_call | solution.py:784
  14.0 2.0 %collective-permute-start.3 = (bf16[36,16,128]{2,1,0:T(8,128)(2,1)S(1)}, bf16[36,16,128]{2,1,0:T(8,128)(2,1)S(1)}, u32[]{:S(2)}, u32[]{:S(2)}) collective-permute-start(bf16[36,16,128]{2,1,0:T(8,128)(2,1)S(1)} %get-tuple-element.89), channel_id=1, source_target_pairs={{0,2},{1,4},{2,0},{3,6},{4,1},{5,8},{6,3},{7,10},{8,5},{9,12},{10,... | collective-permute-start | bytes 442376 | tf_op jit(solution)/shard_map/ppermute | solution.py:61
  15.9 0.0 collective-permute-done.4.near
  15.9 2.8 %last_near.1 = (bf16[2,11,16,128]{3,2,1,0:T(8,128)(2,1)S(1)}, f32[2,144,128]{2,1,0:T(8,128)S(1)}, bf16[2,11,16,128]{3,2,1,0:T(8,128)(2,1)S(1)}, bf16[2,11,16,128...) custom-call(bf16[4,11,16,128]{3,2,1,0:T(8,128)(2,1)S(1)} %get-tuple-, ...), custom_call_target="tpu_custom_call" | custom-call | flops 1585446912 | bytes 10000000 | tf_op jit(solution)/shard_map/last_near/pallas_call | solution.py:797
  18.8 0.4 %collective-permute-done.3.far = bf16[36,16,128]{2,1,0:T(8,128)(2,1)S(1)} collective-permute-done((bf16[36,16,128]{2,1,0:T(8,128)(2,1)S(1)}, bf16[36,16,128]{2,1,0:T(8,128)(2,1)S(1)}, u32[]{:S(2)}, u32[]{:S(2)}) %collective-permute-start.3) | collective-permute-done | bytes 147488 | tf_op jit(solution)/shard_map/ppermute | solution.py:61
  19.2 2.7 %last_far.1 = (f32[8,128,128]{2,1,0:T(8,128)}, f32[8,128,128]{2,1,0:T(8,128)}, f32[8,128,128]{2,1,0:T(8,128)}) custom-call(bf16[4,11,16,128]{3,2,1,0:T(8,128)(2,1)S(1)} %get-tuple-element.88.low, bf16[36,16,128]{2,1,0:T(8,128)(2,1)S(1)} %collective-permute-done.3.far, f32[4,144,128]{2,1,0:T(8,128)S(1)} %get-tuple-element.90.z_in, ...), custom_call_target="tpu_custom_call" | custom-call | flops 905969664 | bytes 10000000 | tf_op jit(solution)/shard_map/last_far/pallas_call | solution.py:807
Async XLA Ops:
  0.6 4.0 %copy-start.3 = (bf16[3,3,128,128]{3,2,1,0:T(8,128)(2,1)S(1)}, bf16[3,3,128,128]{3,2,1,0:T(8,128)(2,1)}, u32[]{:S(2)}) copy-start(bf16[3,3,128,128]{3,2,1,0:T(8,128)(2,1)} %two.1) | copy-start | bytes 884740
  0.6 4.0 %copy-start.2 = (bf16[3,3,128,128]{3,2,1,0:T(8,128)(2,1)S(1)}, bf16[3,3,128,128]{3,2,1,0:T(8,128)(2,1)}, u32[]{:S(2)}) copy-start(bf16[3,3,128,128]{3,2,1,0:T(8,128)(2,1)} %one.1) | copy-start | bytes 884740
  1.6 5.0 %collective-permute-start = (bf16[18,8,128]{2,1,0:T(8,128)(2,1)S(1)}, bf16[18,8,128]{2,1,0:T(8,128)(2,1)S(1)}, u32[]{:S(2)}, u32[]{:S(2)}) collective-permute-start(bf16[18,8,128]{2,1,0:T(8,128)(2,1)S(1)} %get-tuple-element.60), channel_id=1, source_target_pairs={{0,2},{2,0},{1,3},{3,1},{4,6},{6,4},{5,7},{7,5},{8,10},{10,8},{9,1... | collective-permute-start | bytes 110600 | tf_op jit(solution)/shard_map/ppermute | solution.py:42
  4.7 4.2 %copy-start.1 = (f32[8,128,128]{2,1,0:T(8,128)S(1)}, f32[8,128,128]{2,1,0:T(8,128)}, u32[]{:S(2)}) copy-start(f32[8,128,128]{2,1,0:T(8,128)} %moment_two.1) | copy-start | bytes 1572868
  5.9 3.0 %copy-start = (f32[8,128,128]{2,1,0:T(8,128)S(1)}, f32[8,128,128]{2,1,0:T(8,128)}, u32[]{:S(2)}) copy-start(f32[8,128,128]{2,1,0:T(8,128)} %moment_one.1) | copy-start | bytes 1572868
  6.8 2.2 %collective-permute-start.1 = (bf16[38,16,128]{2,1,0:T(8,128)(2,1)S(1)}, bf16[38,16,128]{2,1,0:T(8,128)(2,1)S(1)}, u32[]{:S(2)}, u32[]{:S(2)}) collective-permute-start(bf16[38,16,128]{2,1,0:T(8,128)(2,1)S(1)} %get-tuple-element.71), channel_id=1, source_target_pairs={{0,1},{1,0},{4,5},{5,4},{8,9},{9,8},{12,13},{13,12},{2,3},{3,2},{6... | collective-permute-start | bytes 466952 | tf_op jit(solution)/shard_map/ppermute | solution.py:42
  6.8 5.4 %collective-permute-start.2 = (bf16[38,16,128]{2,1,0:T(8,128)(2,1)S(1)}, bf16[38,16,128]{2,1,0:T(8,128)(2,1)S(1)}, u32[]{:S(2)}, u32[]{:S(2)}) collective-permute-start(bf16[38,16,128]{2,1,0:T(8,128)(2,1)S(1)} %get-tuple-element.83), channel_id=1, source_target_pairs={{0,2},{1,4},{2,0},{3,6},{4,1},{5,8},{6,3},{7,10},{8,5},{9,12},{10,... | collective-permute-start | bytes 466952 | tf_op jit(solution)/shard_map/ppermute | solution.py:61
  12.0 3.9 %collective-permute-start.4 = (bf16[36,16,128]{2,1,0:T(8,128)(2,1)S(1)}, bf16[36,16,128]{2,1,0:T(8,128)(2,1)S(1)}, u32[]{:S(2)}, u32[]{:S(2)}) collective-permute-start(bf16[36,16,128]{2,1,0:T(8,128)(2,1)S(1)} %get-tuple-element.96), channel_id=1, source_target_pairs={{0,1},{1,0},{4,5},{5,4},{8,9},{9,8},{12,13},{13,12},{2,3},{3,2},{6... | collective-permute-start | bytes 442376 | tf_op jit(solution)/shard_map/ppermute | solution.py:42
  14.0 5.2 %collective-permute-start.3 = (bf16[36,16,128]{2,1,0:T(8,128)(2,1)S(1)}, bf16[36,16,128]{2,1,0:T(8,128)(2,1)S(1)}, u32[]{:S(2)}, u32[]{:S(2)}) collective-permute-start(bf16[36,16,128]{2,1,0:T(8,128)(2,1)S(1)} %get-tuple-element.89), channel_id=1, source_target_pairs={{0,2},{1,4},{2,0},{3,6},{4,1},{5,8},{6,3},{7,10},{8,5},{9,12},{10,... | collective-permute-start | bytes 442376 | tf_op jit(solution)/shard_map/ppermute | solution.py:61

commit v8 on v7

--- a/solution.py
+++ b/solution.py
@@ -575,7 +575,7 @@
             near_out[(height - 1 - row) * strip : (height - row) * strip] = short
 
     rows = near_rows(height, place_rows((4, height + 4, own, 0)), halo, passed, scratch)
-    gradient(first_near_order(height), rows, weights, aims, known, inside, emit, pair_up(tasks), False, 2)
+    gradient(first_near_order(height), rows, weights, aims, known, inside, emit, pair_up(tasks), False, 3)
 
 
 def first_far(own, lines, m_rest, v_rest, far, spots, inside, *refs):
@@ -631,7 +631,7 @@
 
     own = place_rows((4, 8, low, 0), (8, height + 4, high, 0))
     rows = near_rows(height, own, halo, passed, scratch)
-    gradient(last_near_order(height), rows, weights, aims, known, inside, emit, (), False, 2)
+    gradient(last_near_order(height), rows, weights, aims, known, inside, emit, (), False, 3)
 
 
 def last_far(low, far, z_in, m_in, v_in, aims, known, inside, *refs):

time: 22 us -> 22 us (level)
  no operation moved by 1% of the time
where the time goes in v8:
time: 22 us; the launch traced here: 21.9 us
  Pallas kernels  12.6 us (57%)
  starting transfers between devices  7.38 us (34%)
  waiting for transfers between devices  1.17 us (5%)
  between operations  0.71 us (3%)
    ppermute x2, starting transfers between devices, swap_far(): return lax.ppermute(block, ('row', 'col', 'cores'), sorted(chosen))  4.01 us
    ppermute x3, starting transfers between devices, swap(): return lax.ppermute(block, axes, pairs(lax.axis_size(axes), parity))  3.37 us
    pallas_call x1, Pallas kernels, body(): call(functools.partial(first_near, sides), passed + [tall(rest), short(0)...  3.08 us
    pallas_call x1, Pallas kernels, body(): call(last_near, passed + [lines_of(rest)] * 3, [VMEM] * (9 + 7), [VMEM] *...  2.83 us
    pallas_call x1, Pallas kernels, body(): call(last_far, [out] * 3, [VMEM] * (8 + 4 + 7 + 3), [HBM] * 3, [vmem(line...  2.68 us
    pallas_call x1, Pallas kernels, body(): call(first_far, [tall(some), short(0), lines_of(some), lines_of(some), li...  1.71 us
    pallas_call x1, Pallas kernels, body(): call(pack_weights, [matrix] * 4 + [shape((2 * size, 2 * size), BF16)] * 2...  1.19 us
    pallas_call x1, Pallas kernels, body(): call(functools.partial(pack_columns, sides), [shape(block, BF16)] * sides...  0.98 us
  transfers between devices with their start and end apart: 5, of which 2 were waited for; matrix products, arithmetic and copies ran while one was open for 0% of the time, Pallas kernels for 40%

profile of v8, /device:TPU:0, one launch (start us, length us, event | category | flops | bytes accessed | tf_op | source)
XLA Modules:
  0.0 21.9 jit_solution(6240992150915813749)
XLA Ops:
  0.6 0.0 copy-start.3
  0.6 0.0 copy-start.2
  0.7 1.0 %pack_columns.1 = (bf16[18,8,128]{2,1,0:T(8,128)(2,1)S(1)}, bf16[128,128]{1,0:T(8,128)(2,1)S(1)}, bf16[16,128]{1,0:T(8,128)(2,1)S(1)}, bf16[16,128]{1,0:T(8,128)(2,1)S(1)}) custom-call(f32[8,128,128]{2,1,0:T(8,128)} %latent.1, f32[8,128,128]{2,1,0:T(8,128)} %moment_one.1, f32[8,128,128]{2,1,0:T(8,128)} %moment_two.1, f32[3,8,128]{2,1,0:T(8,128)} %target.1, ...), custom_call_target="tpu_custom_call" | custom-call | flops 1000000 | bytes 1000000 | tf_op jit(solution)/shard_map/pack_columns/pallas_call | solution.py:700
  1.6 3.0 %collective-permute-start = (bf16[18,8,128]{2,1,0:T(8,128)(2,1)S(1)}, bf16[18,8,128]{2,1,0:T(8,128)(2,1)S(1)}, u32[]{:S(2)}, u32[]{:S(2)}) collective-permute-start(bf16[18,8,128]{2,1,0:T(8,128)(2,1)S(1)} %get-tuple-element.60), channel_id=1, source_target_pairs={{0,2},{2,0},{1,3},{3,1},{4,6},{6,4},{5,7},{7,5},{8,10},{10,8},{9,1... | collective-permute-start | bytes 110600 | tf_op jit(solution)/shard_map/ppermute | solution.py:42
  4.7 0.0 copy-done.3
  4.7 0.0 copy-done.2
  4.7 0.0 copy-start.1
  4.7 1.2 %pack_weights.1 = (bf16[1536,256]{1,0:T(8,128)(2,1)S(1)}, bf16[1536,256]{1,0:T(8,128)(2,1)S(1)}, bf16[1536,256]{1,0:T(8,128)(2,1)S(1)}, bf16[1536,256]{1,0:T(8,1...) custom-call(bf16[3,3,128,128]{3,2,1,0:T(8,128)(2,1)S(1)} %copy-done., ...), custom_call_target="tpu_custom_call" | custom-call | flops 1000000 | bytes 4000000 | tf_op jit(solution)/shard_map/pack_weights/pallas_call | solution.py:721
  5.9 0.0 copy-start
  5.9 0.7 %collective-permute-done.rest_0_.refs_0_ = bf16[18,8,128]{2,1,0:T(8,128)(2,1)S(1)} collective-permute-done((bf16[18,8,128]{2,1,0:T(8,128)(2,1)S(1)}, bf16[18,8,128]{2,1,0:T(8,128)(2,1)S(1)}, u32[]{:S(2)}, u32[]{:S(2)}) %collective-permute-start) | collective-permute-done | bytes 36896 | tf_op jit(solution)/shard_map/ppermute | solution.py:42
  6.6 0.1 pack_rows.1
  6.8 0.1 collective-permute-start.1
  6.8 2.1 %collective-permute-start.2 = (bf16[38,16,128]{2,1,0:T(8,128)(2,1)S(1)}, bf16[38,16,128]{2,1,0:T(8,128)(2,1)S(1)}, u32[]{:S(2)}, u32[]{:S(2)}) collective-permute-start(bf16[38,16,128]{2,1,0:T(8,128)(2,1)S(1)} %get-tuple-element.83), channel_id=1, source_target_pairs={{0,2},{1,4},{2,0},{3,6},{4,1},{5,8},{6,3},{7,10},{8,5},{9,12},{10,... | collective-permute-start | bytes 466952 | tf_op jit(solution)/shard_map/ppermute | solution.py:61
  8.9 0.0 collective-permute-done.1.near
  8.9 0.0 copy-done.1
  8.9 0.0 copy-done
  8.9 3.1 %first_near.1 = (bf16[2,11,16,128]{3,2,1,0:T(8,128)(2,1)S(1)}, f32[2,144,128]{2,1,0:T(8,128)S(1)}, bf16[2,11,16,128]{3,2,1,0:T(8,128)(2,1)S(1)}, bf16[2,11,16,12...) custom-call(bf16[8,11,16,128]{3,2,1,0:T(8,128)(2,1)S(1)} %get-tuple-, ...), custom_call_target="tpu_custom_call" | custom-call | flops 1585446912 | bytes 10000000 | tf_op jit(solution)/shard_map/first_near/pallas_call | solution.py:769
  12.0 0.3 %collective-permute-start.4 = (bf16[36,16,128]{2,1,0:T(8,128)(2,1)S(1)}, bf16[36,16,128]{2,1,0:T(8,128)(2,1)S(1)}, u32[]{:S(2)}, u32[]{:S(2)}) collective-permute-start(bf16[36,16,128]{2,1,0:T(8,128)(2,1)S(1)} %get-tuple-element.96), channel_id=1, source_target_pairs={{0,1},{1,0},{4,5},{5,4},{8,9},{9,8},{12,13},{13,12},{2,3},{3,2},{6... | collective-permute-start | bytes 442376 | tf_op jit(solution)/shard_map/ppermute | solution.py:42
  12.3 0.0 collective-permute-done.2.far
  12.3 1.7 %first_far.1 = (bf16[4,11,16,128]{3,2,1,0:T(8,128)(2,1)S(1)}, bf16[36,16,128]{2,1,0:T(8,128)(2,1)S(1)}, f32[4,144,128]{2,1,0:T(8,128)S(1)}, f32[4,144,128]{2,1,0...) custom-call(bf16[8,11,16,128]{3,2,1,0:T(8,128)(2,1)S(1)} %get-tuple-element.69.own, ...), custom_call_target="tpu_custom_call" | custom-call | flops 905969664 | bytes 10000000 | tf_op jit(solution)/shard_map/first_far/pallas_call | solution.py:784
  14.0 1.9 %collective-permute-start.3 = (bf16[36,16,128]{2,1,0:T(8,128)(2,1)S(1)}, bf16[36,16,128]{2,1,0:T(8,128)(2,1)S(1)}, u32[]{:S(2)}, u32[]{:S(2)}) collective-permute-start(bf16[36,16,128]{2,1,0:T(8,128)(2,1)S(1)} %get-tuple-element.89), channel_id=1, source_target_pairs={{0,2},{1,4},{2,0},{3,6},{4,1},{5,8},{6,3},{7,10},{8,5},{9,12},{10,... | collective-permute-start | bytes 442376 | tf_op jit(solution)/shard_map/ppermute | solution.py:61
  15.9 0.0 collective-permute-done.4.near
  15.9 2.8 %last_near.1 = (bf16[2,11,16,128]{3,2,1,0:T(8,128)(2,1)S(1)}, f32[2,144,128]{2,1,0:T(8,128)S(1)}, bf16[2,11,16,128]{3,2,1,0:T(8,128)(2,1)S(1)}, bf16[2,11,16,128...) custom-call(bf16[4,11,16,128]{3,2,1,0:T(8,128)(2,1)S(1)} %get-tuple-, ...), custom_call_target="tpu_custom_call" | custom-call | flops 1585446912 | bytes 10000000 | tf_op jit(solution)/shard_map/last_near/pallas_call | solution.py:797
  18.8 0.4 %collective-permute-done.3.far = bf16[36,16,128]{2,1,0:T(8,128)(2,1)S(1)} collective-permute-done((bf16[36,16,128]{2,1,0:T(8,128)(2,1)S(1)}, bf16[36,16,128]{2,1,0:T(8,128)(2,1)S(1)}, u32[]{:S(2)}, u32[]{:S(2)}) %collective-permute-start.3) | collective-permute-done | bytes 147488 | tf_op jit(solution)/shard_map/ppermute | solution.py:61
  19.2 2.7 %last_far.1 = (f32[8,128,128]{2,1,0:T(8,128)}, f32[8,128,128]{2,1,0:T(8,128)}, f32[8,128,128]{2,1,0:T(8,128)}) custom-call(bf16[4,11,16,128]{3,2,1,0:T(8,128)(2,1)S(1)} %get-tuple-element.88.low, bf16[36,16,128]{2,1,0:T(8,128)(2,1)S(1)} %collective-permute-done.3.far, f32[4,144,128]{2,1,0:T(8,128)S(1)} %get-tuple-element.90.z_in, ...), custom_call_target="tpu_custom_call" | custom-call | flops 905969664 | bytes 10000000 | tf_op jit(solution)/shard_map/last_far/pallas_call | solution.py:807
Async XLA Ops:
  0.6 4.0 %copy-start.3 = (bf16[3,3,128,128]{3,2,1,0:T(8,128)(2,1)S(1)}, bf16[3,3,128,128]{3,2,1,0:T(8,128)(2,1)}, u32[]{:S(2)}) copy-start(bf16[3,3,128,128]{3,2,1,0:T(8,128)(2,1)} %two.1) | copy-start | bytes 884740
  0.6 4.0 %copy-start.2 = (bf16[3,3,128,128]{3,2,1,0:T(8,128)(2,1)S(1)}, bf16[3,3,128,128]{3,2,1,0:T(8,128)(2,1)}, u32[]{:S(2)}) copy-start(bf16[3,3,128,128]{3,2,1,0:T(8,128)(2,1)} %one.1) | copy-start | bytes 884740
  1.6 5.0 %collective-permute-start = (bf16[18,8,128]{2,1,0:T(8,128)(2,1)S(1)}, bf16[18,8,128]{2,1,0:T(8,128)(2,1)S(1)}, u32[]{:S(2)}, u32[]{:S(2)}) collective-permute-start(bf16[18,8,128]{2,1,0:T(8,128)(2,1)S(1)} %get-tuple-element.60), channel_id=1, source_target_pairs={{0,2},{2,0},{1,3},{3,1},{4,6},{6,4},{5,7},{7,5},{8,10},{10,8},{9,1... | collective-permute-start | bytes 110600 | tf_op jit(solution)/shard_map/ppermute | solution.py:42
  4.7 4.2 %copy-start.1 = (f32[8,128,128]{2,1,0:T(8,128)S(1)}, f32[8,128,128]{2,1,0:T(8,128)}, u32[]{:S(2)}) copy-start(f32[8,128,128]{2,1,0:T(8,128)} %moment_two.1) | copy-start | bytes 1572868
  5.9 3.0 %copy-start = (f32[8,128,128]{2,1,0:T(8,128)S(1)}, f32[8,128,128]{2,1,0:T(8,128)}, u32[]{:S(2)}) copy-start(f32[8,128,128]{2,1,0:T(8,128)} %moment_one.1) | copy-start | bytes 1572868
  6.8 2.2 %collective-permute-start.1 = (bf16[38,16,128]{2,1,0:T(8,128)(2,1)S(1)}, bf16[38,16,128]{2,1,0:T(8,128)(2,1)S(1)}, u32[]{:S(2)}, u32[]{:S(2)}) collective-permute-start(bf16[38,16,128]{2,1,0:T(8,128)(2,1)S(1)} %get-tuple-element.71), channel_id=1, source_target_pairs={{0,1},{1,0},{4,5},{5,4},{8,9},{9,8},{12,13},{13,12},{2,3},{3,2},{6... | collective-permute-start | bytes 466952 | tf_op jit(solution)/shard_map/ppermute | solution.py:42
  6.8 5.5 %collective-permute-start.2 = (bf16[38,16,128]{2,1,0:T(8,128)(2,1)S(1)}, bf16[38,16,128]{2,1,0:T(8,128)(2,1)S(1)}, u32[]{:S(2)}, u32[]{:S(2)}) collective-permute-start(bf16[38,16,128]{2,1,0:T(8,128)(2,1)S(1)} %get-tuple-element.83), channel_id=1, source_target_pairs={{0,2},{1,4},{2,0},{3,6},{4,1},{5,8},{6,3},{7,10},{8,5},{9,12},{10,... | collective-permute-start | bytes 466952 | tf_op jit(solution)/shard_map/ppermute | solution.py:61
  12.0 3.9 %collective-permute-start.4 = (bf16[36,16,128]{2,1,0:T(8,128)(2,1)S(1)}, bf16[36,16,128]{2,1,0:T(8,128)(2,1)S(1)}, u32[]{:S(2)}, u32[]{:S(2)}) collective-permute-start(bf16[36,16,128]{2,1,0:T(8,128)(2,1)S(1)} %get-tuple-element.96), channel_id=1, source_target_pairs={{0,1},{1,0},{4,5},{5,4},{8,9},{9,8},{12,13},{13,12},{2,3},{3,2},{6... | collective-permute-start | bytes 442376 | tf_op jit(solution)/shard_map/ppermute | solution.py:42
  14.0 5.2 %collective-permute-start.3 = (bf16[36,16,128]{2,1,0:T(8,128)(2,1)S(1)}, bf16[36,16,128]{2,1,0:T(8,128)(2,1)S(1)}, u32[]{:S(2)}, u32[]{:S(2)}) collective-permute-start(bf16[36,16,128]{2,1,0:T(8,128)(2,1)S(1)} %get-tuple-element.89), channel_id=1, source_target_pairs={{0,2},{1,4},{2,0},{3,6},{4,1},{5,8},{6,3},{7,10},{8,5},{9,12},{10,... | collective-permute-start | bytes 442376 | tf_op jit(solution)/shard_map/ppermute | solution.py:61
